TPU v7x, 1024 devices: a whole 4x8x16 slice. The times are simulated.
1024 devices in a mesh: dp: 64 (over y_hi, z, core), tensor: 16 (over x, y_lo).
Axes of the slice: x: 4, y: 8 (y_hi: 2, y_lo: 4; y = y_hi * 4 + y_lo), z: 16, core: 2. Of those that a mesh axis runs over, the one named last changes fastest.
Arguments:
- acts: bfloat16 [8192, 8192], P('dp', 'tensor'), may hold values from -6 to 6
- grad_out: bfloat16 [8192, 14336], P('dp', 'tensor'), may hold values from -6 to 6
- proj_t: bfloat16 [512, 8192], P(None, 'tensor'), may hold values from -6 to 6
- first_moment: float32 [512, 14336], P('dp', 'tensor'), may hold values from -0.15625 to 0.15625
- second_moment: float32 [512, 14336], P('dp', 'tensor'), may hold values from 1e-05 to 0.001
Outputs:
- adam_step: float32 [512, 14336], P('dp', 'tensor')
- new_proj_t: float32 [512, 8192], P('dp', 'tensor')
All inputs are finite; a program needn't handle non-finite values.
Results may differ from a plain program's by a relative error of at most 0.023.
Values may be sent and summed in bfloat16 or wider, within the bound.
No kernel may reach another device: no remote copies, remote signals or barrier semaphores. Data moves between devices by JAX's collectives and lax.ppermute only.
A program may use at most 32 MiB of HBM per device.

v0:
```python
import jax
import jax.numpy as jnp
from jax import lax
from jax.sharding import PartitionSpec as P

D = 8192


def sent_to_all(x, axis):
    copies = jnp.broadcast_to(x, (lax.axis_size(axis), *x.shape))
    return lax.all_to_all(copies, axis, split_axis=0, concat_axis=0, tiled=True)


def of_everyone(x, axis):
    everything = sent_to_all(x, axis)
    return jnp.sum(everything.astype(jnp.float32), axis=0)


def in_blocks(x, dim, length):
    shape = x.shape
    pieces = x.reshape(*shape[:dim], length, shape[dim] // length, *shape[dim + 1 :])
    return jnp.moveaxis(pieces, dim, 0)


def sum_at_owner(x, axis, dim):
    pieces = in_blocks(x, dim, lax.axis_size(axis))
    arrived = lax.all_to_all(pieces, axis, split_axis=0, concat_axis=0, tiled=True)
    return arrived.sum(axis=0)


def contract_rows(left, right):
    return lax.dot_general(
        left, right, (((0,), (0,)), ((), ())), preferred_element_type=jnp.float32
    )


def contract_cols(left, right):
    return lax.dot_general(
        left, right, (((1,), (1,)), ((), ())), preferred_element_type=jnp.float32
    )


def local(acts, grad_out, proj_t, first_moment, second_moment):
    tok_rows = acts.shape[0]
    total_tokens = tok_rows * lax.axis_size("dp")
    rank_rows = first_moment.shape[0]
    inv_root = 1.0 / jnp.sqrt(jnp.float32(D))
    row_start = lax.axis_index("dp") * rank_rows
    local_coords = contract_cols(acts, proj_t) * inv_root
    coords = (
        of_everyone(local_coords.astype(jnp.bfloat16), "tensor")
        .astype(jnp.float32)
        .astype(jnp.bfloat16)
    )
    picked = coords
    grad_full = lax.psum(contract_rows(picked, grad_out) / total_tokens, "dp")
    grad_part = lax.dynamic_slice_in_dim(grad_full, row_start, rank_rows, 0)
    low_full = grad_full.astype(jnp.bfloat16)
    low_part = lax.dynamic_slice_in_dim(low_full, row_start, rank_rows, 0)
    back_part = contract_cols(grad_out, low_full)
    cross_part = contract_cols(low_part, low_full)
    moment_one = 0.9 * first_moment + 0.1 * grad_part
    moment_two = 0.999 * second_moment + 0.001 * grad_part * grad_part
    adam_step = moment_one / (1.0 - 0.9**10) / (jnp.sqrt(moment_two / (1.0 - 0.999**10)) + 1e-08)
    back, cross = (
        of_everyone(back_part.astype(jnp.bfloat16), "tensor").astype(jnp.float32),
        of_everyone(cross_part.astype(jnp.bfloat16), "tensor").astype(jnp.float32),
    )
    back_low = back.astype(jnp.bfloat16)
    picked = back_low
    pull = sum_at_owner(contract_rows(picked, acts) / total_tokens, "dp", 0)
    proj_wide = proj_t.astype(jnp.float32)
    own_rows = lax.dynamic_slice_in_dim(proj_wide, row_start, rank_rows, 0)
    correction = jnp.dot(cross, proj_wide, precision=lax.Precision.HIGHEST)
    new_proj_t = own_rows + jnp.sqrt(jnp.float32(D)) * pull - correction
    return (adam_step, new_proj_t)


def solution(mesh):
    placed = (
        P("dp", "tensor"),
        P("dp", "tensor"),
        P(None, "tensor"),
        P("dp", "tensor"),
        P("dp", "tensor"),
    )
    return jax.shard_map(
        local,
        mesh=mesh,
        in_specs=placed,
        out_specs=(P("dp", "tensor"), P("dp", "tensor")),
        check_vma=False,
    )
```

profile of v0, /device:TPU:65, one launch (start us, length us, event | category | flops | bytes accessed | tf_op | source)
XLA Modules:
  0.0 890.5 jit_solution(2706577975239923247)
XLA Ops:
  7.2 0.0 copy-start
  7.2 0.0 all-reduce.2.cloned.1.call-start
  7.2 1.5 fusion.1
  8.7 0.2 broadcast_in_dim.9
  8.9 56.4 %all_to_all.20 = bf16[16,128,512]{2,1,0:T(8,128)(2,1)S(1)} all-to-all(bf16[16,128,512]{2,1,0:T(8,128)(2,1)S(1)} %broadcast_in_dim.9), channel_id=1, replica_groups=mesh['dp'=64,'tensor'=16] {'tensor'}, dimensions={0} | all-to-all | bytes 4194304 | tf_op jit(solution)/shard_map/all_to_all | solution.py:11
  65.3 0.3 reduce_sum.42
  65.6 0.0 copy-done
  65.6 1.7 convolution_multiply_fusion
  67.3 0.0 all-reduce.2.cloned.1.call-update
  67.3 668.1 %all-reduce.2.cloned.1.call-done = f32[512,896]{1,0:T(8,128)} async-done(((f32[512,896]{1,0:T(8,128)}), f32[512,896]{1,0:T(8,128)}) %all-reduce.2.cloned.1.call-update) | async-done | bytes 1835024 | tf_op jit(solution)/shard_map/psum | solution.py:56
  735.4 1.6 convert_element_type.27
  737.0 0.4 fusion.2
  737.5 1.6 broadcast_in_dim.10
  739.0 4.4 all-to-all-start.1
  743.4 0.0 copy-start.2
  743.4 0.3 convolution_convert_fusion.1
  743.8 49.5 %all-to-all-done.1 = bf16[16,128,512]{2,1,0:T(8,128)(2,1)S(1)} async-done(((bf16[16,128,512]{2,1,0:T(8,128)(2,1)}), bf16[16,128,512]{2,1,0:T(8,128)(2,1)S(1)}, u32[]{:S(2)}, u32[]{:S(2)}) %all-to-all-start.1) | async-done | bytes 2097184 | tf_op jit(solution)/shard_map/all_to_all | solution.py:11
  793.2 0.7 broadcast_in_dim.11
  793.9 3.5 all-to-all-start.3
  797.4 0.3 reduce_sum.43
  797.7 0.0 copy-done.2
  797.7 0.0 copy-start.3
  797.7 0.0 copy-start.4
  797.7 1.3 fusion
  799.1 0.0 copy-start.1
  799.1 5.6 all-to-all-done.3
  804.6 19.9 %all-to-all-start.2 = ((f32[64,8,512]{2,1,0:T(8,128)}), f32[64,8,512]{2,1,0:T(8,128)S(1)}, u32[]{:S(2)}, u32[]{:S(2)}) async-start(f32[64,8,512]{2,1,0:T(8,128)} %fusion), calls=%async_computation.2 | async-start | bytes 2097152 | tf_op jit(solution)/shard_map/all_to_all | solution.py:27
  824.5 0.0 copy-done.3
  824.5 0.0 copy-done.4
  824.5 1.4 fusion.7
  825.9 56.7 %all-to-all-done.2 = f32[64,8,512]{2,1,0:T(8,128)S(1)} async-done(((f32[64,8,512]{2,1,0:T(8,128)}), f32[64,8,512]{2,1,0:T(8,128)S(1)}, u32[]{:S(2)}, u32[]{:S(2)}) %all-to-all-start.2) | async-done | bytes 1048608 | tf_op jit(solution)/shard_map/all_to_all | solution.py:27
  882.6 0.1 reduce_sum.44
  882.7 0.0 copy-done.1
  882.7 0.9 convolution_subtract_fusion
  (1 shorter events, 0.0 us)
Async XLA Ops:
  7.2 58.5 %copy-start = (bf16[128,896]{1,0:T(8,128)(2,1)S(1)}, bf16[128,896]{1,0:T(8,128)(2,1)}, u32[]{:S(2)}) copy-start(bf16[128,896]{1,0:T(8,128)(2,1)} %param.6) | copy-start | bytes 688132
  7.2 728.3 %all-reduce.2.cloned.1.call-start = ((), (), s32[]{:S(2)}) async-start(), calls=%async_computation.4 | async-start | bytes 3670016 | tf_op jit(solution)/shard_map/psum | solution.py:56
  739.0 54.2 %all-to-all-start.1 = ((bf16[16,128,512]{2,1,0:T(8,128)(2,1)}), bf16[16,128,512]{2,1,0:T(8,128)(2,1)S(1)}, u32[]{:S(2)}, u32[]{:S(2)}) async-start(bf16[16,128,512]{2,1,0:T(8,128)(2,1)} %broadcast_in_dim.10), calls=%async_computation.1 | async-start | bytes 4194304 | tf_op jit(solution)/shard_map/all_to_all | solution.py:11
  743.4 54.3 %copy-start.2 = (bf16[128,512]{1,0:T(8,128)(2,1)S(1)}, bf16[128,512]{1,0:T(8,128)(2,1)}, u32[]{:S(2)}) copy-start(bf16[128,512]{1,0:T(8,128)(2,1)} %param.5) | copy-start | bytes 393220
  793.9 10.7 %all-to-all-start.3 = ((bf16[16,8,512]{2,1,0:T(8,128)(2,1)}), bf16[16,8,512]{2,1,0:T(8,128)(2,1)S(1)}, u32[]{:S(2)}, u32[]{:S(2)}) async-start(bf16[16,8,512]{2,1,0:T(8,128)(2,1)} %broadcast_in_dim.11), calls=%async_computation.3 | async-start | bytes 262144 | tf_op jit(solution)/shard_map/all_to_all | solution.py:11
  797.7 26.8 %copy-start.3 = (f32[8,896]{1,0:T(8,128)S(1)}, f32[8,896]{1,0:T(8,128)}, u32[]{:S(2)}) copy-start(f32[8,896]{1,0:T(8,128)} %param.9) | copy-start | bytes 86020
  797.7 26.8 %copy-start.4 = (f32[8,896]{1,0:T(8,128)S(1)}, f32[8,896]{1,0:T(8,128)}, u32[]{:S(2)}) copy-start(f32[8,896]{1,0:T(8,128)} %param.8) | copy-start | bytes 86020
  799.1 83.7 %copy-start.1 = (bf16[512,512]{1,0:T(8,128)(2,1)S(1)}, bf16[512,512]{1,0:T(8,128)(2,1)}, u32[]{:S(2)}) copy-start(bf16[512,512]{1,0:T(8,128)(2,1)} %param.7) | copy-start | bytes 1572868
  804.6 78.0 %all-to-all-start.2 = ((f32[64,8,512]{2,1,0:T(8,128)}), f32[64,8,512]{2,1,0:T(8,128)S(1)}, u32[]{:S(2)}, u32[]{:S(2)}) async-start(f32[64,8,512]{2,1,0:T(8,128)} %fusion), calls=%async_computation.2 | async-start | bytes 2097152 | tf_op jit(solution)/shard_map/all_to_all | solution.py:27
Sparse Core Ops, SparseCore 0:
  67.5 667.9 all-reduce.1
where the time goes:
time: 891 us
  waiting for transfers between devices  780 us (88%)
  blocking collectives  56.4 us (6%)
  starting transfers between devices  27.8 us (3%)
  between operations  14.2 us (2%)
    psum x1, waiting for transfers between devices, local(): grad_full = lax.psum(contract_rows(picked, grad_out) / total_tokens, 'dp')  668 us
    all_to_all x1, waiting for transfers between devices, sum_at_owner(): lax.all_to_all(pieces, axis, split_axis=0, concat_axis=0, tiled=True)  56.7 us
    all_to_all x1, blocking collectives, sent_to_all(): return lax.all_to_all(copies, axis, split_axis=0, concat_axis=0, tiled=True)  56.4 us
    all_to_all x2, waiting for transfers between devices, sent_to_all(): return lax.all_to_all(copies, axis, split_axis=0, concat_axis=0, tiled=True)  55 us
    all_to_all x1, starting transfers between devices, sum_at_owner(): lax.all_to_all(pieces, axis, split_axis=0, concat_axis=0, tiled=True)  19.9 us
  transfers between devices with their start and end apart: 4, of which 4 were waited for; matrix products, arithmetic and copies ran while one was open for 0% of the time, Pallas kernels for 0%

commit v1 on v0

v1 whole, which is shorter than its diff:
```python
import math

import jax
import jax.numpy as jnp
from jax import lax
from jax.sharding import Mesh, PartitionSpec as P

D = 8192
TOKENS = 8192
DP = ("yh", "z3", "z2", "z1", "z0", "c")
SIZES = (2, 2, 2, 2, 2, 2)
TENSOR = ("x", "yl")
NEAR = ("c",)
FAR = tuple(a for a in DP if a not in NEAR)


def size(axes):
    return math.prod(SIZES[DP.index(a)] for a in axes)


def swap(pieces, axes):
    return lax.all_to_all(pieces, axes, split_axis=0, concat_axis=0, tiled=True)


def to_all(x, axes, count):
    return swap(jnp.broadcast_to(x, (count, *x.shape)), axes)


def total(pieces):
    return jnp.sum(pieces.astype(jnp.float32), axis=0)


def dot(left, right, dims):
    return lax.dot_general(left, right, (dims, ((), ())), preferred_element_type=jnp.float32)


def by_near(x):
    rows, cols = x.shape
    order = [DP.index(a) for a in NEAR + FAR]
    x = x.reshape(*SIZES, rows // size(DP), cols).transpose(*order, len(DP), len(DP) + 1)
    return x.reshape(size(NEAR), rows // size(NEAR), cols)


def local(acts, grad_out, proj_t, first_moment, second_moment):
    bf16 = jnp.bfloat16
    n_near, n_far, n_t = size(NEAR), size(FAR), 16
    rank = proj_t.shape[0]
    own = rank // (n_near * n_far)
    toks = acts.shape[0]
    inv_root = 1.0 / jnp.sqrt(jnp.float32(D))
    acts_all = to_all(acts, NEAR, n_near)
    grad_all = to_all(grad_out, NEAR, n_near)
    part = (dot(proj_t, acts, ((1,), (1,))) * inv_root).astype(bf16)
    mine = total(swap(part.reshape(n_t, rank // n_t, toks), TENSOR)).astype(bf16)
    coords = to_all(mine, TENSOR, n_t).reshape(rank, toks)
    coords = swap(by_near(coords), NEAR)
    grad_part = dot(coords, grad_all, ((0, 2), (0, 1))) / TOKENS
    per = rank // n_near
    grad_own = total(swap(grad_part.astype(bf16).reshape(n_far, own, -1), FAR))
    moment_one = 0.9 * first_moment + 0.1 * grad_own
    moment_two = 0.999 * second_moment + 0.001 * grad_own * grad_own
    adam_step = moment_one / (1.0 - 0.9**10) / (jnp.sqrt(moment_two / (1.0 - 0.999**10)) + 1e-08)
    low_own = grad_own.astype(bf16)
    low = to_all(low_own, FAR, n_far).reshape(per, -1)
    low_rows = to_all(low_own, NEAR, n_near).reshape(n_near * own, -1)
    grad_rows = jnp.concatenate([grad_all.reshape(n_near * toks, -1), low_rows], axis=0)
    both = dot(low, grad_rows, ((1,), (1,))).astype(bf16)
    pieces = both.reshape(n_t, per // n_t, -1)
    mine = total(swap(pieces, TENSOR)).astype(bf16)
    both = to_all(mine, TENSOR, n_t).reshape(per, -1)
    n_tok = n_near * toks
    pull = dot(both[:, :n_tok], acts_all.reshape(n_tok, -1), ((1,), (0,))) * (
        jnp.sqrt(jnp.float32(D)) / TOKENS
    )
    grid = proj_t.reshape(*SIZES, own, -1)
    for a in FAR:
        here = lax.axis_index(a)
        grid = lax.dynamic_slice_in_dim(grid, here, 1, DP.index(a))
    proj_rows = grid.reshape(n_near * own, -1)
    correction = dot(both[:, n_tok:], proj_rows, ((1,), (0,)))
    step = total(swap((pull - correction).astype(bf16).reshape(n_far, own, -1), FAR))
    place = lax.axis_index(DP) * own
    own_rows = lax.dynamic_slice_in_dim(proj_t, place, own, 0).astype(jnp.float32)
    return (adam_step, own_rows + step)


def solution(mesh):
    fine = Mesh(mesh.devices.reshape(*SIZES, 4, 4), DP + TENSOR)
    whole = P(DP, TENSOR)
    placed = (whole, whole, P(None, TENSOR), whole, whole)
    return jax.shard_map(
        local, mesh=fine, in_specs=placed, out_specs=(whole, whole), check_vma=False
    )
```

time: 891 us -> 202 us (0.23)
  the two profiles are of different devices: /device:TPU:65 before, /device:TPU:8 now
where the time goes in v1:
time: 202 us
  blocking collectives  138 us (68%)
  waiting for transfers between devices  37.2 us (18%)
  starting transfers between devices  16.9 us (8%)
  matrix products  3.83 us (2%)
  local copies, waits for them, and re-layouts  3.12 us (2%)
  other arithmetic  2.15 us (1%)
    all_to_all x7, blocking collectives, swap(): return lax.all_to_all(pieces, axes, split_axis=0, concat_axis=0, tiled=True)  138 us
    all_to_all x4, waiting for transfers between devices, swap(): return lax.all_to_all(pieces, axes, split_axis=0, concat_axis=0, tiled=True)  37.2 us
    all_to_all x4, starting transfers between devices, swap(): return lax.all_to_all(pieces, axes, split_axis=0, concat_axis=0, tiled=True)  16.9 us
  transfers between devices with their start and end apart: 4, of which 4 were waited for; matrix products, arithmetic and copies ran while one was open for 0% of the time, Pallas kernels for 0%

profile of v1, /device:TPU:8, one launch (start us, length us, event | category | flops | bytes accessed | tf_op | source)
XLA Modules:
  0.0 201.5 jit_solution(7609639907726931087)
XLA Ops:
  0.6 1.4 fusion.5
  2.0 23.2 %all_to_all.55 = bf16[16,32,128]{2,1,0:T(8,128)(2,1)S(1)} all-to-all(bf16[16,32,128]{2,1,0:T(8,128)(2,1)S(1)} %bitcast.42), channel_id=1, replica_groups=mesh['yh'=2,'z3'=2,'z2'=2,'z1'=2,'z0'=2,'c'=2,'x'=4,'yl'=4] {'x','yl'}, dimensions={0} | all-to-all | bytes 262144 | tf_op jit(solution)/shard_map/all_to_all | solution.py:22
  25.2 0.0 copy-start.1
  25.3 11.9 %all_to_all.56 = bf16[16,32,128]{2,1,0:T(8,128)(2,1)S(1)} all-to-all(bf16[16,32,128]{2,1,0:T(8,128)(2,1)S(1)} %broadcast_in_dim.18), channel_id=1, replica_groups=mesh['yh'=2,'z3'=2,'z2'=2,'z1'=2,'z0'=2,'c'=2,'x'=4,'yl'=4] {'x','yl'}, dimensions={0} | all-to-all | bytes 262144 | tf_op jit(solution)/shard_map/all_to_all | solution.py:22
  37.2 0.0 copy-done.1
  37.2 0.8 broadcast_in_dim.19
  38.0 3.5 %all-to-all-start.3 = ((bf16[2,128,896]{2,1,0:T(8,128)(2,1)}), bf16[2,128,896]{2,1,0:T(8,128)(2,1)S(1)}, u32[]{:S(2)}, u32[]{:S(2)}) async-start(bf16[2,128,896]{2,1,0:T(8,128)(2,1)} %broadcast_in_dim.19), calls=%async_computation.3 | async-start | bytes 917504 | tf_op jit(solution)/shard_map/all_to_all | solution.py:22
  41.5 1.6 all-to-all-done.3
  43.1 3.8 %all_to_all.57 = bf16[2,256,128]{2,1,0:T(8,128)(2,1)S(1)} all-to-all(bf16[2,256,128]{2,1,0:T(8,128)(2,1)S(1)} %bitcast.41), channel_id=1, replica_groups=mesh['yh'=2,'z3'=2,'z2'=2,'z1'=2,'z0'=2,'c'=2,'x'=4,'yl'=4] {'c'}, dimensions={0} | all-to-all | bytes 262144 | tf_op jit(solution)/shard_map/all_to_all | solution.py:22
  47.0 0.3 fusion.2
  47.3 45.4 %all_to_all.58 = bf16[32,8,896]{2,1,0:T(8,128)(2,1)S(1)} all-to-all(bf16[32,8,896]{2,1,0:T(8,128)(2,1)S(1)} %fusion.2), channel_id=1, replica_groups=mesh['yh'=2,'z3'=2,'z2'=2,'z1'=2,'z0'=2,'c'=2,'x'=4,'yl'=4] {'yh','z3','..., dimensions={0} | all-to-all | bytes 917504 | tf_op jit(solution)/shard_map/all_to_all | solution.py:22
  92.7 0.0 copy-start.2
  92.7 0.0 copy-start.3
  92.7 0.1 convert_reduce_fusion
  92.8 0.7 copy-done.2
  93.4 0.0 copy-done.3
  93.4 0.6 fusion.21
  94.1 3.7 %all_to_all.59 = bf16[2,8,896]{2,1,0:T(8,128)(2,1)S(1)} all-to-all(bf16[2,8,896]{2,1,0:T(8,128)(2,1)S(1)} %broadcast_in_dim.21), channel_id=1, replica_groups=mesh['yh'=2,'z3'=2,'z2'=2,'z1'=2,'z0'=2,'c'=2,'x'=4,'yl'=4] {'c'}, dimensions={0} | all-to-all | bytes 57344 | tf_op jit(solution)/shard_map/all_to_all | solution.py:22
  97.9 37.7 %all_to_all.60 = bf16[32,8,896]{2,1,0:T(8,128)(2,1)S(1)} all-to-all(bf16[32,8,896]{2,1,0:T(8,128)(2,1)S(1)} %broadcast_in_dim.20), channel_id=1, replica_groups=mesh['yh'=2,'z3'=2,'z2'=2,'z1'=2,'z0'=2,'c'=2,'x'=4,'yl'=4] {'yh','z3','..., dimensions={0} | all-to-all | bytes 917504 | tf_op jit(solution)/shard_map/all_to_all | solution.py:22
  135.5 0.3 convolution_convert_fusion
  135.9 0.2 copy.8
  136.1 0.0 copy-start
  136.1 11.8 %all_to_all.61 = bf16[16,16,272]{2,1,0:T(8,128)(2,1)S(1)} all-to-all(bf16[16,16,272]{2,1,0:T(8,128)(2,1)S(1)} %bitcast.38), channel_id=1, replica_groups=mesh['yh'=2,'z3'=2,'z2'=2,'z1'=2,'z0'=2,'c'=2,'x'=4,'yl'=4] {'x','yl'}, dimensions={0} | all-to-all | bytes 278528 | tf_op jit(solution)/shard_map/all_to_all | solution.py:22
  147.9 0.0 copy-done
  147.9 0.7 broadcast_in_dim.23
  148.6 3.4 %all-to-all-start.9 = ((bf16[2,128,512]{2,1,0:T(8,128)(2,1)}), bf16[2,128,512]{2,1,0:T(8,128)(2,1)S(1)}, u32[]{:S(2)}, u32[]{:S(2)}) async-start(bf16[2,128,512]{2,1,0:T(8,128)(2,1)} %broadcast_in_dim.23), calls=%async_computation.9 | async-start | bytes 524288 | tf_op jit(solution)/shard_map/all_to_all | solution.py:22
  152.1 1.5 all-to-all-done.9
  153.6 0.7 broadcast_in_dim.22
  154.2 4.6 %all-to-all-start.8 = ((bf16[16,16,272]{2,1,0:T(8,128)(2,1)}), bf16[16,16,272]{2,1,0:T(8,128)(2,1)S(1)}, u32[]{:S(2)}, u32[]{:S(2)}) async-start(bf16[16,16,272]{2,1,0:T(8,128)(2,1)} %broadcast_in_dim.22), calls=%async_computation.8 | async-start | bytes 393216 | tf_op jit(solution)/shard_map/all_to_all | solution.py:22
  158.9 8.7 %all-to-all-done.8 = bf16[16,16,272]{2,1,0:T(8,128)(2,1)S(1)} async-done(((bf16[16,16,272]{2,1,0:T(8,128)(2,1)}), bf16[16,16,272]{2,1,0:T(8,128)(2,1)S(1)}, u32[]{:S(2)}, u32[]{:S(2)}) %all-to-all-start.8) | async-done | bytes 139296 | tf_op jit(solution)/shard_map/all_to_all | solution.py:22
  167.5 0.2 convolution_multiply_fusion
  167.7 1.6 fusion.4
  169.4 5.4 %all-to-all-start.10 = ((bf16[32,8,512]{2,1,0:T(8,128)(2,1)}), bf16[32,8,512]{2,1,0:T(8,128)(2,1)S(1)}, u32[]{:S(2)}, u32[]{:S(2)}) async-start(bf16[32,8,512]{2,1,0:T(8,128)(2,1)} %fusion.4), calls=%async_computation.10 | async-start | bytes 524288 | tf_op jit(solution)/shard_map/all_to_all | solution.py:22
  174.8 25.4 %all-to-all-done.10 = bf16[32,8,512]{2,1,0:T(8,128)(2,1)S(1)} async-done(((bf16[32,8,512]{2,1,0:T(8,128)(2,1)}), bf16[32,8,512]{2,1,0:T(8,128)(2,1)S(1)}, u32[]{:S(2)}, u32[]{:S(2)}) %all-to-all-start.10) | async-done | bytes 262176 | tf_op jit(solution)/shard_map/all_to_all | solution.py:22
  200.2 1.3 convert_add_fusion
  (7 shorter events, 0.2 us)
Async XLA Ops:
  25.2 11.9 %copy-start.1 = (bf16[128,896]{1,0:T(8,128)(2,1)S(1)}, bf16[128,896]{1,0:T(8,128)(2,1)}, u32[]{:S(2)}) copy-start(bf16[128,896]{1,0:T(8,128)(2,1)} %param.6) | copy-start | bytes 688132
  38.0 5.2 %all-to-all-start.3 = ((bf16[2,128,896]{2,1,0:T(8,128)(2,1)}), bf16[2,128,896]{2,1,0:T(8,128)(2,1)S(1)}, u32[]{:S(2)}, u32[]{:S(2)}) async-start(bf16[2,128,896]{2,1,0:T(8,128)(2,1)} %broadcast_in_dim.19), calls=%async_computation.3 | async-start | bytes 917504 | tf_op jit(solution)/shard_map/all_to_all | solution.py:22
  92.7 0.7 copy-start.2
  92.7 0.8 copy-start.3
  136.1 11.8 %copy-start = (bf16[128,512]{1,0:T(8,128)(2,1)S(1)}, bf16[128,512]{1,0:T(8,128)(2,1)}, u32[]{:S(2)}) copy-start(bf16[128,512]{1,0:T(8,128)(2,1)} %param.5) | copy-start | bytes 393220
  148.6 5.0 %all-to-all-start.9 = ((bf16[2,128,512]{2,1,0:T(8,128)(2,1)}), bf16[2,128,512]{2,1,0:T(8,128)(2,1)S(1)}, u32[]{:S(2)}, u32[]{:S(2)}) async-start(bf16[2,128,512]{2,1,0:T(8,128)(2,1)} %broadcast_in_dim.23), calls=%async_computation.9 | async-start | bytes 524288 | tf_op jit(solution)/shard_map/all_to_all | solution.py:22
  154.2 13.3 %all-to-all-start.8 = ((bf16[16,16,272]{2,1,0:T(8,128)(2,1)}), bf16[16,16,272]{2,1,0:T(8,128)(2,1)S(1)}, u32[]{:S(2)}, u32[]{:S(2)}) async-start(bf16[16,16,272]{2,1,0:T(8,128)(2,1)} %broadcast_in_dim.22), calls=%async_computation.8 | async-start | bytes 393216 | tf_op jit(solution)/shard_map/all_to_all | solution.py:22
  169.4 30.8 %all-to-all-start.10 = ((bf16[32,8,512]{2,1,0:T(8,128)(2,1)}), bf16[32,8,512]{2,1,0:T(8,128)(2,1)S(1)}, u32[]{:S(2)}, u32[]{:S(2)}) async-start(bf16[32,8,512]{2,1,0:T(8,128)(2,1)} %fusion.4), calls=%async_computation.10 | async-start | bytes 524288 | tf_op jit(solution)/shard_map/all_to_all | solution.py:22

commit v2 on v1

v2 whole, which is shorter than its diff:
```python
import jax
import jax.numpy as jnp
from jax import lax
from jax.sharding import Mesh, PartitionSpec as P

D = 8192
TOKENS = 8192
DP = ("yh", "z", "c")
TENSOR = ("x", "yl")
OWN = 8


def swap(pieces, axes):
    return lax.all_to_all(pieces, axes, split_axis=0, concat_axis=0, tiled=True)


def to_all(x, axes, count):
    return swap(jnp.broadcast_to(x, (count, *x.shape)), axes)


def total(pieces):
    return jnp.sum(pieces.astype(jnp.float32), axis=0)


def dot(left, right, dims):
    return lax.dot_general(left, right, (dims, ((), ())), preferred_element_type=jnp.float32)


def pair(x, axis):
    return jnp.stack([x, lax.ppermute(x, axis, [(0, 1), (1, 0)])])


def near(x, axes):
    for axis in axes:
        x = pair(x, axis)
    return x


def from_own(x, axes):
    for dim, axis in enumerate(axes):
        x = jnp.where(lax.axis_index(axis) == 0, x, jnp.flip(x, dim))
    return x


def step(acts, grad_out, proj_t, first_moment, second_moment):
    bf16 = jnp.bfloat16
    root = jnp.sqrt(jnp.float32(D))
    grad_all = near(grad_out, ("yh", "c"))
    acts_all = near(acts, ("yh", "c"))
    rows = proj_t.reshape(2, 16, 2, OWN, -1)
    rows = lax.dynamic_index_in_dim(rows, lax.axis_index("z"), 1, keepdims=False)
    rows = from_own(rows, ("yh", "c")).reshape(4 * OWN, -1)
    own_rows = lax.dynamic_slice_in_dim(proj_t, lax.axis_index(DP) * OWN, OWN, 0)
    own_rows = lax.optimization_barrier(own_rows.astype(jnp.float32))
    part = (dot(proj_t, acts, ((1,), (1,))) * (1.0 / root)).astype(bf16)
    part = part.reshape(2, 4, 4, 2, OWN, 128).transpose(1, 3, 0, 2, 4, 5)
    got = swap(part.reshape(8, 64, 128), ("x", "c"))
    part = total(got.reshape(4, 2, 2, 4, OWN, 128)).astype(bf16)
    part = part.transpose(2, 1, 0, 3, 4)
    got = swap(part.reshape(8, 2 * OWN, 128), ("yl", "yh"))
    part = from_own(total(got.reshape(4, 2, 2, OWN, 128)), ("yh", "c")).astype(bf16)
    coords = to_all(part, TENSOR, 16)
    coords = coords.transpose(2, 1, 0, 3, 4).reshape(2, 2, 128, 128)
    grad_part = (dot(coords, grad_all, ((0, 1, 3), (0, 1, 2))) / TOKENS).astype(bf16)
    grad_own = total(swap(grad_part.reshape(16, OWN, -1), "z"))
    moment_one = 0.9 * first_moment + 0.1 * grad_own
    moment_two = 0.999 * second_moment + 0.001 * grad_own * grad_own
    adam_step = moment_one / (1.0 - 0.9**10) / (jnp.sqrt(moment_two / (1.0 - 0.999**10)) + 1e-08)
    low_own = grad_own.astype(bf16)
    low = to_all(low_own, "z", 16).reshape(128, -1)
    low_rows = near(low_own, ("c", "yh")).reshape(4 * OWN, -1)
    back = dot(low, grad_all.reshape(512, -1), ((1,), (1,))).astype(bf16)
    cross = dot(low, low_rows, ((1,), (1,))).astype(bf16)
    both = jnp.concatenate([back, cross], axis=1)
    both = total(swap(both.reshape(16, OWN, 544), TENSOR)).astype(bf16)
    both = to_all(both, TENSOR, 16).reshape(128, 544)
    pull = dot(both[:, :512], acts_all.reshape(512, -1), ((1,), (0,))) * (root / TOKENS)
    correction = dot(both[:, 512:], rows, ((1,), (0,)))
    moved = total(swap((pull - correction).astype(bf16).reshape(16, OWN, -1), "z"))
    return (adam_step, own_rows + moved)


def solution(mesh):
    fine = Mesh(mesh.devices.reshape(2, 16, 2, 4, 4), DP + TENSOR)
    whole = P(DP, TENSOR)
    placed = (whole, whole, P(None, TENSOR), whole, whole)
    return jax.shard_map(
        step, mesh=fine, in_specs=placed, out_specs=(whole, whole), check_vma=False
    )
```

time: 202 us -> 168 us (0.83)
  blocking collectives: 138 us -> 50.8 us
  starting transfers between devices: 16.9 us -> 63.2 us
  waiting for transfers between devices: 37.2 us -> 42.3 us
    all_to_all x7 -> x3, blocking collectives: 138 us -> 50.8 us  [swap(): return lax.all_to_all(pieces, axes, split_axis=0, concat_axis=0, tiled=True)]
    all_to_all x4 -> x5, starting transfers between devices: 16.9 us -> 41.3 us  [swap(): return lax.all_to_all(pieces, axes, split_axis=0, concat_axis=0, tiled=True)]
    ppermute x0 -> x6, starting transfers between devices: none -> 21.9 us  [pair(): return jnp.stack([x, lax.ppermute(x, axis, [(0, 1), (1, 0)])])]
    ppermute x0 -> x6, waiting for transfers between devices: none -> 16.7 us  [pair(): return jnp.stack([x, lax.ppermute(x, axis, [(0, 1), (1, 0)])])]
    all_to_all x4 -> x5, waiting for transfers between devices: 37.2 us -> 25.7 us  [swap(): return lax.all_to_all(pieces, axes, split_axis=0, concat_axis=0, tiled=True)]
  transfers between devices with their start and end apart: 4 -> 11, of which waited for: 4 -> 7; matrix products, arithmetic and copies ran while one was open for 0% -> 2% of each run, Pallas kernels for 0% -> 0%
where the time goes in v2:
time: 168 us; the launch traced here: 167 us
  starting transfers between devices  63.2 us (38%)
  blocking collectives  50.8 us (30%)
  waiting for transfers between devices  42.3 us (25%)
  local copies, waits for them, and re-layouts  3.69 us (2%)
  matrix products  3.31 us (2%)
  other arithmetic  3.07 us (2%)
    all_to_all x3, blocking collectives, swap(): return lax.all_to_all(pieces, axes, split_axis=0, concat_axis=0, tiled=True)  50.8 us
    all_to_all x5, starting transfers between devices, swap(): return lax.all_to_all(pieces, axes, split_axis=0, concat_axis=0, tiled=True)  41.3 us
    all_to_all x5, waiting for transfers between devices, swap(): return lax.all_to_all(pieces, axes, split_axis=0, concat_axis=0, tiled=True)  25.7 us
    ppermute x6, starting transfers between devices, pair(): return jnp.stack([x, lax.ppermute(x, axis, [(0, 1), (1, 0)])])  21.9 us
    ppermute x6, waiting for transfers between devices, pair(): return jnp.stack([x, lax.ppermute(x, axis, [(0, 1), (1, 0)])])  16.7 us
  transfers between devices with their start and end apart: 11, of which 7 were waited for; matrix products, arithmetic and copies ran while one was open for 2% of the time, Pallas kernels for 0%

profile of v2, /device:TPU:8, one launch (start us, length us, event | category | flops | bytes accessed | tf_op | source)
XLA Modules:
  0.0 167.3 jit_solution(6405706473421569688)
XLA Ops:
  0.6 1.4 fusion.4
  2.0 0.0 copy-start.1
  2.0 10.3 %all_to_all.40 = bf16[8,64,128]{2,1,0:T(8,128)(2,1)S(1)} all-to-all(bf16[8,64,128]{2,1,0:T(8,128)(2,1)S(1)} %bitcast.72), channel_id=1, replica_groups=mesh['yh'=2,'z'=16,'c'=2,'x'=4,'yl'=4] {'x','c'}, dimensions={0} | all-to-all | bytes 262144 | tf_op jit(solution)/shard_map/all_to_all | solution.py:14
  12.4 0.6 copy.16
  13.0 14.6 %all-to-all-start.1 = ((bf16[8,16,128]{2,1,0:T(8,128)(2,1)}), bf16[8,16,128]{2,1,0:T(8,128)(2,1)S(1)}, u32[]{:S(2)}, u32[]{:S(2)}) async-start(bf16[8,16,128]{2,1,0:T(8,128)(2,1)} %bitcast.5), calls=%async_computation.1 | async-start | bytes 65536 | tf_op jit(solution)/shard_map/all_to_all | solution.py:14
  27.6 0.0 copy-done.1
  27.6 6.4 %collective-permute-start = (bf16[128,896]{1,0:T(8,128)(2,1)S(1)}, bf16[128,896]{1,0:T(8,128)(2,1)S(1)}, u32[]{:S(2)}, u32[]{:S(2)}) collective-permute-start(bf16[128,896]{1,0:T(8,128)(2,1)S(1)} %copy-done.1), channel_id=1, source_target_pairs={{0,512},{512,0},{1,513},{513,1},{2,514},{514,2},{3,515},{515,3},{4... | collective-permute-start | bytes 688136 | tf_op jit(solution)/shard_map/ppermute | solution.py:30
  34.0 0.1 all-to-all-done.1
  34.1 11.0 %collective-permute-done = bf16[128,896]{1,0:T(8,128)(2,1)S(1)} collective-permute-done((bf16[128,896]{1,0:T(8,128)(2,1)S(1)}, bf16[128,896]{1,0:T(8,128)(2,1)S(1)}, u32[]{:S(2)}, u32[]{:S(2)}) %collective-permute-start) | collective-permute-done | bytes 229408 | tf_op jit(solution)/shard_map/ppermute | solution.py:30
  45.2 0.1 fusion.22
  45.3 1.9 %collective-permute-start.1 = (bf16[2,128,896]{2,1,0:T(8,128)(2,1)S(1)}, bf16[2,128,896]{2,1,0:T(8,128)(2,1)S(1)}, u32[]{:S(2)}, u32[]{:S(2)}) collective-permute-start(bf16[2,128,896]{2,1,0:T(8,128)(2,1)S(1)} %get-tuple-element.3), channel_id=1, source_target_pairs={{0,16},{16,0},{1,17},{17,1},{2,18},{18,2},{3,19},{19,3},{4,20},{20... | collective-permute-start | bytes 1376264 | tf_op jit(solution)/shard_map/ppermute | solution.py:30
  47.2 12.2 %all_to_all.41 = bf16[16,2,2,8,128]{4,3,1,2,0:T(8,128)(2,1)S(1)} all-to-all(bf16[16,2,2,8,128]{4,3,1,2,0:T(8,128)(2,1)S(1)} %broadcast_in_dim.9), channel_id=1, replica_groups=mesh['yh'=2,'z'=16,'c'=2,'x'=4,'yl'=4] {'x','yl'}, dimensions={0} | all-to-all | bytes 262144 | tf_op jit(solution)/shard_map/all_to_all | solution.py:14
  59.4 0.0 collective-permute-done.1
  59.4 0.3 fusion.3
  59.7 28.3 %all_to_all.42 = bf16[16,8,896]{2,1,0:T(8,128)(2,1)S(1)} all-to-all(bf16[16,8,896]{2,1,0:T(8,128)(2,1)S(1)} %fusion.3), channel_id=1, replica_groups=mesh['yh'=2,'z'=16,'c'=2,'x'=4,'yl'=4] {'z'}, dimensions={0} | all-to-all | bytes 458752 | tf_op jit(solution)/shard_map/all_to_all | solution.py:14
  88.1 0.7 copy-done.2
  88.8 0.0 copy-done.3
  88.8 0.6 fusion.23
  89.5 0.7 broadcast_in_dim.10
  90.2 5.5 %all-to-all-start.4 = ((bf16[16,8,896]{2,1,0:T(8,128)(2,1)}), bf16[16,8,896]{2,1,0:T(8,128)(2,1)S(1)}, u32[]{:S(2)}, u32[]{:S(2)}) async-start(bf16[16,8,896]{2,1,0:T(8,128)(2,1)} %broadcast_in_dim.10), calls=%async_computation.4 | async-start | bytes 458752 | tf_op jit(solution)/shard_map/all_to_all | solution.py:14
  95.7 0.0 copy-done
  95.7 5.4 %collective-permute-start.4 = (bf16[128,512]{1,0:T(8,128)(2,1)S(1)}, bf16[128,512]{1,0:T(8,128)(2,1)S(1)}, u32[]{:S(2)}, u32[]{:S(2)}) collective-permute-start(bf16[128,512]{1,0:T(8,128)(2,1)S(1)} %copy-done), channel_id=1, source_target_pairs={{0,512},{512,0},{1,513},{513,1},{2,514},{514,2},{3,515},{515,3},{4... | collective-permute-start | bytes 393224 | tf_op jit(solution)/shard_map/ppermute | solution.py:30
  101.1 1.9 %collective-permute-start.2 = (bf16[8,896]{1,0:T(8,128)(2,1)S(1)}, bf16[8,896]{1,0:T(8,128)(2,1)S(1)}, u32[]{:S(2)}, u32[]{:S(2)}) collective-permute-start(bf16[8,896]{1,0:T(8,128)(2,1)S(1)} %get-tuple-element.8), channel_id=1, source_target_pairs={{0,16},{16,0},{1,17},{17,1},{2,18},{18,2},{3,19},{19,3},{4,20},{20... | collective-permute-start | bytes 43016 | tf_op jit(solution)/shard_map/ppermute | solution.py:30
  103.1 0.8 dynamic-slice_bitcast_fusion
  103.8 0.4 collective-permute-done.2
  104.2 4.3 %collective-permute-start.3 = (bf16[2,8,896]{2,1,0:T(8,128)(2,1)S(1)}, bf16[2,8,896]{2,1,0:T(8,128)(2,1)S(1)}, u32[]{:S(2)}, u32[]{:S(2)}) collective-permute-start(bf16[2,8,896]{2,1,0:T(8,128)(2,1)S(1)} %get-tuple-element.7), channel_id=1, source_target_pairs={{0,512},{512,0},{1,513},{513,1},{2,514},{514,2},{3,515},{515,3},{4... | collective-permute-start | bytes 86024 | tf_op jit(solution)/shard_map/ppermute | solution.py:30
  108.5 0.1 pad_maximum_fusion
  108.6 5.2 %collective-permute-done.3 = bf16[2,8,896]{2,1,0:T(8,128)(2,1)S(1)} collective-permute-done((bf16[2,8,896]{2,1,0:T(8,128)(2,1)S(1)}, bf16[2,8,896]{2,1,0:T(8,128)(2,1)S(1)}, u32[]{:S(2)}, u32[]{:S(2)}) %collective-permute-start.3) | collective-permute-done | bytes 28704 | tf_op jit(solution)/shard_map/ppermute | solution.py:30
  113.9 0.0 all-to-all-done.4
  113.9 0.4 convolution_convert_fusion
  114.4 0.2 convolution_convert_fusion.1
  114.5 0.1 copy.19
  114.7 0.7 maximum_bitcast_fusion
  115.4 4.8 %all-to-all-start.5 = ((bf16[16,8,544]{2,1,0:T(8,128)(2,1)}), bf16[16,8,544]{2,1,0:T(8,128)(2,1)S(1)}, u32[]{:S(2)}, u32[]{:S(2)}) async-start(bf16[16,8,544]{2,1,0:T(8,128)(2,1)} %maximum_bitcast_fusion), calls=%async_computation.5 | async-start | bytes 327680 | tf_op jit(solution)/shard_map/all_to_all | solution.py:14
  120.2 0.0 collective-permute-done.4
  120.2 1.9 %collective-permute-start.5 = (bf16[2,128,512]{2,1,0:T(8,128)(2,1)S(1)}, bf16[2,128,512]{2,1,0:T(8,128)(2,1)S(1)}, u32[]{:S(2)}, u32[]{:S(2)}) collective-permute-start(bf16[2,128,512]{2,1,0:T(8,128)(2,1)S(1)} %get-tuple-element.5), channel_id=1, source_target_pairs={{0,16},{16,0},{1,17},{17,1},{2,18},{18,2},{3,19},{19,3},{4,20},{20... | collective-permute-start | bytes 786440 | tf_op jit(solution)/shard_map/ppermute | solution.py:30
  122.2 5.5 %all-to-all-done.5 = bf16[16,8,544]{2,1,0:T(8,128)(2,1)S(1)} async-done(((bf16[16,8,544]{2,1,0:T(8,128)(2,1)}), bf16[16,8,544]{2,1,0:T(8,128)(2,1)S(1)}, u32[]{:S(2)}, u32[]{:S(2)}) %all-to-all-start.5) | async-done | bytes 139296 | tf_op jit(solution)/shard_map/all_to_all | solution.py:14
  127.7 0.7 broadcast_in_dim.11
  128.4 4.4 %all-to-all-start.6 = ((bf16[16,8,544]{2,1,0:T(8,128)(2,1)}), bf16[16,8,544]{2,1,0:T(8,128)(2,1)S(1)}, u32[]{:S(2)}, u32[]{:S(2)}) async-start(bf16[16,8,544]{2,1,0:T(8,128)(2,1)} %broadcast_in_dim.11), calls=%async_computation.6 | async-start | bytes 327680 | tf_op jit(solution)/shard_map/all_to_all | solution.py:14
  132.8 0.0 collective-permute-done.5
  132.8 0.1 pad_maximum_fusion.1
  132.9 7.5 %all-to-all-done.6 = bf16[16,8,544]{2,1,0:T(8,128)(2,1)S(1)} async-done(((bf16[16,8,544]{2,1,0:T(8,128)(2,1)}), bf16[16,8,544]{2,1,0:T(8,128)(2,1)S(1)}, u32[]{:S(2)}, u32[]{:S(2)}) %all-to-all-start.6) | async-done | bytes 139296 | tf_op jit(solution)/shard_map/all_to_all | solution.py:14
  140.4 0.2 fusion.12
  140.6 0.9 fusion.6
  141.5 12.0 %all-to-all-start.7 = ((bf16[16,8,512]{2,1,0:T(8,128)(2,1)}), bf16[16,8,512]{2,1,0:T(8,128)(2,1)S(1)}, u32[]{:S(2)}, u32[]{:S(2)}) async-start(bf16[16,8,512]{2,1,0:T(8,128)(2,1)} %fusion.6), calls=%async_computation.7 | async-start | bytes 262144 | tf_op jit(solution)/shard_map/all_to_all | solution.py:14
  153.5 0.7 dynamic-slice_convert_fusion
  154.2 12.5 %all-to-all-done.7 = bf16[16,8,512]{2,1,0:T(8,128)(2,1)S(1)} async-done(((bf16[16,8,512]{2,1,0:T(8,128)(2,1)}), bf16[16,8,512]{2,1,0:T(8,128)(2,1)S(1)}, u32[]{:S(2)}, u32[]{:S(2)}) %all-to-all-start.7) | async-done | bytes 131104 | tf_op jit(solution)/shard_map/all_to_all | solution.py:14
  166.7 0.6 add.36
  (18 shorter events, 0.3 us)
Async XLA Ops:
  2.0 25.6 %copy-start.1 = (bf16[128,896]{1,0:T(8,128)(2,1)S(1)}, bf16[128,896]{1,0:T(8,128)(2,1)}, u32[]{:S(2)}) copy-start(bf16[128,896]{1,0:T(8,128)(2,1)} %param.6) | copy-start | bytes 688132
  13.0 21.1 %all-to-all-start.1 = ((bf16[8,16,128]{2,1,0:T(8,128)(2,1)}), bf16[8,16,128]{2,1,0:T(8,128)(2,1)S(1)}, u32[]{:S(2)}, u32[]{:S(2)}) async-start(bf16[8,16,128]{2,1,0:T(8,128)(2,1)} %bitcast.5), calls=%async_computation.1 | async-start | bytes 65536 | tf_op jit(solution)/shard_map/all_to_all | solution.py:14
  27.6 17.6 %collective-permute-start = (bf16[128,896]{1,0:T(8,128)(2,1)S(1)}, bf16[128,896]{1,0:T(8,128)(2,1)S(1)}, u32[]{:S(2)}, u32[]{:S(2)}) collective-permute-start(bf16[128,896]{1,0:T(8,128)(2,1)S(1)} %copy-done.1), channel_id=1, source_target_pairs={{0,512},{512,0},{1,513},{513,1},{2,514},{514,2},{3,515},{515,3},{4... | collective-permute-start | bytes 688136 | tf_op jit(solution)/shard_map/ppermute | solution.py:30
  45.3 14.1 %collective-permute-start.1 = (bf16[2,128,896]{2,1,0:T(8,128)(2,1)S(1)}, bf16[2,128,896]{2,1,0:T(8,128)(2,1)S(1)}, u32[]{:S(2)}, u32[]{:S(2)}) collective-permute-start(bf16[2,128,896]{2,1,0:T(8,128)(2,1)S(1)} %get-tuple-element.3), channel_id=1, source_target_pairs={{0,16},{16,0},{1,17},{17,1},{2,18},{18,2},{3,19},{19,3},{4,20},{20... | collective-permute-start | bytes 1376264 | tf_op jit(solution)/shard_map/ppermute | solution.py:30
  88.1 0.7 copy-start.2
  88.1 0.8 copy-start.3
  90.2 5.5 %copy-start = (bf16[128,512]{1,0:T(8,128)(2,1)S(1)}, bf16[128,512]{1,0:T(8,128)(2,1)}, u32[]{:S(2)}) copy-start(bf16[128,512]{1,0:T(8,128)(2,1)} %param.5) | copy-start | bytes 393220
  90.2 23.7 %all-to-all-start.4 = ((bf16[16,8,896]{2,1,0:T(8,128)(2,1)}), bf16[16,8,896]{2,1,0:T(8,128)(2,1)S(1)}, u32[]{:S(2)}, u32[]{:S(2)}) async-start(bf16[16,8,896]{2,1,0:T(8,128)(2,1)} %broadcast_in_dim.10), calls=%async_computation.4 | async-start | bytes 458752 | tf_op jit(solution)/shard_map/all_to_all | solution.py:14
  95.7 24.5 %collective-permute-start.4 = (bf16[128,512]{1,0:T(8,128)(2,1)S(1)}, bf16[128,512]{1,0:T(8,128)(2,1)S(1)}, u32[]{:S(2)}, u32[]{:S(2)}) collective-permute-start(bf16[128,512]{1,0:T(8,128)(2,1)S(1)} %copy-done), channel_id=1, source_target_pairs={{0,512},{512,0},{1,513},{513,1},{2,514},{514,2},{3,515},{515,3},{4... | collective-permute-start | bytes 393224 | tf_op jit(solution)/shard_map/ppermute | solution.py:30
  101.1 3.1 %collective-permute-start.2 = (bf16[8,896]{1,0:T(8,128)(2,1)S(1)}, bf16[8,896]{1,0:T(8,128)(2,1)S(1)}, u32[]{:S(2)}, u32[]{:S(2)}) collective-permute-start(bf16[8,896]{1,0:T(8,128)(2,1)S(1)} %get-tuple-element.8), channel_id=1, source_target_pairs={{0,16},{16,0},{1,17},{17,1},{2,18},{18,2},{3,19},{19,3},{4,20},{20... | collective-permute-start | bytes 43016 | tf_op jit(solution)/shard_map/ppermute | solution.py:30
  104.2 9.7 %collective-permute-start.3 = (bf16[2,8,896]{2,1,0:T(8,128)(2,1)S(1)}, bf16[2,8,896]{2,1,0:T(8,128)(2,1)S(1)}, u32[]{:S(2)}, u32[]{:S(2)}) collective-permute-start(bf16[2,8,896]{2,1,0:T(8,128)(2,1)S(1)} %get-tuple-element.7), channel_id=1, source_target_pairs={{0,512},{512,0},{1,513},{513,1},{2,514},{514,2},{3,515},{515,3},{4... | collective-permute-start | bytes 86024 | tf_op jit(solution)/shard_map/ppermute | solution.py:30
  115.4 12.4 %all-to-all-start.5 = ((bf16[16,8,544]{2,1,0:T(8,128)(2,1)}), bf16[16,8,544]{2,1,0:T(8,128)(2,1)S(1)}, u32[]{:S(2)}, u32[]{:S(2)}) async-start(bf16[16,8,544]{2,1,0:T(8,128)(2,1)} %maximum_bitcast_fusion), calls=%async_computation.5 | async-start | bytes 327680 | tf_op jit(solution)/shard_map/all_to_all | solution.py:14
  120.2 12.6 %collective-permute-start.5 = (bf16[2,128,512]{2,1,0:T(8,128)(2,1)S(1)}, bf16[2,128,512]{2,1,0:T(8,128)(2,1)S(1)}, u32[]{:S(2)}, u32[]{:S(2)}) collective-permute-start(bf16[2,128,512]{2,1,0:T(8,128)(2,1)S(1)} %get-tuple-element.5), channel_id=1, source_target_pairs={{0,16},{16,0},{1,17},{17,1},{2,18},{18,2},{3,19},{19,3},{4,20},{20... | collective-permute-start | bytes 786440 | tf_op jit(solution)/shard_map/ppermute | solution.py:30
  128.4 12.0 %all-to-all-start.6 = ((bf16[16,8,544]{2,1,0:T(8,128)(2,1)}), bf16[16,8,544]{2,1,0:T(8,128)(2,1)S(1)}, u32[]{:S(2)}, u32[]{:S(2)}) async-start(bf16[16,8,544]{2,1,0:T(8,128)(2,1)} %broadcast_in_dim.11), calls=%async_computation.6 | async-start | bytes 327680 | tf_op jit(solution)/shard_map/all_to_all | solution.py:14
  141.5 25.2 %all-to-all-start.7 = ((bf16[16,8,512]{2,1,0:T(8,128)(2,1)}), bf16[16,8,512]{2,1,0:T(8,128)(2,1)S(1)}, u32[]{:S(2)}, u32[]{:S(2)}) async-start(bf16[16,8,512]{2,1,0:T(8,128)(2,1)} %fusion.6), calls=%async_computation.7 | async-start | bytes 262144 | tf_op jit(solution)/shard_map/all_to_all | solution.py:14

commit v3 on v2

--- a/solution.py
+++ b/solution.py
@@ -53,12 +53,9 @@
     own_rows = lax.dynamic_slice_in_dim(proj_t, lax.axis_index(DP) * OWN, OWN, 0)
     own_rows = lax.optimization_barrier(own_rows.astype(jnp.float32))
     part = (dot(proj_t, acts, ((1,), (1,))) * (1.0 / root)).astype(bf16)
-    part = part.reshape(2, 4, 4, 2, OWN, 128).transpose(1, 3, 0, 2, 4, 5)
-    got = swap(part.reshape(8, 64, 128), ("x", "c"))
-    part = total(got.reshape(4, 2, 2, 4, OWN, 128)).astype(bf16)
-    part = part.transpose(2, 1, 0, 3, 4)
-    got = swap(part.reshape(8, 2 * OWN, 128), ("yl", "yh"))
-    part = from_own(total(got.reshape(4, 2, 2, OWN, 128)), ("yh", "c")).astype(bf16)
+    got = swap(part.reshape(64, OWN, 128), ("yh", "x", "yl", "c"))
+    part = jnp.sum(got.reshape(2, 16, 2, OWN, 128).astype(jnp.float32), axis=1)
+    part = from_own(part, ("yh", "c")).astype(bf16)
     coords = to_all(part, TENSOR, 16)
     coords = coords.transpose(2, 1, 0, 3, 4).reshape(2, 2, 128, 128)
     grad_part = (dot(coords, grad_all, ((0, 1, 3), (0, 1, 2))) / TOKENS).astype(bf16)

time: 168 us -> 152 us (0.905)
  blocking collectives: 50.8 us -> 37.6 us
  waiting for transfers between devices: 42.3 us -> 38.1 us
    all_to_all x3 -> x2, blocking collectives: 50.8 us -> 37.6 us  [swap(): return lax.all_to_all(pieces, axes, split_axis=0, concat_axis=0, tiled=True)]
    ppermute x6, waiting for transfers between devices: 16.7 us -> 4.08 us  [pair(): return jnp.stack([x, lax.ppermute(x, axis, [(0, 1), (1, 0)])])]
    all_to_all x5, waiting for transfers between devices: 25.7 us -> 34 us  [swap(): return lax.all_to_all(pieces, axes, split_axis=0, concat_axis=0, tiled=True)]
  transfers between devices with their start and end apart: 11 -> 11, of which waited for: 7 -> 7; matrix products, arithmetic and copies ran while one was open for 2% -> 4% of each run, Pallas kernels for 0% -> 0%
where the time goes in v3:
time: 152 us; the launch traced here: 151 us
  starting transfers between devices  64.4 us (42%)
  waiting for transfers between devices  38.1 us (25%)
  blocking collectives  37.6 us (25%)
  matrix products  3.97 us (3%)
  local copies, waits for them, and re-layouts  3.08 us (2%)
  other arithmetic  3.08 us (2%)
    all_to_all x5, starting transfers between devices, swap(): return lax.all_to_all(pieces, axes, split_axis=0, concat_axis=0, tiled=True)  42 us
    all_to_all x2, blocking collectives, swap(): return lax.all_to_all(pieces, axes, split_axis=0, concat_axis=0, tiled=True)  37.6 us
    all_to_all x5, waiting for transfers between devices, swap(): return lax.all_to_all(pieces, axes, split_axis=0, concat_axis=0, tiled=True)  34 us
    ppermute x6, starting transfers between devices, pair(): return jnp.stack([x, lax.ppermute(x, axis, [(0, 1), (1, 0)])])  22.5 us
    ppermute x6, waiting for transfers between devices, pair(): return jnp.stack([x, lax.ppermute(x, axis, [(0, 1), (1, 0)])])  4.08 us
    dot_general x6, matrix products, dot(): lax.dot_general(left, right, (dims, ((), ())), preferred_element_type=jnp...  3.97 us
  transfers between devices with their start and end apart: 11, of which 7 were waited for; matrix products, arithmetic and copies ran while one was open for 4% of the time, Pallas kernels for 0%

profile of v3, /device:TPU:8, one launch (start us, length us, event | category | flops | bytes accessed | tf_op | source)
XLA Modules:
  0.0 151.2 jit_solution(14679492010183517193)
XLA Ops:
  0.6 6.8 %collective-permute-start = (bf16[128,896]{1,0:T(8,128)(2,1)}, bf16[128,896]{1,0:T(8,128)(2,1)S(1)}, u32[]{:S(2)}, u32[]{:S(2)}) collective-permute-start(bf16[128,896]{1,0:T(8,128)(2,1)} %param.6), channel_id=1, source_target_pairs={{0,512},{512,0},{1,513},{513,1},{2,514},{514,2},{3,515},{515,3},{4... | collective-permute-start | bytes 688136 | tf_op jit(solution)/shard_map/ppermute | solution.py:30
  7.5 2.0 %fusion.6 = bf16[64,8,128]{2,1,0:T(8,128)(2,1)} fusion(bf16[512,512]{1,0:T(8,128)(2,1)} %param.7, bf16[128,512]{1,0:T(8,128)(2,1)} %param.5), kind=kOutput, calls=%fused_computation.10 | convolution fusion | flops 67239936 | bytes 786432 | tf_op jit(solution)/shard_map/dot_general | solution.py:26
  9.5 0.0 copy-start.1
  9.5 16.0 %all-to-all-start = ((bf16[64,8,128]{2,1,0:T(8,128)(2,1)}), bf16[64,8,128]{2,1,0:T(8,128)(2,1)S(1)}, u32[]{:S(2)}, u32[]{:S(2)}) async-start(bf16[64,8,128]{2,1,0:T(8,128)(2,1)} %fusion.6), calls=%async_computation | async-start | bytes 262144 | tf_op jit(solution)/shard_map/all_to_all | solution.py:14
  25.5 0.0 collective-permute-done
  25.6 0.0 copy-done.1
  25.6 0.1 fusion.23
  25.6 2.0 %collective-permute-start.1 = (bf16[2,128,896]{2,1,0:T(8,128)(2,1)S(1)}, bf16[2,128,896]{2,1,0:T(8,128)(2,1)S(1)}, u32[]{:S(2)}, u32[]{:S(2)}) collective-permute-start(bf16[2,128,896]{2,1,0:T(8,128)(2,1)S(1)} %get-tuple-element.3), channel_id=1, source_target_pairs={{0,16},{16,0},{1,17},{17,1},{2,18},{18,2},{3,19},{19,3},{4,20},{20... | collective-permute-start | bytes 1376264 | tf_op jit(solution)/shard_map/ppermute | solution.py:30
  27.7 8.3 %all-to-all-done = bf16[64,8,128]{2,1,0:T(8,128)(2,1)S(1)} async-done(((bf16[64,8,128]{2,1,0:T(8,128)(2,1)}), bf16[64,8,128]{2,1,0:T(8,128)(2,1)S(1)}, u32[]{:S(2)}, u32[]{:S(2)}) %all-to-all-start) | async-done | bytes 131104 | tf_op jit(solution)/shard_map/all_to_all | solution.py:14
  36.1 11.3 %all_to_all.35 = bf16[16,2,2,8,128]{4,3,1,2,0:T(8,128)(2,1)S(1)} all-to-all(bf16[16,2,2,8,128]{4,3,1,2,0:T(8,128)(2,1)S(1)} %broadcast_in_dim.9), channel_id=1, replica_groups=mesh['yh'=2,'z'=16,'c'=2,'x'=4,'yl'=4] {'x','yl'}, dimensions={0} | all-to-all | bytes 262144 | tf_op jit(solution)/shard_map/all_to_all | solution.py:14
  47.4 0.0 collective-permute-done.1
  47.4 0.3 fusion.3
  47.7 26.3 %all_to_all.36 = bf16[16,8,896]{2,1,0:T(8,128)(2,1)S(1)} all-to-all(bf16[16,8,896]{2,1,0:T(8,128)(2,1)S(1)} %fusion.3), channel_id=1, replica_groups=mesh['yh'=2,'z'=16,'c'=2,'x'=4,'yl'=4] {'z'}, dimensions={0} | all-to-all | bytes 458752 | tf_op jit(solution)/shard_map/all_to_all | solution.py:14
  74.0 0.0 copy-start.2
  74.0 0.0 copy-start.3
  74.1 0.7 copy-done.2
  74.8 0.0 copy-done.3
  74.8 0.6 fusion.24
  75.4 0.7 broadcast_in_dim.10
  76.2 5.4 %all-to-all-start.3 = ((bf16[16,8,896]{2,1,0:T(8,128)(2,1)}), bf16[16,8,896]{2,1,0:T(8,128)(2,1)S(1)}, u32[]{:S(2)}, u32[]{:S(2)}) async-start(bf16[16,8,896]{2,1,0:T(8,128)(2,1)} %broadcast_in_dim.10), calls=%async_computation.3 | async-start | bytes 458752 | tf_op jit(solution)/shard_map/all_to_all | solution.py:14
  81.6 0.0 copy-done
  81.6 3.6 %collective-permute-start.4 = (bf16[128,512]{1,0:T(8,128)(2,1)S(1)}, bf16[128,512]{1,0:T(8,128)(2,1)S(1)}, u32[]{:S(2)}, u32[]{:S(2)}) collective-permute-start(bf16[128,512]{1,0:T(8,128)(2,1)S(1)} %copy-done), channel_id=1, source_target_pairs={{0,512},{512,0},{1,513},{513,1},{2,514},{514,2},{3,515},{515,3},{4... | collective-permute-start | bytes 393224 | tf_op jit(solution)/shard_map/ppermute | solution.py:30
  85.2 1.9 %collective-permute-start.2 = (bf16[8,896]{1,0:T(8,128)(2,1)S(1)}, bf16[8,896]{1,0:T(8,128)(2,1)S(1)}, u32[]{:S(2)}, u32[]{:S(2)}) collective-permute-start(bf16[8,896]{1,0:T(8,128)(2,1)S(1)} %get-tuple-element.8), channel_id=1, source_target_pairs={{0,16},{16,0},{1,17},{17,1},{2,18},{18,2},{3,19},{19,3},{4,20},{20... | collective-permute-start | bytes 43016 | tf_op jit(solution)/shard_map/ppermute | solution.py:30
  87.1 0.8 dynamic-slice_bitcast_fusion
  87.9 0.4 collective-permute-done.2
  88.3 6.2 %collective-permute-start.3 = (bf16[2,8,896]{2,1,0:T(8,128)(2,1)S(1)}, bf16[2,8,896]{2,1,0:T(8,128)(2,1)S(1)}, u32[]{:S(2)}, u32[]{:S(2)}) collective-permute-start(bf16[2,8,896]{2,1,0:T(8,128)(2,1)S(1)} %get-tuple-element.7), channel_id=1, source_target_pairs={{0,512},{512,0},{1,513},{513,1},{2,514},{514,2},{3,515},{515,3},{4... | collective-permute-start | bytes 86024 | tf_op jit(solution)/shard_map/ppermute | solution.py:30
  94.5 0.1 pad_maximum_fusion
  94.6 3.7 %collective-permute-done.3 = bf16[2,8,896]{2,1,0:T(8,128)(2,1)S(1)} collective-permute-done((bf16[2,8,896]{2,1,0:T(8,128)(2,1)S(1)}, bf16[2,8,896]{2,1,0:T(8,128)(2,1)S(1)}, u32[]{:S(2)}, u32[]{:S(2)}) %collective-permute-start.3) | collective-permute-done | bytes 28704 | tf_op jit(solution)/shard_map/ppermute | solution.py:30
  98.3 0.3 all-to-all-done.3
  98.5 0.4 convolution_convert_fusion
  99.0 0.2 convolution_convert_fusion.1
  99.1 0.1 copy.13
  99.3 0.7 maximum_bitcast_fusion
  100.0 5.0 %all-to-all-start.4 = ((bf16[16,8,544]{2,1,0:T(8,128)(2,1)}), bf16[16,8,544]{2,1,0:T(8,128)(2,1)S(1)}, u32[]{:S(2)}, u32[]{:S(2)}) async-start(bf16[16,8,544]{2,1,0:T(8,128)(2,1)} %maximum_bitcast_fusion), calls=%async_computation.4 | async-start | bytes 327680 | tf_op jit(solution)/shard_map/all_to_all | solution.py:14
  105.0 0.0 collective-permute-done.4
  105.0 1.9 %collective-permute-start.5 = (bf16[2,128,512]{2,1,0:T(8,128)(2,1)S(1)}, bf16[2,128,512]{2,1,0:T(8,128)(2,1)S(1)}, u32[]{:S(2)}, u32[]{:S(2)}) collective-permute-start(bf16[2,128,512]{2,1,0:T(8,128)(2,1)S(1)} %get-tuple-element.5), channel_id=1, source_target_pairs={{0,16},{16,0},{1,17},{17,1},{2,18},{18,2},{3,19},{19,3},{4,20},{20... | collective-permute-start | bytes 786440 | tf_op jit(solution)/shard_map/ppermute | solution.py:30
  107.0 5.5 %all-to-all-done.4 = bf16[16,8,544]{2,1,0:T(8,128)(2,1)S(1)} async-done(((bf16[16,8,544]{2,1,0:T(8,128)(2,1)}), bf16[16,8,544]{2,1,0:T(8,128)(2,1)S(1)}, u32[]{:S(2)}, u32[]{:S(2)}) %all-to-all-start.4) | async-done | bytes 139296 | tf_op jit(solution)/shard_map/all_to_all | solution.py:14
  112.5 0.7 broadcast_in_dim.11
  113.2 4.4 %all-to-all-start.5 = ((bf16[16,8,544]{2,1,0:T(8,128)(2,1)}), bf16[16,8,544]{2,1,0:T(8,128)(2,1)S(1)}, u32[]{:S(2)}, u32[]{:S(2)}) async-start(bf16[16,8,544]{2,1,0:T(8,128)(2,1)} %broadcast_in_dim.11), calls=%async_computation.5 | async-start | bytes 327680 | tf_op jit(solution)/shard_map/all_to_all | solution.py:14
  117.6 0.0 collective-permute-done.5
  117.6 0.1 pad_maximum_fusion.1
  117.7 7.5 %all-to-all-done.5 = bf16[16,8,544]{2,1,0:T(8,128)(2,1)S(1)} async-done(((bf16[16,8,544]{2,1,0:T(8,128)(2,1)}), bf16[16,8,544]{2,1,0:T(8,128)(2,1)S(1)}, u32[]{:S(2)}, u32[]{:S(2)}) %all-to-all-start.5) | async-done | bytes 139296 | tf_op jit(solution)/shard_map/all_to_all | solution.py:14
  125.3 0.2 fusion.13
  125.4 0.9 fusion.7
  126.3 11.2 %all-to-all-start.6 = ((bf16[16,8,512]{2,1,0:T(8,128)(2,1)}), bf16[16,8,512]{2,1,0:T(8,128)(2,1)S(1)}, u32[]{:S(2)}, u32[]{:S(2)}) async-start(bf16[16,8,512]{2,1,0:T(8,128)(2,1)} %fusion.7), calls=%async_computation.6 | async-start | bytes 262144 | tf_op jit(solution)/shard_map/all_to_all | solution.py:14
  137.5 0.7 dynamic-slice_convert_fusion
  138.2 12.4 %all-to-all-done.6 = bf16[16,8,512]{2,1,0:T(8,128)(2,1)S(1)} async-done(((bf16[16,8,512]{2,1,0:T(8,128)(2,1)}), bf16[16,8,512]{2,1,0:T(8,128)(2,1)S(1)}, u32[]{:S(2)}, u32[]{:S(2)}) %all-to-all-start.6) | async-done | bytes 131104 | tf_op jit(solution)/shard_map/all_to_all | solution.py:14
  150.6 0.6 add.36
  (14 shorter events, 0.2 us)
Async XLA Ops:
  0.6 24.9 %collective-permute-start = (bf16[128,896]{1,0:T(8,128)(2,1)}, bf16[128,896]{1,0:T(8,128)(2,1)S(1)}, u32[]{:S(2)}, u32[]{:S(2)}) collective-permute-start(bf16[128,896]{1,0:T(8,128)(2,1)} %param.6), channel_id=1, source_target_pairs={{0,512},{512,0},{1,513},{513,1},{2,514},{514,2},{3,515},{515,3},{4... | collective-permute-start | bytes 688136 | tf_op jit(solution)/shard_map/ppermute | solution.py:30
  9.5 16.1 %copy-start.1 = (bf16[128,896]{1,0:T(8,128)(2,1)S(1)}, bf16[128,896]{1,0:T(8,128)(2,1)}, u32[]{:S(2)}) copy-start(bf16[128,896]{1,0:T(8,128)(2,1)} %param.6) | copy-start | bytes 688132
  9.5 26.5 %all-to-all-start = ((bf16[64,8,128]{2,1,0:T(8,128)(2,1)}), bf16[64,8,128]{2,1,0:T(8,128)(2,1)S(1)}, u32[]{:S(2)}, u32[]{:S(2)}) async-start(bf16[64,8,128]{2,1,0:T(8,128)(2,1)} %fusion.6), calls=%async_computation | async-start | bytes 262144 | tf_op jit(solution)/shard_map/all_to_all | solution.py:14
  25.6 21.7 %collective-permute-start.1 = (bf16[2,128,896]{2,1,0:T(8,128)(2,1)S(1)}, bf16[2,128,896]{2,1,0:T(8,128)(2,1)S(1)}, u32[]{:S(2)}, u32[]{:S(2)}) collective-permute-start(bf16[2,128,896]{2,1,0:T(8,128)(2,1)S(1)} %get-tuple-element.3), channel_id=1, source_target_pairs={{0,16},{16,0},{1,17},{17,1},{2,18},{18,2},{3,19},{19,3},{4,20},{20... | collective-permute-start | bytes 1376264 | tf_op jit(solution)/shard_map/ppermute | solution.py:30
  74.0 0.7 copy-start.2
  74.0 0.8 copy-start.3
  76.2 5.4 %copy-start = (bf16[128,512]{1,0:T(8,128)(2,1)S(1)}, bf16[128,512]{1,0:T(8,128)(2,1)}, u32[]{:S(2)}) copy-start(bf16[128,512]{1,0:T(8,128)(2,1)} %param.5) | copy-start | bytes 393220
  76.2 22.4 %all-to-all-start.3 = ((bf16[16,8,896]{2,1,0:T(8,128)(2,1)}), bf16[16,8,896]{2,1,0:T(8,128)(2,1)S(1)}, u32[]{:S(2)}, u32[]{:S(2)}) async-start(bf16[16,8,896]{2,1,0:T(8,128)(2,1)} %broadcast_in_dim.10), calls=%async_computation.3 | async-start | bytes 458752 | tf_op jit(solution)/shard_map/all_to_all | solution.py:14
  81.6 23.4 %collective-permute-start.4 = (bf16[128,512]{1,0:T(8,128)(2,1)S(1)}, bf16[128,512]{1,0:T(8,128)(2,1)S(1)}, u32[]{:S(2)}, u32[]{:S(2)}) collective-permute-start(bf16[128,512]{1,0:T(8,128)(2,1)S(1)} %copy-done), channel_id=1, source_target_pairs={{0,512},{512,0},{1,513},{513,1},{2,514},{514,2},{3,515},{515,3},{4... | collective-permute-start | bytes 393224 | tf_op jit(solution)/shard_map/ppermute | solution.py:30
  85.2 3.1 %collective-permute-start.2 = (bf16[8,896]{1,0:T(8,128)(2,1)S(1)}, bf16[8,896]{1,0:T(8,128)(2,1)S(1)}, u32[]{:S(2)}, u32[]{:S(2)}) collective-permute-start(bf16[8,896]{1,0:T(8,128)(2,1)S(1)} %get-tuple-element.8), channel_id=1, source_target_pairs={{0,16},{16,0},{1,17},{17,1},{2,18},{18,2},{3,19},{19,3},{4,20},{20... | collective-permute-start | bytes 43016 | tf_op jit(solution)/shard_map/ppermute | solution.py:30
  88.3 10.0 %collective-permute-start.3 = (bf16[2,8,896]{2,1,0:T(8,128)(2,1)S(1)}, bf16[2,8,896]{2,1,0:T(8,128)(2,1)S(1)}, u32[]{:S(2)}, u32[]{:S(2)}) collective-permute-start(bf16[2,8,896]{2,1,0:T(8,128)(2,1)S(1)} %get-tuple-element.7), channel_id=1, source_target_pairs={{0,512},{512,0},{1,513},{513,1},{2,514},{514,2},{3,515},{515,3},{4... | collective-permute-start | bytes 86024 | tf_op jit(solution)/shard_map/ppermute | solution.py:30
  100.0 12.5 %all-to-all-start.4 = ((bf16[16,8,544]{2,1,0:T(8,128)(2,1)}), bf16[16,8,544]{2,1,0:T(8,128)(2,1)S(1)}, u32[]{:S(2)}, u32[]{:S(2)}) async-start(bf16[16,8,544]{2,1,0:T(8,128)(2,1)} %maximum_bitcast_fusion), calls=%async_computation.4 | async-start | bytes 327680 | tf_op jit(solution)/shard_map/all_to_all | solution.py:14
  105.0 12.6 %collective-permute-start.5 = (bf16[2,128,512]{2,1,0:T(8,128)(2,1)S(1)}, bf16[2,128,512]{2,1,0:T(8,128)(2,1)S(1)}, u32[]{:S(2)}, u32[]{:S(2)}) collective-permute-start(bf16[2,128,512]{2,1,0:T(8,128)(2,1)S(1)} %get-tuple-element.5), channel_id=1, source_target_pairs={{0,16},{16,0},{1,17},{17,1},{2,18},{18,2},{3,19},{19,3},{4,20},{20... | collective-permute-start | bytes 786440 | tf_op jit(solution)/shard_map/ppermute | solution.py:30
  113.2 12.0 %all-to-all-start.5 = ((bf16[16,8,544]{2,1,0:T(8,128)(2,1)}), bf16[16,8,544]{2,1,0:T(8,128)(2,1)S(1)}, u32[]{:S(2)}, u32[]{:S(2)}) async-start(bf16[16,8,544]{2,1,0:T(8,128)(2,1)} %broadcast_in_dim.11), calls=%async_computation.5 | async-start | bytes 327680 | tf_op jit(solution)/shard_map/all_to_all | solution.py:14
  126.3 24.3 %all-to-all-start.6 = ((bf16[16,8,512]{2,1,0:T(8,128)(2,1)}), bf16[16,8,512]{2,1,0:T(8,128)(2,1)S(1)}, u32[]{:S(2)}, u32[]{:S(2)}) async-start(bf16[16,8,512]{2,1,0:T(8,128)(2,1)} %fusion.7), calls=%async_computation.6 | async-start | bytes 262144 | tf_op jit(solution)/shard_map/all_to_all | solution.py:14

commit v4 on v3

--- a/solution.py
+++ b/solution.py
@@ -26,13 +26,10 @@
     return lax.dot_general(left, right, (dims, ((), ())), preferred_element_type=jnp.float32)
 
 
-def pair(x, axis):
-    return jnp.stack([x, lax.ppermute(x, axis, [(0, 1), (1, 0)])])
-
-
 def near(x, axes):
     for axis in axes:
-        x = pair(x, axis)
+        other = lax.ppermute(x, axis, [(0, 1), (1, 0)])
+        x = lax.optimization_barrier(jnp.stack([x, other]))
     return x
 
 
@@ -46,7 +43,7 @@
     bf16 = jnp.bfloat16
     root = jnp.sqrt(jnp.float32(D))
     grad_all = near(grad_out, ("yh", "c"))
-    acts_all = near(acts, ("yh", "c"))
+    acts_all = near(acts, ("c", "yh")).swapaxes(0, 1)
     rows = proj_t.reshape(2, 16, 2, OWN, -1)
     rows = lax.dynamic_index_in_dim(rows, lax.axis_index("z"), 1, keepdims=False)
     rows = from_own(rows, ("yh", "c")).reshape(4 * OWN, -1)
@@ -60,10 +57,12 @@
     coords = coords.transpose(2, 1, 0, 3, 4).reshape(2, 2, 128, 128)
     grad_part = (dot(coords, grad_all, ((0, 1, 3), (0, 1, 2))) / TOKENS).astype(bf16)
     grad_own = total(swap(grad_part.reshape(16, OWN, -1), "z"))
+    low_own = grad_own.astype(bf16)
+    low_own, grad_own = lax.optimization_barrier((low_own, grad_own))
     moment_one = 0.9 * first_moment + 0.1 * grad_own
     moment_two = 0.999 * second_moment + 0.001 * grad_own * grad_own
-    adam_step = moment_one / (1.0 - 0.9**10) / (jnp.sqrt(moment_two / (1.0 - 0.999**10)) + 1e-08)
-    low_own = grad_own.astype(bf16)
+    root_two = jnp.sqrt(moment_two / (1.0 - 0.999**10)) + 1e-08
+    adam_step = moment_one / (1.0 - 0.9**10) / root_two
     low = to_all(low_own, "z", 16).reshape(128, -1)
     low_rows = near(low_own, ("c", "yh")).reshape(4 * OWN, -1)
     back = dot(low, grad_all.reshape(512, -1), ((1,), (1,))).astype(bf16)

time: 152 us -> 159 us (1.046)
  waiting for transfers between devices: 38.1 us -> 56.3 us
  blocking collectives: 37.6 us -> 26.3 us
    all_to_all x5 -> x6, waiting for transfers between devices: 34 us -> 51.2 us  [swap(): return lax.all_to_all(pieces, axes, split_axis=0, concat_axis=0, tiled=True)]
    all_to_all x2 -> x1, blocking collectives: 37.6 us -> 26.3 us  [swap(): return lax.all_to_all(pieces, axes, split_axis=0, concat_axis=0, tiled=True)]
    ppermute x6, starting transfers between devices: 22.5 us -> 20.8 us  [near(): other = lax.ppermute(x, axis, [(0, 1), (1, 0)])]
    all_to_all x5 -> x6, starting transfers between devices: 42 us -> 43.2 us  [swap(): return lax.all_to_all(pieces, axes, split_axis=0, concat_axis=0, tiled=True)]
  transfers between devices with their start and end apart: 11 -> 12, of which waited for: 7 -> 7; matrix products, arithmetic and copies ran while one was open for 4% -> 5% of each run, Pallas kernels for 0% -> 0%
where the time goes in v4:
time: 159 us; the launch traced here: 158 us
  starting transfers between devices  64 us (40%)
  waiting for transfers between devices  56.3 us (35%)
  blocking collectives  26.3 us (17%)
  matrix products  3.93 us (2%)
  other arithmetic  3.04 us (2%)
  local copies, waits for them, and re-layouts  3 us (2%)
    all_to_all x6, waiting for transfers between devices, swap(): return lax.all_to_all(pieces, axes, split_axis=0, concat_axis=0, tiled=True)  51.2 us
    all_to_all x6, starting transfers between devices, swap(): return lax.all_to_all(pieces, axes, split_axis=0, concat_axis=0, tiled=True)  43.2 us
    all_to_all x1, blocking collectives, swap(): return lax.all_to_all(pieces, axes, split_axis=0, concat_axis=0, tiled=True)  26.3 us
    ppermute x6, starting transfers between devices, near(): other = lax.ppermute(x, axis, [(0, 1), (1, 0)])  20.8 us
    ppermute x6, waiting for transfers between devices, near(): other = lax.ppermute(x, axis, [(0, 1), (1, 0)])  5.15 us
    dot_general x6, matrix products, dot(): lax.dot_general(left, right, (dims, ((), ())), preferred_element_type=jnp...  3.93 us
  transfers between devices with their start and end apart: 12, of which 7 were waited for; matrix products, arithmetic and copies ran while one was open for 5% of the time, Pallas kernels for 0%

profile of v4, /device:TPU:8, one launch (start us, length us, event | category | flops | bytes accessed | tf_op | source)
XLA Modules:
  0.0 157.6 jit_solution(17541856164671742804)
XLA Ops:
  0.6 6.8 %collective-permute-start = (bf16[128,896]{1,0:T(8,128)(2,1)}, bf16[128,896]{1,0:T(8,128)(2,1)S(1)}, u32[]{:S(2)}, u32[]{:S(2)}) collective-permute-start(bf16[128,896]{1,0:T(8,128)(2,1)} %param.6), channel_id=1, source_target_pairs={{0,512},{512,0},{1,513},{513,1},{2,514},{514,2},{3,515},{515,3},{4... | collective-permute-start | bytes 688136 | tf_op jit(solution)/shard_map/ppermute | solution.py:31
  7.5 2.0 %fusion.6 = bf16[64,8,128]{2,1,0:T(8,128)(2,1)} fusion(bf16[512,512]{1,0:T(8,128)(2,1)} %param.7, bf16[128,512]{1,0:T(8,128)(2,1)} %param.5), kind=kOutput, calls=%fused_computation.10 | convolution fusion | flops 67239936 | bytes 786432 | tf_op jit(solution)/shard_map/dot_general | solution.py:26
  9.5 16.0 %all-to-all-start = ((bf16[64,8,128]{2,1,0:T(8,128)(2,1)}), bf16[64,8,128]{2,1,0:T(8,128)(2,1)S(1)}, u32[]{:S(2)}, u32[]{:S(2)}) async-start(bf16[64,8,128]{2,1,0:T(8,128)(2,1)} %fusion.6), calls=%async_computation | async-start | bytes 262144 | tf_op jit(solution)/shard_map/all_to_all | solution.py:14
  25.5 0.0 collective-permute-done
  25.5 0.0 copy-done.1
  25.6 0.1 pad_maximum_fusion.2
  25.6 2.0 %collective-permute-start.1 = (bf16[2,128,896]{2,1,0:T(8,128)(2,1)S(1)}, bf16[2,128,896]{2,1,0:T(8,128)(2,1)S(1)}, u32[]{:S(2)}, u32[]{:S(2)}) collective-permute-start(bf16[2,128,896]{2,1,0:T(8,128)(2,1)S(1)} %pad_maximum_fusion.2), channel_id=1, source_target_pairs={{0,16},{16,0},{1,17},{17,1},{2,18},{18,2},{3,19},{19,3},{4,20},{20... | collective-permute-start | bytes 1376264 | tf_op jit(solution)/shard_map/ppermute | solution.py:31
  27.6 8.3 %all-to-all-done = bf16[64,8,128]{2,1,0:T(8,128)(2,1)S(1)} async-done(((bf16[64,8,128]{2,1,0:T(8,128)(2,1)}), bf16[64,8,128]{2,1,0:T(8,128)(2,1)S(1)}, u32[]{:S(2)}, u32[]{:S(2)}) %all-to-all-start) | async-done | bytes 131104 | tf_op jit(solution)/shard_map/all_to_all | solution.py:14
  36.0 0.7 broadcast_in_dim.9
  36.7 4.6 %all-to-all-start.1 = ((bf16[16,2,2,8,128]{4,3,1,2,0:T(8,128)(2,1)}), bf16[16,2,2,8,128]{4,3,1,2,0:T(8,128)(2,1)S(1)}, u32[]{:S(2)}, u32[]{:S(2)}) async-start(bf16[16,2,2,8,128]{4,3,1,2,0:T(8,128)(2,1)} %broadcast_in_dim.9), calls=%async_computation.1 | async-start | bytes 262144 | tf_op jit(solution)/shard_map/all_to_all | solution.py:14
  41.3 0.0 collective-permute-done.1
  41.4 0.1 pad_maximum_fusion
  41.5 7.4 %all-to-all-done.1 = bf16[16,2,2,8,128]{4,3,1,2,0:T(8,128)(2,1)S(1)} async-done(((bf16[16,2,2,8,128]{4,3,1,2,0:T(8,128)(2,1)}), bf16[16,2,2,8,128]{4,3,1,2,0:T(8,128)(2,1)S(1)}, u32[]{:S(2)}, u32[]{:S(2)}) %all-to-all-start.1) | async-done | bytes 131104 | tf_op jit(solution)/shard_map/all_to_all | solution.py:14
  48.9 0.3 fusion.3
  49.2 26.3 %all_to_all.35 = bf16[16,8,896]{2,1,0:T(8,128)(2,1)S(1)} all-to-all(bf16[16,8,896]{2,1,0:T(8,128)(2,1)S(1)} %fusion.3), channel_id=1, replica_groups=mesh['yh'=2,'z'=16,'c'=2,'x'=4,'yl'=4] {'z'}, dimensions={0} | all-to-all | bytes 458752 | tf_op jit(solution)/shard_map/all_to_all | solution.py:14
  75.6 0.7 broadcast_in_dim.10
  76.3 5.4 %all-to-all-start.3 = ((bf16[16,8,896]{2,1,0:T(8,128)(2,1)}), bf16[16,8,896]{2,1,0:T(8,128)(2,1)S(1)}, u32[]{:S(2)}, u32[]{:S(2)}) async-start(bf16[16,8,896]{2,1,0:T(8,128)(2,1)} %broadcast_in_dim.10), calls=%async_computation.3 | async-start | bytes 458752 | tf_op jit(solution)/shard_map/all_to_all | solution.py:14
  81.7 1.9 %collective-permute-start.2 = (bf16[8,896]{1,0:T(8,128)(2,1)S(1)}, bf16[8,896]{1,0:T(8,128)(2,1)S(1)}, u32[]{:S(2)}, u32[]{:S(2)}) collective-permute-start(bf16[8,896]{1,0:T(8,128)(2,1)S(1)} %convert_element_type.44), channel_id=1, source_target_pairs={{0,16},{16,0},{1,17},{17,1},{2,18},{18,2},{3,19},{19,3},{4,20},{20... | collective-permute-start | bytes 43016 | tf_op jit(solution)/shard_map/ppermute | solution.py:31
  83.6 0.0 copy-done
  83.6 2.4 %collective-permute-start.4 = (bf16[128,512]{1,0:T(8,128)(2,1)S(1)}, bf16[128,512]{1,0:T(8,128)(2,1)S(1)}, u32[]{:S(2)}, u32[]{:S(2)}) collective-permute-start(bf16[128,512]{1,0:T(8,128)(2,1)S(1)} %copy-done), channel_id=1, source_target_pairs={{0,16},{16,0},{1,17},{17,1},{2,18},{18,2},{3,19},{19,3},{4,20},{20... | collective-permute-start | bytes 393224 | tf_op jit(solution)/shard_map/ppermute | solution.py:31
  86.1 0.0 collective-permute-done.2
  86.1 3.8 %collective-permute-start.3 = (bf16[2,8,896]{2,1,0:T(8,128)(2,1)S(1)}, bf16[2,8,896]{2,1,0:T(8,128)(2,1)S(1)}, u32[]{:S(2)}, u32[]{:S(2)}) collective-permute-start(bf16[2,8,896]{2,1,0:T(8,128)(2,1)S(1)} %pad_maximum_fusion.5), channel_id=1, source_target_pairs={{0,512},{512,0},{1,513},{513,1},{2,514},{514,2},{3,515},{515,3},{4... | collective-permute-start | bytes 86024 | tf_op jit(solution)/shard_map/ppermute | solution.py:31
  89.9 0.8 dynamic-slice_bitcast_fusion
  90.6 5.1 %collective-permute-done.3 = bf16[2,8,896]{2,1,0:T(8,128)(2,1)S(1)} collective-permute-done((bf16[2,8,896]{2,1,0:T(8,128)(2,1)S(1)}, bf16[2,8,896]{2,1,0:T(8,128)(2,1)S(1)}, u32[]{:S(2)}, u32[]{:S(2)}) %collective-permute-start.3) | collective-permute-done | bytes 28704 | tf_op jit(solution)/shard_map/ppermute | solution.py:31
  95.8 2.9 %all-to-all-done.3 = bf16[16,8,896]{2,1,0:T(8,128)(2,1)S(1)} async-done(((bf16[16,8,896]{2,1,0:T(8,128)(2,1)}), bf16[16,8,896]{2,1,0:T(8,128)(2,1)S(1)}, u32[]{:S(2)}, u32[]{:S(2)}) %all-to-all-start.3) | async-done | bytes 229408 | tf_op jit(solution)/shard_map/all_to_all | solution.py:14
  98.7 0.4 convolution_convert_fusion
  99.1 0.2 convolution_convert_fusion.1
  99.3 0.1 copy.16
  99.4 0.7 maximum_bitcast_fusion
  100.1 5.0 %all-to-all-start.4 = ((bf16[16,8,544]{2,1,0:T(8,128)(2,1)}), bf16[16,8,544]{2,1,0:T(8,128)(2,1)S(1)}, u32[]{:S(2)}, u32[]{:S(2)}) async-start(bf16[16,8,544]{2,1,0:T(8,128)(2,1)} %maximum_bitcast_fusion), calls=%async_computation.4 | async-start | bytes 327680 | tf_op jit(solution)/shard_map/all_to_all | solution.py:14
  105.1 0.0 collective-permute-done.4
  105.1 3.9 %collective-permute-start.5 = (bf16[2,128,512]{2,1,0:T(8,128)(2,1)S(1)}, bf16[2,128,512]{2,1,0:T(8,128)(2,1)S(1)}, u32[]{:S(2)}, u32[]{:S(2)}) collective-permute-start(bf16[2,128,512]{2,1,0:T(8,128)(2,1)S(1)} %pad_maximum_fusion.3), channel_id=1, source_target_pairs={{0,512},{512,0},{1,513},{513,1},{2,514},{514,2},{3,515},{515,3},{4... | collective-permute-start | bytes 786440 | tf_op jit(solution)/shard_map/ppermute | solution.py:31
  109.0 13.3 %all-to-all-done.4 = bf16[16,8,544]{2,1,0:T(8,128)(2,1)S(1)} async-done(((bf16[16,8,544]{2,1,0:T(8,128)(2,1)}), bf16[16,8,544]{2,1,0:T(8,128)(2,1)S(1)}, u32[]{:S(2)}, u32[]{:S(2)}) %all-to-all-start.4) | async-done | bytes 139296 | tf_op jit(solution)/shard_map/all_to_all | solution.py:14
  122.3 0.7 broadcast_in_dim.11
  123.0 6.4 %all-to-all-start.5 = ((bf16[16,8,544]{2,1,0:T(8,128)(2,1)}), bf16[16,8,544]{2,1,0:T(8,128)(2,1)S(1)}, u32[]{:S(2)}, u32[]{:S(2)}) async-start(bf16[16,8,544]{2,1,0:T(8,128)(2,1)} %broadcast_in_dim.11), calls=%async_computation.5 | async-start | bytes 327680 | tf_op jit(solution)/shard_map/all_to_all | solution.py:14
  129.4 0.0 collective-permute-done.5
  129.4 0.1 pad_maximum_fusion.1
  129.5 7.5 %all-to-all-done.5 = bf16[16,8,544]{2,1,0:T(8,128)(2,1)S(1)} async-done(((bf16[16,8,544]{2,1,0:T(8,128)(2,1)}), bf16[16,8,544]{2,1,0:T(8,128)(2,1)S(1)}, u32[]{:S(2)}, u32[]{:S(2)}) %all-to-all-start.5) | async-done | bytes 139296 | tf_op jit(solution)/shard_map/all_to_all | solution.py:14
  137.0 0.1 fusion.13
  137.2 0.9 fusion.7
  138.1 5.7 %all-to-all-start.6 = ((bf16[16,8,512]{2,1,0:T(8,128)(2,1)}), bf16[16,8,512]{2,1,0:T(8,128)(2,1)S(1)}, u32[]{:S(2)}, u32[]{:S(2)}) async-start(bf16[16,8,512]{2,1,0:T(8,128)(2,1)} %fusion.7), calls=%async_computation.6 | async-start | bytes 262144 | tf_op jit(solution)/shard_map/all_to_all | solution.py:14
  143.8 0.0 copy-start.2
  143.8 0.7 dynamic-slice_convert_fusion
  144.5 0.0 copy-done.3
  144.5 0.0 copy-done.2
  144.6 0.6 fusion.19
  145.2 11.7 %all-to-all-done.6 = bf16[16,8,512]{2,1,0:T(8,128)(2,1)S(1)} async-done(((bf16[16,8,512]{2,1,0:T(8,128)(2,1)}), bf16[16,8,512]{2,1,0:T(8,128)(2,1)S(1)}, u32[]{:S(2)}, u32[]{:S(2)}) %all-to-all-start.6) | async-done | bytes 131104 | tf_op jit(solution)/shard_map/all_to_all | solution.py:14
  156.9 0.6 add.36
  (16 shorter events, 0.2 us)
Async XLA Ops:
  0.6 24.9 %collective-permute-start = (bf16[128,896]{1,0:T(8,128)(2,1)}, bf16[128,896]{1,0:T(8,128)(2,1)S(1)}, u32[]{:S(2)}, u32[]{:S(2)}) collective-permute-start(bf16[128,896]{1,0:T(8,128)(2,1)} %param.6), channel_id=1, source_target_pairs={{0,512},{512,0},{1,513},{513,1},{2,514},{514,2},{3,515},{515,3},{4... | collective-permute-start | bytes 688136 | tf_op jit(solution)/shard_map/ppermute | solution.py:31
  9.5 16.1 %copy-start.1 = (bf16[128,896]{1,0:T(8,128)(2,1)S(1)}, bf16[128,896]{1,0:T(8,128)(2,1)}, u32[]{:S(2)}) copy-start(bf16[128,896]{1,0:T(8,128)(2,1)} %param.6) | copy-start | bytes 688132
  9.5 26.5 %all-to-all-start = ((bf16[64,8,128]{2,1,0:T(8,128)(2,1)}), bf16[64,8,128]{2,1,0:T(8,128)(2,1)S(1)}, u32[]{:S(2)}, u32[]{:S(2)}) async-start(bf16[64,8,128]{2,1,0:T(8,128)(2,1)} %fusion.6), calls=%async_computation | async-start | bytes 262144 | tf_op jit(solution)/shard_map/all_to_all | solution.py:14
  25.6 15.7 %collective-permute-start.1 = (bf16[2,128,896]{2,1,0:T(8,128)(2,1)S(1)}, bf16[2,128,896]{2,1,0:T(8,128)(2,1)S(1)}, u32[]{:S(2)}, u32[]{:S(2)}) collective-permute-start(bf16[2,128,896]{2,1,0:T(8,128)(2,1)S(1)} %pad_maximum_fusion.2), channel_id=1, source_target_pairs={{0,16},{16,0},{1,17},{17,1},{2,18},{18,2},{3,19},{19,3},{4,20},{20... | collective-permute-start | bytes 1376264 | tf_op jit(solution)/shard_map/ppermute | solution.py:31
  36.7 12.2 %all-to-all-start.1 = ((bf16[16,2,2,8,128]{4,3,1,2,0:T(8,128)(2,1)}), bf16[16,2,2,8,128]{4,3,1,2,0:T(8,128)(2,1)S(1)}, u32[]{:S(2)}, u32[]{:S(2)}) async-start(bf16[16,2,2,8,128]{4,3,1,2,0:T(8,128)(2,1)} %broadcast_in_dim.9), calls=%async_computation.1 | async-start | bytes 262144 | tf_op jit(solution)/shard_map/all_to_all | solution.py:14
  76.3 7.4 %copy-start = (bf16[128,512]{1,0:T(8,128)(2,1)S(1)}, bf16[128,512]{1,0:T(8,128)(2,1)}, u32[]{:S(2)}) copy-start(bf16[128,512]{1,0:T(8,128)(2,1)} %param.5) | copy-start | bytes 393220
  76.3 22.4 %all-to-all-start.3 = ((bf16[16,8,896]{2,1,0:T(8,128)(2,1)}), bf16[16,8,896]{2,1,0:T(8,128)(2,1)S(1)}, u32[]{:S(2)}, u32[]{:S(2)}) async-start(bf16[16,8,896]{2,1,0:T(8,128)(2,1)} %broadcast_in_dim.10), calls=%async_computation.3 | async-start | bytes 458752 | tf_op jit(solution)/shard_map/all_to_all | solution.py:14
  81.7 4.4 %collective-permute-start.2 = (bf16[8,896]{1,0:T(8,128)(2,1)S(1)}, bf16[8,896]{1,0:T(8,128)(2,1)S(1)}, u32[]{:S(2)}, u32[]{:S(2)}) collective-permute-start(bf16[8,896]{1,0:T(8,128)(2,1)S(1)} %convert_element_type.44), channel_id=1, source_target_pairs={{0,16},{16,0},{1,17},{17,1},{2,18},{18,2},{3,19},{19,3},{4,20},{20... | collective-permute-start | bytes 43016 | tf_op jit(solution)/shard_map/ppermute | solution.py:31
  83.6 21.4 %collective-permute-start.4 = (bf16[128,512]{1,0:T(8,128)(2,1)S(1)}, bf16[128,512]{1,0:T(8,128)(2,1)S(1)}, u32[]{:S(2)}, u32[]{:S(2)}) collective-permute-start(bf16[128,512]{1,0:T(8,128)(2,1)S(1)} %copy-done), channel_id=1, source_target_pairs={{0,16},{16,0},{1,17},{17,1},{2,18},{18,2},{3,19},{19,3},{4,20},{20... | collective-permute-start | bytes 393224 | tf_op jit(solution)/shard_map/ppermute | solution.py:31
  86.1 9.7 %collective-permute-start.3 = (bf16[2,8,896]{2,1,0:T(8,128)(2,1)S(1)}, bf16[2,8,896]{2,1,0:T(8,128)(2,1)S(1)}, u32[]{:S(2)}, u32[]{:S(2)}) collective-permute-start(bf16[2,8,896]{2,1,0:T(8,128)(2,1)S(1)} %pad_maximum_fusion.5), channel_id=1, source_target_pairs={{0,512},{512,0},{1,513},{513,1},{2,514},{514,2},{3,515},{515,3},{4... | collective-permute-start | bytes 86024 | tf_op jit(solution)/shard_map/ppermute | solution.py:31
  100.1 22.2 %all-to-all-start.4 = ((bf16[16,8,544]{2,1,0:T(8,128)(2,1)}), bf16[16,8,544]{2,1,0:T(8,128)(2,1)S(1)}, u32[]{:S(2)}, u32[]{:S(2)}) async-start(bf16[16,8,544]{2,1,0:T(8,128)(2,1)} %maximum_bitcast_fusion), calls=%async_computation.4 | async-start | bytes 327680 | tf_op jit(solution)/shard_map/all_to_all | solution.py:14
  105.1 24.3 %collective-permute-start.5 = (bf16[2,128,512]{2,1,0:T(8,128)(2,1)S(1)}, bf16[2,128,512]{2,1,0:T(8,128)(2,1)S(1)}, u32[]{:S(2)}, u32[]{:S(2)}) collective-permute-start(bf16[2,128,512]{2,1,0:T(8,128)(2,1)S(1)} %pad_maximum_fusion.3), channel_id=1, source_target_pairs={{0,512},{512,0},{1,513},{513,1},{2,514},{514,2},{3,515},{515,3},{4... | collective-permute-start | bytes 786440 | tf_op jit(solution)/shard_map/ppermute | solution.py:31
  123.0 14.0 %all-to-all-start.5 = ((bf16[16,8,544]{2,1,0:T(8,128)(2,1)}), bf16[16,8,544]{2,1,0:T(8,128)(2,1)S(1)}, u32[]{:S(2)}, u32[]{:S(2)}) async-start(bf16[16,8,544]{2,1,0:T(8,128)(2,1)} %broadcast_in_dim.11), calls=%async_computation.5 | async-start | bytes 327680 | tf_op jit(solution)/shard_map/all_to_all | solution.py:14
  138.1 6.5 %copy-start.3 = (f32[8,896]{1,0:T(8,128)S(1)}, f32[8,896]{1,0:T(8,128)}, u32[]{:S(2)}) copy-start(f32[8,896]{1,0:T(8,128)} %param.8) | copy-start | bytes 86020
  138.1 18.8 %all-to-all-start.6 = ((bf16[16,8,512]{2,1,0:T(8,128)(2,1)}), bf16[16,8,512]{2,1,0:T(8,128)(2,1)S(1)}, u32[]{:S(2)}, u32[]{:S(2)}) async-start(bf16[16,8,512]{2,1,0:T(8,128)(2,1)} %fusion.7), calls=%async_computation.6 | async-start | bytes 262144 | tf_op jit(solution)/shard_map/all_to_all | solution.py:14
  143.8 0.8 copy-start.2

commit v5 on v4

--- a/solution.py
+++ b/solution.py
@@ -43,12 +43,13 @@
     bf16 = jnp.bfloat16
     root = jnp.sqrt(jnp.float32(D))
     grad_all = near(grad_out, ("yh", "c"))
-    acts_all = near(acts, ("c", "yh")).swapaxes(0, 1)
+    acts_here = near(acts, ("c",))
+    acts_there = lax.ppermute(acts_here, "yh", [(0, 1), (1, 0)])
     rows = proj_t.reshape(2, 16, 2, OWN, -1)
     rows = lax.dynamic_index_in_dim(rows, lax.axis_index("z"), 1, keepdims=False)
     rows = from_own(rows, ("yh", "c")).reshape(4 * OWN, -1)
     own_rows = lax.dynamic_slice_in_dim(proj_t, lax.axis_index(DP) * OWN, OWN, 0)
-    own_rows = lax.optimization_barrier(own_rows.astype(jnp.float32))
+    own_rows = own_rows.astype(jnp.float32)
     part = (dot(proj_t, acts, ((1,), (1,))) * (1.0 / root)).astype(bf16)
     got = swap(part.reshape(64, OWN, 128), ("yh", "x", "yl", "c"))
     part = jnp.sum(got.reshape(2, 16, 2, OWN, 128).astype(jnp.float32), axis=1)
@@ -65,12 +66,17 @@
     adam_step = moment_one / (1.0 - 0.9**10) / root_two
     low = to_all(low_own, "z", 16).reshape(128, -1)
     low_rows = near(low_own, ("c", "yh")).reshape(4 * OWN, -1)
+    low, low_rows, own_rows, adam_step = lax.optimization_barrier(
+        (low, low_rows, own_rows, adam_step)
+    )
     back = dot(low, grad_all.reshape(512, -1), ((1,), (1,))).astype(bf16)
     cross = dot(low, low_rows, ((1,), (1,))).astype(bf16)
     both = jnp.concatenate([back, cross], axis=1)
     both = total(swap(both.reshape(16, OWN, 544), TENSOR)).astype(bf16)
     both = to_all(both, TENSOR, 16).reshape(128, 544)
-    pull = dot(both[:, :512], acts_all.reshape(512, -1), ((1,), (0,))) * (root / TOKENS)
+    back = both[:, :512].reshape(128, 2, 2, 128)
+    pull = dot(back[:, :, 0], acts_here, ((1, 2), (0, 1)))
+    pull = (pull + dot(back[:, :, 1], acts_there, ((1, 2), (0, 1)))) * (root / TOKENS)
     correction = dot(both[:, 512:], rows, ((1,), (0,)))
     moved = total(swap((pull - correction).astype(bf16).reshape(16, OWN, -1), "z"))
     return (adam_step, own_rows + moved)

time: 159 us -> 157 us (0.987)
  blocking collectives: 26.3 us -> 48.7 us
  waiting for transfers between devices: 56.3 us -> 37.9 us
  starting transfers between devices: 64 us -> 58.7 us
    all_to_all x1 -> x2, blocking collectives: 26.3 us -> 48.7 us  [swap(): return lax.all_to_all(pieces, axes, split_axis=0, concat_axis=0, tiled=True)]
    all_to_all x6 -> x5, waiting for transfers between devices: 51.2 us -> 31.6 us  [swap(): return lax.all_to_all(pieces, axes, split_axis=0, concat_axis=0, tiled=True)]
    all_to_all x6 -> x5, starting transfers between devices: 43.2 us -> 38.2 us  [swap(): return lax.all_to_all(pieces, axes, split_axis=0, concat_axis=0, tiled=True)]
    ppermute x6 -> x5, starting transfers between devices: 20.8 us -> 16.6 us  [near(): other = lax.ppermute(x, axis, [(0, 1), (1, 0)])]
    ppermute x0 -> x1, starting transfers between devices: none -> 3.86 us  [step(): acts_there = lax.ppermute(acts_here, 'yh', [(0, 1), (1, 0)])]
    ppermute x6 -> x5, waiting for transfers between devices: 5.15 us -> 6.24 us  [near(): other = lax.ppermute(x, axis, [(0, 1), (1, 0)])]
    dot_general x6 -> x7, matrix products: 3.93 us -> 3.49 us  [dot(): lax.dot_general(left, right, (dims, ((), ())), preferred_element_type=jnp...]
  transfers between devices with their start and end apart: 12 -> 11, of which waited for: 7 -> 8; matrix products, arithmetic and copies ran while one was open for 5% -> 4% of each run, Pallas kernels for 0% -> 0%
where the time goes in v5:
time: 157 us; the launch traced here: 156 us
  starting transfers between devices  58.7 us (37%)
  blocking collectives  48.7 us (31%)
  waiting for transfers between devices  37.9 us (24%)
  matrix products  3.49 us (2%)
  local copies, waits for them, and re-layouts  3.1 us (2%)
  other arithmetic  2.97 us (2%)
    all_to_all x2, blocking collectives, swap(): return lax.all_to_all(pieces, axes, split_axis=0, concat_axis=0, tiled=True)  48.7 us
    all_to_all x5, starting transfers between devices, swap(): return lax.all_to_all(pieces, axes, split_axis=0, concat_axis=0, tiled=True)  38.2 us
    all_to_all x5, waiting for transfers between devices, swap(): return lax.all_to_all(pieces, axes, split_axis=0, concat_axis=0, tiled=True)  31.6 us
    ppermute x5, starting transfers between devices, near(): other = lax.ppermute(x, axis, [(0, 1), (1, 0)])  16.6 us
    ppermute x5, waiting for transfers between devices, near(): other = lax.ppermute(x, axis, [(0, 1), (1, 0)])  6.24 us
    ppermute x1, starting transfers between devices, step(): acts_there = lax.ppermute(acts_here, 'yh', [(0, 1), (1, 0)])  3.86 us
    dot_general x7, matrix products, dot(): lax.dot_general(left, right, (dims, ((), ())), preferred_element_type=jnp...  3.49 us
  transfers between devices with their start and end apart: 11, of which 8 were waited for; matrix products, arithmetic and copies ran while one was open for 4% of the time, Pallas kernels for 0%

profile of v5, /device:TPU:8, one launch (start us, length us, event | category | flops | bytes accessed | tf_op | source)
XLA Modules:
  0.0 155.7 jit_solution(5211950839995138418)
XLA Ops:
  0.6 6.8 %collective-permute-start = (bf16[128,896]{1,0:T(8,128)(2,1)}, bf16[128,896]{1,0:T(8,128)(2,1)S(1)}, u32[]{:S(2)}, u32[]{:S(2)}) collective-permute-start(bf16[128,896]{1,0:T(8,128)(2,1)} %param.6), channel_id=1, source_target_pairs={{0,512},{512,0},{1,513},{513,1},{2,514},{514,2},{3,515},{515,3},{4... | collective-permute-start | bytes 688136 | tf_op jit(solution)/shard_map/ppermute | solution.py:31
  7.5 2.0 %fusion.7 = bf16[64,8,128]{2,1,0:T(8,128)(2,1)} fusion(bf16[512,512]{1,0:T(8,128)(2,1)} %param.7, bf16[128,512]{1,0:T(8,128)(2,1)} %param.5), kind=kOutput, calls=%fused_computation.13 | convolution fusion | flops 67239936 | bytes 786432 | tf_op jit(solution)/shard_map/dot_general | solution.py:26
  9.5 0.0 copy-start.1
  9.5 16.0 %all-to-all-start = ((bf16[64,8,128]{2,1,0:T(8,128)(2,1)}), bf16[64,8,128]{2,1,0:T(8,128)(2,1)S(1)}, u32[]{:S(2)}, u32[]{:S(2)}) async-start(bf16[64,8,128]{2,1,0:T(8,128)(2,1)} %fusion.7), calls=%async_computation | async-start | bytes 262144 | tf_op jit(solution)/shard_map/all_to_all | solution.py:14
  25.5 0.0 collective-permute-done
  25.6 0.0 copy-done.1
  25.6 0.1 pad_maximum_fusion.1
  25.6 2.0 %collective-permute-start.1 = (bf16[2,128,896]{2,1,0:T(8,128)(2,1)S(1)}, bf16[2,128,896]{2,1,0:T(8,128)(2,1)S(1)}, u32[]{:S(2)}, u32[]{:S(2)}) collective-permute-start(bf16[2,128,896]{2,1,0:T(8,128)(2,1)S(1)} %pad_maximum_fusion.1), channel_id=1, source_target_pairs={{0,16},{16,0},{1,17},{17,1},{2,18},{18,2},{3,19},{19,3},{4,20},{20... | collective-permute-start | bytes 1376264 | tf_op jit(solution)/shard_map/ppermute | solution.py:31
  27.7 8.3 %all-to-all-done = bf16[64,8,128]{2,1,0:T(8,128)(2,1)S(1)} async-done(((bf16[64,8,128]{2,1,0:T(8,128)(2,1)}), bf16[64,8,128]{2,1,0:T(8,128)(2,1)S(1)}, u32[]{:S(2)}, u32[]{:S(2)}) %all-to-all-start) | async-done | bytes 131104 | tf_op jit(solution)/shard_map/all_to_all | solution.py:14
  36.1 0.7 broadcast_in_dim.9
  36.7 4.6 %all-to-all-start.1 = ((bf16[16,2,2,8,128]{4,3,1,2,0:T(8,128)(2,1)}), bf16[16,2,2,8,128]{4,3,1,2,0:T(8,128)(2,1)S(1)}, u32[]{:S(2)}, u32[]{:S(2)}) async-start(bf16[16,2,2,8,128]{4,3,1,2,0:T(8,128)(2,1)} %broadcast_in_dim.9), calls=%async_computation.1 | async-start | bytes 262144 | tf_op jit(solution)/shard_map/all_to_all | solution.py:14
  41.4 0.0 collective-permute-done.1
  41.4 0.1 pad_maximum_fusion
  41.5 7.4 %all-to-all-done.1 = bf16[16,2,2,8,128]{4,3,1,2,0:T(8,128)(2,1)S(1)} async-done(((bf16[16,2,2,8,128]{4,3,1,2,0:T(8,128)(2,1)}), bf16[16,2,2,8,128]{4,3,1,2,0:T(8,128)(2,1)S(1)}, u32[]{:S(2)}, u32[]{:S(2)}) %all-to-all-start.1) | async-done | bytes 131104 | tf_op jit(solution)/shard_map/all_to_all | solution.py:14
  48.9 0.3 fusion.2
  49.2 26.3 %all_to_all.35 = bf16[16,8,896]{2,1,0:T(8,128)(2,1)S(1)} all-to-all(bf16[16,8,896]{2,1,0:T(8,128)(2,1)S(1)} %fusion.2), channel_id=1, replica_groups=mesh['yh'=2,'z'=16,'c'=2,'x'=4,'yl'=4] {'z'}, dimensions={0} | all-to-all | bytes 458752 | tf_op jit(solution)/shard_map/all_to_all | solution.py:14
  75.6 0.7 broadcast_in_dim.10
  76.3 5.3 %all-to-all-start.3 = ((bf16[16,8,896]{2,1,0:T(8,128)(2,1)}), bf16[16,8,896]{2,1,0:T(8,128)(2,1)S(1)}, u32[]{:S(2)}, u32[]{:S(2)}) async-start(bf16[16,8,896]{2,1,0:T(8,128)(2,1)} %broadcast_in_dim.10), calls=%async_computation.3 | async-start | bytes 458752 | tf_op jit(solution)/shard_map/all_to_all | solution.py:14
  81.6 1.9 %collective-permute-start.2 = (bf16[8,896]{1,0:T(8,128)(2,1)S(1)}, bf16[8,896]{1,0:T(8,128)(2,1)S(1)}, u32[]{:S(2)}, u32[]{:S(2)}) collective-permute-start(bf16[8,896]{1,0:T(8,128)(2,1)S(1)} %convert_element_type.44), channel_id=1, source_target_pairs={{0,16},{16,0},{1,17},{17,1},{2,18},{18,2},{3,19},{19,3},{4,20},{20... | collective-permute-start | bytes 43016 | tf_op jit(solution)/shard_map/ppermute | solution.py:31
  83.5 0.7 dynamic-slice_convert_fusion
  84.2 0.4 collective-permute-done.2
  84.7 3.9 %collective-permute-start.3 = (bf16[2,8,896]{2,1,0:T(8,128)(2,1)S(1)}, bf16[2,8,896]{2,1,0:T(8,128)(2,1)S(1)}, u32[]{:S(2)}, u32[]{:S(2)}) collective-permute-start(bf16[2,8,896]{2,1,0:T(8,128)(2,1)S(1)} %pad_maximum_fusion.4), channel_id=1, source_target_pairs={{0,512},{512,0},{1,513},{513,1},{2,514},{514,2},{3,515},{515,3},{4... | collective-permute-start | bytes 86024 | tf_op jit(solution)/shard_map/ppermute | solution.py:31
  88.6 0.0 copy-done.2
  88.6 0.0 copy-done.3
  88.6 0.6 fusion.16
  89.2 5.2 %collective-permute-done.3 = bf16[2,8,896]{2,1,0:T(8,128)(2,1)S(1)} collective-permute-done((bf16[2,8,896]{2,1,0:T(8,128)(2,1)S(1)}, bf16[2,8,896]{2,1,0:T(8,128)(2,1)S(1)}, u32[]{:S(2)}, u32[]{:S(2)}) %collective-permute-start.3) | collective-permute-done | bytes 28704 | tf_op jit(solution)/shard_map/ppermute | solution.py:31
  94.5 4.0 %all-to-all-done.3 = bf16[16,8,896]{2,1,0:T(8,128)(2,1)S(1)} async-done(((bf16[16,8,896]{2,1,0:T(8,128)(2,1)}), bf16[16,8,896]{2,1,0:T(8,128)(2,1)S(1)}, u32[]{:S(2)}, u32[]{:S(2)}) %all-to-all-start.3) | async-done | bytes 229408 | tf_op jit(solution)/shard_map/all_to_all | solution.py:14
  98.5 0.2 convolution_convert_fusion.1
  98.7 0.1 copy.23
  98.9 0.4 convolution_convert_fusion
  99.3 0.7 maximum_bitcast_fusion
  100.0 5.1 %all-to-all-start.4 = ((bf16[16,8,544]{2,1,0:T(8,128)(2,1)}), bf16[16,8,544]{2,1,0:T(8,128)(2,1)S(1)}, u32[]{:S(2)}, u32[]{:S(2)}) async-start(bf16[16,8,544]{2,1,0:T(8,128)(2,1)} %maximum_bitcast_fusion), calls=%async_computation.4 | async-start | bytes 327680 | tf_op jit(solution)/shard_map/all_to_all | solution.py:14
  105.1 0.0 copy-done
  105.1 1.9 %collective-permute-start.4 = (bf16[128,512]{1,0:T(8,128)(2,1)S(1)}, bf16[128,512]{1,0:T(8,128)(2,1)S(1)}, u32[]{:S(2)}, u32[]{:S(2)}) collective-permute-start(bf16[128,512]{1,0:T(8,128)(2,1)S(1)} %copy-done), channel_id=1, source_target_pairs={{0,16},{16,0},{1,17},{17,1},{2,18},{18,2},{3,19},{19,3},{4,20},{20... | collective-permute-start | bytes 393224 | tf_op jit(solution)/shard_map/ppermute | solution.py:31
  107.0 0.8 dynamic-slice_bitcast_fusion
  107.8 0.5 collective-permute-done.4
  108.4 3.9 %collective-permute-start.5 = (bf16[2,128,512]{2,1,0:T(8,128)(2,1)S(1)}, bf16[2,128,512]{2,1,0:T(8,128)(2,1)S(1)}, u32[]{:S(2)}, u32[]{:S(2)}) collective-permute-start(bf16[2,128,512]{2,1,0:T(8,128)(2,1)S(1)} %pad_maximum_fusion.2), channel_id=1, source_target_pairs={{0,512},{512,0},{1,513},{513,1},{2,514},{514,2},{3,515},{515,3},{4... | collective-permute-start | bytes 786440 | tf_op jit(solution)/shard_map/ppermute | solution.py:47
  112.2 0.4 all-to-all-done.4
  112.7 0.7 broadcast_in_dim.11
  113.3 7.1 %all-to-all-start.5 = ((bf16[16,8,544]{2,1,0:T(8,128)(2,1)}), bf16[16,8,544]{2,1,0:T(8,128)(2,1)S(1)}, u32[]{:S(2)}, u32[]{:S(2)}) async-start(bf16[16,8,544]{2,1,0:T(8,128)(2,1)} %broadcast_in_dim.11), calls=%async_computation.5 | async-start | bytes 327680 | tf_op jit(solution)/shard_map/all_to_all | solution.py:14
  120.5 11.4 %all-to-all-done.5 = bf16[16,8,544]{2,1,0:T(8,128)(2,1)S(1)} async-done(((bf16[16,8,544]{2,1,0:T(8,128)(2,1)}), bf16[16,8,544]{2,1,0:T(8,128)(2,1)S(1)}, u32[]{:S(2)}, u32[]{:S(2)}) %all-to-all-start.5) | async-done | bytes 139296 | tf_op jit(solution)/shard_map/all_to_all | solution.py:14
  131.9 0.1 copy.24
  132.1 0.0 collective-permute-done.5
  132.1 0.2 convolution_bitcast_fusion.1
  132.3 0.2 fusion.4
  132.5 0.2 fusion.8
  132.7 22.4 %all_to_all.36 = bf16[16,8,512]{2,1,0:T(8,128)(2,1)S(1)} all-to-all(bf16[16,8,512]{2,1,0:T(8,128)(2,1)S(1)} %fusion.8), channel_id=1, replica_groups=mesh['yh'=2,'z'=16,'c'=2,'x'=4,'yl'=4] {'z'}, dimensions={0} | all-to-all | bytes 262144 | tf_op jit(solution)/shard_map/all_to_all | solution.py:14
  155.1 0.6 add.40
  (17 shorter events, 0.2 us)
Async XLA Ops:
  0.6 24.9 %collective-permute-start = (bf16[128,896]{1,0:T(8,128)(2,1)}, bf16[128,896]{1,0:T(8,128)(2,1)S(1)}, u32[]{:S(2)}, u32[]{:S(2)}) collective-permute-start(bf16[128,896]{1,0:T(8,128)(2,1)} %param.6), channel_id=1, source_target_pairs={{0,512},{512,0},{1,513},{513,1},{2,514},{514,2},{3,515},{515,3},{4... | collective-permute-start | bytes 688136 | tf_op jit(solution)/shard_map/ppermute | solution.py:31
  9.5 16.1 %copy-start.1 = (bf16[128,896]{1,0:T(8,128)(2,1)S(1)}, bf16[128,896]{1,0:T(8,128)(2,1)}, u32[]{:S(2)}) copy-start(bf16[128,896]{1,0:T(8,128)(2,1)} %param.6) | copy-start | bytes 688132
  9.5 26.5 %all-to-all-start = ((bf16[64,8,128]{2,1,0:T(8,128)(2,1)}), bf16[64,8,128]{2,1,0:T(8,128)(2,1)S(1)}, u32[]{:S(2)}, u32[]{:S(2)}) async-start(bf16[64,8,128]{2,1,0:T(8,128)(2,1)} %fusion.7), calls=%async_computation | async-start | bytes 262144 | tf_op jit(solution)/shard_map/all_to_all | solution.py:14
  25.6 15.7 %collective-permute-start.1 = (bf16[2,128,896]{2,1,0:T(8,128)(2,1)S(1)}, bf16[2,128,896]{2,1,0:T(8,128)(2,1)S(1)}, u32[]{:S(2)}, u32[]{:S(2)}) collective-permute-start(bf16[2,128,896]{2,1,0:T(8,128)(2,1)S(1)} %pad_maximum_fusion.1), channel_id=1, source_target_pairs={{0,16},{16,0},{1,17},{17,1},{2,18},{18,2},{3,19},{19,3},{4,20},{20... | collective-permute-start | bytes 1376264 | tf_op jit(solution)/shard_map/ppermute | solution.py:31
  36.7 12.2 %all-to-all-start.1 = ((bf16[16,2,2,8,128]{4,3,1,2,0:T(8,128)(2,1)}), bf16[16,2,2,8,128]{4,3,1,2,0:T(8,128)(2,1)S(1)}, u32[]{:S(2)}, u32[]{:S(2)}) async-start(bf16[16,2,2,8,128]{4,3,1,2,0:T(8,128)(2,1)} %broadcast_in_dim.9), calls=%async_computation.1 | async-start | bytes 262144 | tf_op jit(solution)/shard_map/all_to_all | solution.py:14
  76.3 22.2 %all-to-all-start.3 = ((bf16[16,8,896]{2,1,0:T(8,128)(2,1)}), bf16[16,8,896]{2,1,0:T(8,128)(2,1)S(1)}, u32[]{:S(2)}, u32[]{:S(2)}) async-start(bf16[16,8,896]{2,1,0:T(8,128)(2,1)} %broadcast_in_dim.10), calls=%async_computation.3 | async-start | bytes 458752 | tf_op jit(solution)/shard_map/all_to_all | solution.py:14
  81.6 3.1 %collective-permute-start.2 = (bf16[8,896]{1,0:T(8,128)(2,1)S(1)}, bf16[8,896]{1,0:T(8,128)(2,1)S(1)}, u32[]{:S(2)}, u32[]{:S(2)}) collective-permute-start(bf16[8,896]{1,0:T(8,128)(2,1)S(1)} %convert_element_type.44), channel_id=1, source_target_pairs={{0,16},{16,0},{1,17},{17,1},{2,18},{18,2},{3,19},{19,3},{4,20},{20... | collective-permute-start | bytes 43016 | tf_op jit(solution)/shard_map/ppermute | solution.py:31
  84.7 3.9 %copy-start.2 = (f32[8,896]{1,0:T(8,128)S(1)}, f32[8,896]{1,0:T(8,128)}, u32[]{:S(2)}) copy-start(f32[8,896]{1,0:T(8,128)} %param.9) | copy-start | bytes 86020
  84.7 3.9 %copy-start.3 = (f32[8,896]{1,0:T(8,128)S(1)}, f32[8,896]{1,0:T(8,128)}, u32[]{:S(2)}) copy-start(f32[8,896]{1,0:T(8,128)} %param.8) | copy-start | bytes 86020
  84.7 9.8 %collective-permute-start.3 = (bf16[2,8,896]{2,1,0:T(8,128)(2,1)S(1)}, bf16[2,8,896]{2,1,0:T(8,128)(2,1)S(1)}, u32[]{:S(2)}, u32[]{:S(2)}) collective-permute-start(bf16[2,8,896]{2,1,0:T(8,128)(2,1)S(1)} %pad_maximum_fusion.4), channel_id=1, source_target_pairs={{0,512},{512,0},{1,513},{513,1},{2,514},{514,2},{3,515},{515,3},{4... | collective-permute-start | bytes 86024 | tf_op jit(solution)/shard_map/ppermute | solution.py:31
  100.0 5.1 %copy-start = (bf16[128,512]{1,0:T(8,128)(2,1)S(1)}, bf16[128,512]{1,0:T(8,128)(2,1)}, u32[]{:S(2)}) copy-start(bf16[128,512]{1,0:T(8,128)(2,1)} %param.5) | copy-start | bytes 393220
  100.0 12.7 %all-to-all-start.4 = ((bf16[16,8,544]{2,1,0:T(8,128)(2,1)}), bf16[16,8,544]{2,1,0:T(8,128)(2,1)S(1)}, u32[]{:S(2)}, u32[]{:S(2)}) async-start(bf16[16,8,544]{2,1,0:T(8,128)(2,1)} %maximum_bitcast_fusion), calls=%async_computation.4 | async-start | bytes 327680 | tf_op jit(solution)/shard_map/all_to_all | solution.py:14
  105.1 3.2 %collective-permute-start.4 = (bf16[128,512]{1,0:T(8,128)(2,1)S(1)}, bf16[128,512]{1,0:T(8,128)(2,1)S(1)}, u32[]{:S(2)}, u32[]{:S(2)}) collective-permute-start(bf16[128,512]{1,0:T(8,128)(2,1)S(1)} %copy-done), channel_id=1, source_target_pairs={{0,16},{16,0},{1,17},{17,1},{2,18},{18,2},{3,19},{19,3},{4,20},{20... | collective-permute-start | bytes 393224 | tf_op jit(solution)/shard_map/ppermute | solution.py:31
  108.4 23.7 %collective-permute-start.5 = (bf16[2,128,512]{2,1,0:T(8,128)(2,1)S(1)}, bf16[2,128,512]{2,1,0:T(8,128)(2,1)S(1)}, u32[]{:S(2)}, u32[]{:S(2)}) collective-permute-start(bf16[2,128,512]{2,1,0:T(8,128)(2,1)S(1)} %pad_maximum_fusion.2), channel_id=1, source_target_pairs={{0,512},{512,0},{1,513},{513,1},{2,514},{514,2},{3,515},{515,3},{4... | collective-permute-start | bytes 786440 | tf_op jit(solution)/shard_map/ppermute | solution.py:47
  113.3 18.6 %all-to-all-start.5 = ((bf16[16,8,544]{2,1,0:T(8,128)(2,1)}), bf16[16,8,544]{2,1,0:T(8,128)(2,1)S(1)}, u32[]{:S(2)}, u32[]{:S(2)}) async-start(bf16[16,8,544]{2,1,0:T(8,128)(2,1)} %broadcast_in_dim.11), calls=%async_computation.5 | async-start | bytes 327680 | tf_op jit(solution)/shard_map/all_to_all | solution.py:14

commit v6 on v5

--- a/solution.py
+++ b/solution.py
@@ -26,9 +26,13 @@
     return lax.dot_general(left, right, (dims, ((), ())), preferred_element_type=jnp.float32)
 
 
+def across(x, axis):
+    return lax.ppermute(x, axis, [(0, 1), (1, 0)])
+
+
 def near(x, axes):
     for axis in axes:
-        other = lax.ppermute(x, axis, [(0, 1), (1, 0)])
+        other = across(x, axis)
         x = lax.optimization_barrier(jnp.stack([x, other]))
     return x
 
@@ -42,9 +46,12 @@
 def step(acts, grad_out, proj_t, first_moment, second_moment):
     bf16 = jnp.bfloat16
     root = jnp.sqrt(jnp.float32(D))
-    grad_all = near(grad_out, ("yh", "c"))
+    grad_yh = across(grad_out, "yh")
+    grad_c = across(grad_out, "c")
+    grad_d = across(grad_yh, "c")
+    grad_all = jnp.stack([grad_out, grad_yh, grad_c, grad_d]).reshape(2, 2, 128, -1)
     acts_here = near(acts, ("c",))
-    acts_there = lax.ppermute(acts_here, "yh", [(0, 1), (1, 0)])
+    acts_there = across(acts_here, "yh")
     rows = proj_t.reshape(2, 16, 2, OWN, -1)
     rows = lax.dynamic_index_in_dim(rows, lax.axis_index("z"), 1, keepdims=False)
     rows = from_own(rows, ("yh", "c")).reshape(4 * OWN, -1)
@@ -52,12 +59,15 @@
     own_rows = own_rows.astype(jnp.float32)
     part = (dot(proj_t, acts, ((1,), (1,))) * (1.0 / root)).astype(bf16)
     got = swap(part.reshape(64, OWN, 128), ("yh", "x", "yl", "c"))
+    got, own_rows = lax.optimization_barrier((got, own_rows))
     part = jnp.sum(got.reshape(2, 16, 2, OWN, 128).astype(jnp.float32), axis=1)
     part = from_own(part, ("yh", "c")).astype(bf16)
     coords = to_all(part, TENSOR, 16)
     coords = coords.transpose(2, 1, 0, 3, 4).reshape(2, 2, 128, 128)
     grad_part = (dot(coords, grad_all, ((0, 1, 3), (0, 1, 2))) / TOKENS).astype(bf16)
-    grad_own = total(swap(grad_part.reshape(16, OWN, -1), "z"))
+    got = swap(grad_part.reshape(16, OWN, -1), "z")
+    got, rows = lax.optimization_barrier((got, rows))
+    grad_own = total(got)
     low_own = grad_own.astype(bf16)
     low_own, grad_own = lax.optimization_barrier((low_own, grad_own))
     moment_one = 0.9 * first_moment + 0.1 * grad_own
@@ -66,9 +76,7 @@
     adam_step = moment_one / (1.0 - 0.9**10) / root_two
     low = to_all(low_own, "z", 16).reshape(128, -1)
     low_rows = near(low_own, ("c", "yh")).reshape(4 * OWN, -1)
-    low, low_rows, own_rows, adam_step = lax.optimization_barrier(
-        (low, low_rows, own_rows, adam_step)
-    )
+    low, low_rows, adam_step = lax.optimization_barrier((low, low_rows, adam_step))
     back = dot(low, grad_all.reshape(512, -1), ((1,), (1,))).astype(bf16)
     cross = dot(low, low_rows, ((1,), (1,))).astype(bf16)
     both = jnp.concatenate([back, cross], axis=1)

time: 157 us -> 168 us (1.070)
  starting transfers between devices: 58.7 us -> 72.3 us
  blocking collectives: 48.7 us -> 42 us
  waiting for transfers between devices: 37.9 us -> 42.7 us
    ppermute x6 -> x7, waiting for transfers between devices: 6.24 us -> 15 us  [across(): return lax.ppermute(x, axis, [(0, 1), (1, 0)])]
    all_to_all x5, starting transfers between devices: 38.2 us -> 46.8 us  [swap(): return lax.all_to_all(pieces, axes, split_axis=0, concat_axis=0, tiled=True)]
    all_to_all x2, blocking collectives: 48.7 us -> 42 us  [swap(): return lax.all_to_all(pieces, axes, split_axis=0, concat_axis=0, tiled=True)]
    ppermute x6 -> x7, starting transfers between devices: 20.4 us -> 25.5 us  [across(): return lax.ppermute(x, axis, [(0, 1), (1, 0)])]
    all_to_all x5, waiting for transfers between devices: 31.6 us -> 27.7 us  [swap(): return lax.all_to_all(pieces, axes, split_axis=0, concat_axis=0, tiled=True)]
  transfers between devices with their start and end apart: 11 -> 12, of which waited for: 8 -> 7; matrix products, arithmetic and copies ran while one was open for 4% -> 2% of each run, Pallas kernels for 0% -> 0%
where the time goes in v6:
time: 168 us; the launch traced here: 167 us
  starting transfers between devices  72.3 us (43%)
  waiting for transfers between devices  42.7 us (25%)
  blocking collectives  42 us (25%)
  matrix products  4.16 us (2%)
  other arithmetic  2.98 us (2%)
  local copies, waits for them, and re-layouts  2.45 us (1%)
    all_to_all x5, starting transfers between devices, swap(): return lax.all_to_all(pieces, axes, split_axis=0, concat_axis=0, tiled=True)  46.8 us
    all_to_all x2, blocking collectives, swap(): return lax.all_to_all(pieces, axes, split_axis=0, concat_axis=0, tiled=True)  42 us
    all_to_all x5, waiting for transfers between devices, swap(): return lax.all_to_all(pieces, axes, split_axis=0, concat_axis=0, tiled=True)  27.7 us
    ppermute x7, starting transfers between devices, across(): return lax.ppermute(x, axis, [(0, 1), (1, 0)])  25.5 us
    ppermute x7, waiting for transfers between devices, across(): return lax.ppermute(x, axis, [(0, 1), (1, 0)])  15 us
    dot_general x7, matrix products, dot(): lax.dot_general(left, right, (dims, ((), ())), preferred_element_type=jnp...  4.16 us
  transfers between devices with their start and end apart: 12, of which 7 were waited for; matrix products, arithmetic and copies ran while one was open for 2% of the time, Pallas kernels for 0%

profile of v6, /device:TPU:8, one launch (start us, length us, event | category | flops | bytes accessed | tf_op | source)
XLA Modules:
  0.0 167.4 jit_solution(12368359938850258145)
XLA Ops:
  0.6 2.0 %fusion.7 = bf16[64,8,128]{2,1,0:T(8,128)(2,1)} fusion(bf16[512,512]{1,0:T(8,128)(2,1)} %param.7, bf16[128,512]{1,0:T(8,128)(2,1)} %param.5), kind=kOutput, calls=%fused_computation.13 | convolution fusion | flops 67239936 | bytes 786432 | tf_op jit(solution)/shard_map/dot_general | solution.py:26
  2.6 0.0 copy-start.1
  2.6 17.2 %all-to-all-start = ((bf16[64,8,128]{2,1,0:T(8,128)(2,1)}), bf16[64,8,128]{2,1,0:T(8,128)(2,1)S(1)}, u32[]{:S(2)}, u32[]{:S(2)}) async-start(bf16[64,8,128]{2,1,0:T(8,128)(2,1)} %fusion.7), calls=%async_computation | async-start | bytes 262144 | tf_op jit(solution)/shard_map/all_to_all | solution.py:14
  19.9 0.0 copy-done.1
  19.9 6.6 %collective-permute-start = (bf16[128,896]{1,0:T(8,128)(2,1)S(1)}, bf16[128,896]{1,0:T(8,128)(2,1)S(1)}, u32[]{:S(2)}, u32[]{:S(2)}) collective-permute-start(bf16[128,896]{1,0:T(8,128)(2,1)S(1)} %copy-done.1), channel_id=1, source_target_pairs={{0,512},{512,0},{1,513},{513,1},{2,514},{514,2},{3,515},{515,3},{4... | collective-permute-start | bytes 688136 | tf_op jit(solution)/shard_map/ppermute | solution.py:30
  26.5 1.9 %collective-permute-start.1 = (bf16[128,896]{1,0:T(8,128)(2,1)S(1)}, bf16[128,896]{1,0:T(8,128)(2,1)S(1)}, u32[]{:S(2)}, u32[]{:S(2)}) collective-permute-start(bf16[128,896]{1,0:T(8,128)(2,1)S(1)} %copy-done.1), channel_id=1, source_target_pairs={{0,16},{16,0},{1,17},{17,1},{2,18},{18,2},{3,19},{19,3},{4,20},{20... | collective-permute-start | bytes 688136 | tf_op jit(solution)/shard_map/ppermute | solution.py:30
  28.4 0.7 dynamic-slice_convert_fusion
  29.1 9.1 %collective-permute-done = bf16[128,896]{1,0:T(8,128)(2,1)S(1)} collective-permute-done((bf16[128,896]{1,0:T(8,128)(2,1)S(1)}, bf16[128,896]{1,0:T(8,128)(2,1)S(1)}, u32[]{:S(2)}, u32[]{:S(2)}) %collective-permute-start) | collective-permute-done | bytes 229408 | tf_op jit(solution)/shard_map/ppermute | solution.py:30
  38.2 1.9 %collective-permute-start.2 = (bf16[128,896]{1,0:T(8,128)(2,1)S(1)}, bf16[128,896]{1,0:T(8,128)(2,1)S(1)}, u32[]{:S(2)}, u32[]{:S(2)}) collective-permute-start(bf16[128,896]{1,0:T(8,128)(2,1)S(1)} %collective-permute-done), channel_id=1, source_target_pairs={{0,16},{16,0},{1,17},{17,1},{2,18},{18,2},{3,19},{19,3},{4,20},{20... | collective-permute-start | bytes 688136 | tf_op jit(solution)/shard_map/ppermute | solution.py:30
  40.1 0.0 all-to-all-done
  40.2 0.7 broadcast_in_dim.9
  40.9 6.9 %all-to-all-start.1 = ((bf16[16,2,2,8,128]{4,3,1,2,0:T(8,128)(2,1)}), bf16[16,2,2,8,128]{4,3,1,2,0:T(8,128)(2,1)S(1)}, u32[]{:S(2)}, u32[]{:S(2)}) async-start(bf16[16,2,2,8,128]{4,3,1,2,0:T(8,128)(2,1)} %broadcast_in_dim.9), calls=%async_computation.1 | async-start | bytes 262144 | tf_op jit(solution)/shard_map/all_to_all | solution.py:14
  47.8 0.0 collective-permute-done.1
  47.8 0.0 collective-permute-done.2
  47.8 0.1 pad_maximum_fusion
  47.9 7.4 %all-to-all-done.1 = bf16[16,2,2,8,128]{4,3,1,2,0:T(8,128)(2,1)S(1)} async-done(((bf16[16,2,2,8,128]{4,3,1,2,0:T(8,128)(2,1)}), bf16[16,2,2,8,128]{4,3,1,2,0:T(8,128)(2,1)S(1)}, u32[]{:S(2)}, u32[]{:S(2)}) %all-to-all-start.1) | async-done | bytes 131104 | tf_op jit(solution)/shard_map/all_to_all | solution.py:14
  55.4 1.0 fusion.2
  56.4 12.2 %all-to-all-start.2 = ((bf16[16,8,896]{2,1,0:T(8,128)(2,1)}), bf16[16,8,896]{2,1,0:T(8,128)(2,1)S(1)}, u32[]{:S(2)}, u32[]{:S(2)}) async-start(bf16[16,8,896]{2,1,0:T(8,128)(2,1)} %fusion.2), calls=%async_computation.2 | async-start | bytes 458752 | tf_op jit(solution)/shard_map/all_to_all | solution.py:14
  68.6 0.8 dynamic-slice_bitcast_fusion
  69.4 16.1 %all-to-all-done.2 = bf16[16,8,896]{2,1,0:T(8,128)(2,1)S(1)} async-done(((bf16[16,8,896]{2,1,0:T(8,128)(2,1)}), bf16[16,8,896]{2,1,0:T(8,128)(2,1)S(1)}, u32[]{:S(2)}, u32[]{:S(2)}) %all-to-all-start.2) | async-done | bytes 229408 | tf_op jit(solution)/shard_map/all_to_all | solution.py:14
  85.6 0.7 broadcast_in_dim.10
  86.3 5.4 %all-to-all-start.3 = ((bf16[16,8,896]{2,1,0:T(8,128)(2,1)}), bf16[16,8,896]{2,1,0:T(8,128)(2,1)S(1)}, u32[]{:S(2)}, u32[]{:S(2)}) async-start(bf16[16,8,896]{2,1,0:T(8,128)(2,1)} %broadcast_in_dim.10), calls=%async_computation.3 | async-start | bytes 458752 | tf_op jit(solution)/shard_map/all_to_all | solution.py:14
  91.6 1.9 %collective-permute-start.3 = (bf16[8,896]{1,0:T(8,128)(2,1)S(1)}, bf16[8,896]{1,0:T(8,128)(2,1)S(1)}, u32[]{:S(2)}, u32[]{:S(2)}) collective-permute-start(bf16[8,896]{1,0:T(8,128)(2,1)S(1)} %convert_element_type.45), channel_id=1, source_target_pairs={{0,16},{16,0},{1,17},{17,1},{2,18},{18,2},{3,19},{19,3},{4,20},{20... | collective-permute-start | bytes 43016 | tf_op jit(solution)/shard_map/ppermute | solution.py:30
  93.6 1.1 collective-permute-done.3
  94.7 5.7 %collective-permute-start.4 = (bf16[2,8,896]{2,1,0:T(8,128)(2,1)S(1)}, bf16[2,8,896]{2,1,0:T(8,128)(2,1)S(1)}, u32[]{:S(2)}, u32[]{:S(2)}) collective-permute-start(bf16[2,8,896]{2,1,0:T(8,128)(2,1)S(1)} %pad_maximum_fusion.3), channel_id=1, source_target_pairs={{0,512},{512,0},{1,513},{513,1},{2,514},{514,2},{3,515},{515,3},{4... | collective-permute-start | bytes 86024 | tf_op jit(solution)/shard_map/ppermute | solution.py:30
  100.4 0.0 copy-done.2
  100.4 0.0 copy-done.3
  100.4 0.6 fusion.16
  101.1 3.4 %collective-permute-done.4 = bf16[2,8,896]{2,1,0:T(8,128)(2,1)S(1)} collective-permute-done((bf16[2,8,896]{2,1,0:T(8,128)(2,1)S(1)}, bf16[2,8,896]{2,1,0:T(8,128)(2,1)S(1)}, u32[]{:S(2)}, u32[]{:S(2)}) %collective-permute-start.4) | collective-permute-done | bytes 28704 | tf_op jit(solution)/shard_map/ppermute | solution.py:30
  104.5 4.1 %all-to-all-done.3 = bf16[16,8,896]{2,1,0:T(8,128)(2,1)S(1)} async-done(((bf16[16,8,896]{2,1,0:T(8,128)(2,1)}), bf16[16,8,896]{2,1,0:T(8,128)(2,1)S(1)}, u32[]{:S(2)}, u32[]{:S(2)}) %all-to-all-start.3) | async-done | bytes 229408 | tf_op jit(solution)/shard_map/all_to_all | solution.py:14
  108.7 0.4 convolution_convert_fusion
  109.1 0.2 convolution_convert_fusion.1
  109.3 0.1 copy.23
  109.4 0.7 maximum_bitcast_fusion
  110.1 5.1 %all-to-all-start.4 = ((bf16[16,8,544]{2,1,0:T(8,128)(2,1)}), bf16[16,8,544]{2,1,0:T(8,128)(2,1)S(1)}, u32[]{:S(2)}, u32[]{:S(2)}) async-start(bf16[16,8,544]{2,1,0:T(8,128)(2,1)} %maximum_bitcast_fusion), calls=%async_computation.4 | async-start | bytes 327680 | tf_op jit(solution)/shard_map/all_to_all | solution.py:14
  115.2 0.0 copy-done
  115.2 1.9 %collective-permute-start.5 = (bf16[128,512]{1,0:T(8,128)(2,1)S(1)}, bf16[128,512]{1,0:T(8,128)(2,1)S(1)}, u32[]{:S(2)}, u32[]{:S(2)}) collective-permute-start(bf16[128,512]{1,0:T(8,128)(2,1)S(1)} %copy-done), channel_id=1, source_target_pairs={{0,16},{16,0},{1,17},{17,1},{2,18},{18,2},{3,19},{19,3},{4,20},{20... | collective-permute-start | bytes 393224 | tf_op jit(solution)/shard_map/ppermute | solution.py:30
  117.1 1.3 collective-permute-done.5
  118.4 5.5 %collective-permute-start.6 = (bf16[2,128,512]{2,1,0:T(8,128)(2,1)S(1)}, bf16[2,128,512]{2,1,0:T(8,128)(2,1)S(1)}, u32[]{:S(2)}, u32[]{:S(2)}) collective-permute-start(bf16[2,128,512]{2,1,0:T(8,128)(2,1)S(1)} %pad_maximum_fusion.1), channel_id=1, source_target_pairs={{0,512},{512,0},{1,513},{513,1},{2,514},{514,2},{3,515},{515,3},{4... | collective-permute-start | bytes 786440 | tf_op jit(solution)/shard_map/ppermute | solution.py:30
  124.0 0.0 all-to-all-done.4
  124.1 19.6 %all_to_all.35 = bf16[16,8,544]{2,1,0:T(8,128)(2,1)S(1)} all-to-all(bf16[16,8,544]{2,1,0:T(8,128)(2,1)S(1)} %broadcast_in_dim.11), channel_id=1, replica_groups=mesh['yh'=2,'z'=16,'c'=2,'x'=4,'yl'=4] {'x','yl'}, dimensions={0} | all-to-all | bytes 278528 | tf_op jit(solution)/shard_map/all_to_all | solution.py:14
  143.6 0.1 copy.24
  143.8 0.0 collective-permute-done.6
  143.8 0.2 convolution_bitcast_fusion.1
  144.0 0.2 fusion.4
  144.2 0.2 fusion.8
  144.4 22.4 %all_to_all.36 = bf16[16,8,512]{2,1,0:T(8,128)(2,1)S(1)} all-to-all(bf16[16,8,512]{2,1,0:T(8,128)(2,1)S(1)} %fusion.8), channel_id=1, replica_groups=mesh['yh'=2,'z'=16,'c'=2,'x'=4,'yl'=4] {'z'}, dimensions={0} | all-to-all | bytes 262144 | tf_op jit(solution)/shard_map/all_to_all | solution.py:14
  166.8 0.6 add.40
  (18 shorter events, 0.2 us)
Async XLA Ops:
  2.6 17.2 %copy-start.1 = (bf16[128,896]{1,0:T(8,128)(2,1)S(1)}, bf16[128,896]{1,0:T(8,128)(2,1)}, u32[]{:S(2)}) copy-start(bf16[128,896]{1,0:T(8,128)(2,1)} %param.6) | copy-start | bytes 688132
  2.6 37.5 %all-to-all-start = ((bf16[64,8,128]{2,1,0:T(8,128)(2,1)}), bf16[64,8,128]{2,1,0:T(8,128)(2,1)S(1)}, u32[]{:S(2)}, u32[]{:S(2)}) async-start(bf16[64,8,128]{2,1,0:T(8,128)(2,1)} %fusion.7), calls=%async_computation | async-start | bytes 262144 | tf_op jit(solution)/shard_map/all_to_all | solution.py:14
  19.9 18.3 %collective-permute-start = (bf16[128,896]{1,0:T(8,128)(2,1)S(1)}, bf16[128,896]{1,0:T(8,128)(2,1)S(1)}, u32[]{:S(2)}, u32[]{:S(2)}) collective-permute-start(bf16[128,896]{1,0:T(8,128)(2,1)S(1)} %copy-done.1), channel_id=1, source_target_pairs={{0,512},{512,0},{1,513},{513,1},{2,514},{514,2},{3,515},{515,3},{4... | collective-permute-start | bytes 688136 | tf_op jit(solution)/shard_map/ppermute | solution.py:30
  26.5 21.3 %collective-permute-start.1 = (bf16[128,896]{1,0:T(8,128)(2,1)S(1)}, bf16[128,896]{1,0:T(8,128)(2,1)S(1)}, u32[]{:S(2)}, u32[]{:S(2)}) collective-permute-start(bf16[128,896]{1,0:T(8,128)(2,1)S(1)} %copy-done.1), channel_id=1, source_target_pairs={{0,16},{16,0},{1,17},{17,1},{2,18},{18,2},{3,19},{19,3},{4,20},{20... | collective-permute-start | bytes 688136 | tf_op jit(solution)/shard_map/ppermute | solution.py:30
  38.2 9.6 %collective-permute-start.2 = (bf16[128,896]{1,0:T(8,128)(2,1)S(1)}, bf16[128,896]{1,0:T(8,128)(2,1)S(1)}, u32[]{:S(2)}, u32[]{:S(2)}) collective-permute-start(bf16[128,896]{1,0:T(8,128)(2,1)S(1)} %collective-permute-done), channel_id=1, source_target_pairs={{0,16},{16,0},{1,17},{17,1},{2,18},{18,2},{3,19},{19,3},{4,20},{20... | collective-permute-start | bytes 688136 | tf_op jit(solution)/shard_map/ppermute | solution.py:30
  40.9 14.5 %all-to-all-start.1 = ((bf16[16,2,2,8,128]{4,3,1,2,0:T(8,128)(2,1)}), bf16[16,2,2,8,128]{4,3,1,2,0:T(8,128)(2,1)S(1)}, u32[]{:S(2)}, u32[]{:S(2)}) async-start(bf16[16,2,2,8,128]{4,3,1,2,0:T(8,128)(2,1)} %broadcast_in_dim.9), calls=%async_computation.1 | async-start | bytes 262144 | tf_op jit(solution)/shard_map/all_to_all | solution.py:14
  56.4 29.1 %all-to-all-start.2 = ((bf16[16,8,896]{2,1,0:T(8,128)(2,1)}), bf16[16,8,896]{2,1,0:T(8,128)(2,1)S(1)}, u32[]{:S(2)}, u32[]{:S(2)}) async-start(bf16[16,8,896]{2,1,0:T(8,128)(2,1)} %fusion.2), calls=%async_computation.2 | async-start | bytes 458752 | tf_op jit(solution)/shard_map/all_to_all | solution.py:14
  86.3 22.4 %all-to-all-start.3 = ((bf16[16,8,896]{2,1,0:T(8,128)(2,1)}), bf16[16,8,896]{2,1,0:T(8,128)(2,1)S(1)}, u32[]{:S(2)}, u32[]{:S(2)}) async-start(bf16[16,8,896]{2,1,0:T(8,128)(2,1)} %broadcast_in_dim.10), calls=%async_computation.3 | async-start | bytes 458752 | tf_op jit(solution)/shard_map/all_to_all | solution.py:14
  91.6 3.1 %collective-permute-start.3 = (bf16[8,896]{1,0:T(8,128)(2,1)S(1)}, bf16[8,896]{1,0:T(8,128)(2,1)S(1)}, u32[]{:S(2)}, u32[]{:S(2)}) collective-permute-start(bf16[8,896]{1,0:T(8,128)(2,1)S(1)} %convert_element_type.45), channel_id=1, source_target_pairs={{0,16},{16,0},{1,17},{17,1},{2,18},{18,2},{3,19},{19,3},{4,20},{20... | collective-permute-start | bytes 43016 | tf_op jit(solution)/shard_map/ppermute | solution.py:30
  94.7 5.7 %copy-start.2 = (f32[8,896]{1,0:T(8,128)S(1)}, f32[8,896]{1,0:T(8,128)}, u32[]{:S(2)}) copy-start(f32[8,896]{1,0:T(8,128)} %param.9) | copy-start | bytes 86020
  94.7 5.7 %copy-start.3 = (f32[8,896]{1,0:T(8,128)S(1)}, f32[8,896]{1,0:T(8,128)}, u32[]{:S(2)}) copy-start(f32[8,896]{1,0:T(8,128)} %param.8) | copy-start | bytes 86020
  94.7 9.8 %collective-permute-start.4 = (bf16[2,8,896]{2,1,0:T(8,128)(2,1)S(1)}, bf16[2,8,896]{2,1,0:T(8,128)(2,1)S(1)}, u32[]{:S(2)}, u32[]{:S(2)}) collective-permute-start(bf16[2,8,896]{2,1,0:T(8,128)(2,1)S(1)} %pad_maximum_fusion.3), channel_id=1, source_target_pairs={{0,512},{512,0},{1,513},{513,1},{2,514},{514,2},{3,515},{515,3},{4... | collective-permute-start | bytes 86024 | tf_op jit(solution)/shard_map/ppermute | solution.py:30
  110.1 5.1 %copy-start = (bf16[128,512]{1,0:T(8,128)(2,1)S(1)}, bf16[128,512]{1,0:T(8,128)(2,1)}, u32[]{:S(2)}) copy-start(bf16[128,512]{1,0:T(8,128)(2,1)} %param.5) | copy-start | bytes 393220
  110.1 13.9 %all-to-all-start.4 = ((bf16[16,8,544]{2,1,0:T(8,128)(2,1)}), bf16[16,8,544]{2,1,0:T(8,128)(2,1)S(1)}, u32[]{:S(2)}, u32[]{:S(2)}) async-start(bf16[16,8,544]{2,1,0:T(8,128)(2,1)} %maximum_bitcast_fusion), calls=%async_computation.4 | async-start | bytes 327680 | tf_op jit(solution)/shard_map/all_to_all | solution.py:14
  115.2 3.2 %collective-permute-start.5 = (bf16[128,512]{1,0:T(8,128)(2,1)S(1)}, bf16[128,512]{1,0:T(8,128)(2,1)S(1)}, u32[]{:S(2)}, u32[]{:S(2)}) collective-permute-start(bf16[128,512]{1,0:T(8,128)(2,1)S(1)} %copy-done), channel_id=1, source_target_pairs={{0,16},{16,0},{1,17},{17,1},{2,18},{18,2},{3,19},{19,3},{4,20},{20... | collective-permute-start | bytes 393224 | tf_op jit(solution)/shard_map/ppermute | solution.py:30
  118.4 25.3 %collective-permute-start.6 = (bf16[2,128,512]{2,1,0:T(8,128)(2,1)S(1)}, bf16[2,128,512]{2,1,0:T(8,128)(2,1)S(1)}, u32[]{:S(2)}, u32[]{:S(2)}) collective-permute-start(bf16[2,128,512]{2,1,0:T(8,128)(2,1)S(1)} %pad_maximum_fusion.1), channel_id=1, source_target_pairs={{0,512},{512,0},{1,513},{513,1},{2,514},{514,2},{3,515},{515,3},{4... | collective-permute-start | bytes 786440 | tf_op jit(solution)/shard_map/ppermute | solution.py:30

commit v7 on v6

--- a/solution.py
+++ b/solution.py
@@ -26,15 +26,9 @@
     return lax.dot_general(left, right, (dims, ((), ())), preferred_element_type=jnp.float32)
 
 
-def across(x, axis):
-    return lax.ppermute(x, axis, [(0, 1), (1, 0)])
-
-
-def near(x, axes):
-    for axis in axes:
-        other = across(x, axis)
-        x = lax.optimization_barrier(jnp.stack([x, other]))
-    return x
+def across(x, *axes):
+    last = 2 ** len(axes) - 1
+    return lax.ppermute(x, axes, [(i, last - i) for i in range(last + 1)])
 
 
 def from_own(x, axes):
@@ -49,8 +43,9 @@
     grad_yh = across(grad_out, "yh")
     grad_c = across(grad_out, "c")
     grad_d = across(grad_yh, "c")
-    grad_all = jnp.stack([grad_out, grad_yh, grad_c, grad_d]).reshape(2, 2, 128, -1)
-    acts_here = near(acts, ("c",))
+    grad_all = jnp.stack([grad_out, grad_c, grad_yh, grad_d]).reshape(2, 2, 128, -1)
+    acts_c = across(acts, "c")
+    acts_here = lax.optimization_barrier(jnp.concatenate([acts, acts_c]))
     acts_there = across(acts_here, "yh")
     rows = proj_t.reshape(2, 16, 2, OWN, -1)
     rows = lax.dynamic_index_in_dim(rows, lax.axis_index("z"), 1, keepdims=False)
@@ -63,7 +58,7 @@
     part = jnp.sum(got.reshape(2, 16, 2, OWN, 128).astype(jnp.float32), axis=1)
     part = from_own(part, ("yh", "c")).astype(bf16)
     coords = to_all(part, TENSOR, 16)
-    coords = coords.transpose(2, 1, 0, 3, 4).reshape(2, 2, 128, 128)
+    coords = coords.transpose(1, 2, 0, 3, 4).reshape(2, 2, 128, 128)
     grad_part = (dot(coords, grad_all, ((0, 1, 3), (0, 1, 2))) / TOKENS).astype(bf16)
     got = swap(grad_part.reshape(16, OWN, -1), "z")
     got, rows = lax.optimization_barrier((got, rows))
@@ -75,16 +70,18 @@
     root_two = jnp.sqrt(moment_two / (1.0 - 0.999**10)) + 1e-08
     adam_step = moment_one / (1.0 - 0.9**10) / root_two
     low = to_all(low_own, "z", 16).reshape(128, -1)
-    low_rows = near(low_own, ("c", "yh")).reshape(4 * OWN, -1)
+    low_yh = across(low_own, "yh")
+    low_d = across(low_own, "yh", "c")
+    low_c = across(low_own, "c")
+    low_rows = jnp.concatenate([low_own, low_c, low_yh, low_d])
     low, low_rows, adam_step = lax.optimization_barrier((low, low_rows, adam_step))
     back = dot(low, grad_all.reshape(512, -1), ((1,), (1,))).astype(bf16)
     cross = dot(low, low_rows, ((1,), (1,))).astype(bf16)
     both = jnp.concatenate([back, cross], axis=1)
     both = total(swap(both.reshape(16, OWN, 544), TENSOR)).astype(bf16)
     both = to_all(both, TENSOR, 16).reshape(128, 544)
-    back = both[:, :512].reshape(128, 2, 2, 128)
-    pull = dot(back[:, :, 0], acts_here, ((1, 2), (0, 1)))
-    pull = (pull + dot(back[:, :, 1], acts_there, ((1, 2), (0, 1)))) * (root / TOKENS)
+    pull = dot(both[:, :256], acts_here, ((1,), (0,)))
+    pull = (pull + dot(both[:, 256:512], acts_there, ((1,), (0,)))) * (root / TOKENS)
     correction = dot(both[:, 512:], rows, ((1,), (0,)))
     moved = total(swap((pull - correction).astype(bf16).reshape(16, OWN, -1), "z"))
     return (adam_step, own_rows + moved)

time: 168 us -> 172 us (1.024)
  the two profiles are of different devices: /device:TPU:8 before, /device:TPU:18 now
where the time goes in v7:
time: 172 us; the launch traced here: 171 us
  starting transfers between devices  83.2 us (48%)
  waiting for transfers between devices  52.6 us (31%)
  blocking collectives  24.3 us (14%)
  matrix products  4.15 us (2%)
  local copies, waits for them, and re-layouts  3.01 us (2%)
  other arithmetic  2.97 us (2%)
    all_to_all x6, starting transfers between devices, swap(): return lax.all_to_all(pieces, axes, split_axis=0, concat_axis=0, tiled=True)  54.7 us
    all_to_all x6, waiting for transfers between devices, swap(): return lax.all_to_all(pieces, axes, split_axis=0, concat_axis=0, tiled=True)  28.5 us
    ppermute x8, starting transfers between devices, across(): return lax.ppermute(x, axes, [(i, last - i) for i in range(last + 1)])  28.5 us
    all_to_all x1, blocking collectives, swap(): return lax.all_to_all(pieces, axes, split_axis=0, concat_axis=0, tiled=True)  24.3 us
    ppermute x8, waiting for transfers between devices, across(): return lax.ppermute(x, axes, [(i, last - i) for i in range(last + 1)])  24.1 us
    dot_general x7, matrix products, dot(): lax.dot_general(left, right, (dims, ((), ())), preferred_element_type=jnp...  4.15 us
  transfers between devices with their start and end apart: 14, of which 7 were waited for; matrix products, arithmetic and copies ran while one was open for 2% of the time, Pallas kernels for 0%

profile of v7, /device:TPU:18, one launch (start us, length us, event | category | flops | bytes accessed | tf_op | source)
XLA Modules:
  0.0 171.1 jit_solution(7839214111631313371)
XLA Ops:
  0.6 2.0 %fusion.8 = bf16[64,8,128]{2,1,0:T(8,128)(2,1)} fusion(bf16[512,512]{1,0:T(8,128)(2,1)} %param.7, bf16[128,512]{1,0:T(8,128)(2,1)} %param.5), kind=kOutput, calls=%fused_computation.12 | convolution fusion | flops 67239936 | bytes 786432 | tf_op jit(solution)/shard_map/dot_general | solution.py:26
  2.6 17.2 %all-to-all-start = ((bf16[64,8,128]{2,1,0:T(8,128)(2,1)}), bf16[64,8,128]{2,1,0:T(8,128)(2,1)S(1)}, u32[]{:S(2)}, u32[]{:S(2)}) async-start(bf16[64,8,128]{2,1,0:T(8,128)(2,1)} %fusion.8), calls=%async_computation | async-start | bytes 262144 | tf_op jit(solution)/shard_map/all_to_all | solution.py:14
  19.8 0.0 copy-done.1
  19.8 5.7 %collective-permute-start.1 = (bf16[128,896]{1,0:T(8,128)(2,1)S(1)}, bf16[128,896]{1,0:T(8,128)(2,1)S(1)}, u32[]{:S(2)}, u32[]{:S(2)}) collective-permute-start(bf16[128,896]{1,0:T(8,128)(2,1)S(1)} %copy-done.1), channel_id=1, source_target_pairs={{0,512},{512,0},{1,513},{513,1},{2,514},{514,2},{3,515},{515,3},{4... | collective-permute-start | bytes 688136 | tf_op jit(solution)/shard_map/ppermute | solution.py:31
  25.5 1.9 %collective-permute-start = (bf16[128,896]{1,0:T(8,128)(2,1)S(1)}, bf16[128,896]{1,0:T(8,128)(2,1)S(1)}, u32[]{:S(2)}, u32[]{:S(2)}) collective-permute-start(bf16[128,896]{1,0:T(8,128)(2,1)S(1)} %copy-done.1), channel_id=1, source_target_pairs={{0,16},{16,0},{1,17},{17,1},{2,18},{18,2},{3,19},{19,3},{4,20},{20... | collective-permute-start | bytes 688136 | tf_op jit(solution)/shard_map/ppermute | solution.py:31
  27.5 0.7 dynamic-slice_convert_fusion
  28.2 10.1 %collective-permute-done.1 = bf16[128,896]{1,0:T(8,128)(2,1)S(1)} collective-permute-done((bf16[128,896]{1,0:T(8,128)(2,1)S(1)}, bf16[128,896]{1,0:T(8,128)(2,1)S(1)}, u32[]{:S(2)}, u32[]{:S(2)}) %collective-permute-start.1) | collective-permute-done | bytes 229408 | tf_op jit(solution)/shard_map/ppermute | solution.py:31
  38.3 1.9 %collective-permute-start.2 = (bf16[128,896]{1,0:T(8,128)(2,1)S(1)}, bf16[128,896]{1,0:T(8,128)(2,1)S(1)}, u32[]{:S(2)}, u32[]{:S(2)}) collective-permute-start(bf16[128,896]{1,0:T(8,128)(2,1)S(1)} %collective-permute-done.1), channel_id=1, source_target_pairs={{0,16},{16,0},{1,17},{17,1},{2,18},{18,2},{3,19},{19,3},{4,20},{20... | collective-permute-start | bytes 688136 | tf_op jit(solution)/shard_map/ppermute | solution.py:31
  40.2 0.0 all-to-all-done
  40.3 0.7 broadcast_in_dim.9
  40.9 6.7 %all-to-all-start.1 = ((bf16[16,2,2,8,128]{4,3,2,1,0:T(8,128)(2,1)}), bf16[16,2,2,8,128]{4,3,2,1,0:T(8,128)(2,1)S(1)}, u32[]{:S(2)}, u32[]{:S(2)}) async-start(bf16[16,2,2,8,128]{4,3,2,1,0:T(8,128)(2,1)} %broadcast_in_dim.9), calls=%async_computation.1 | async-start | bytes 262144 | tf_op jit(solution)/shard_map/all_to_all | solution.py:14
  47.6 0.0 collective-permute-done
  47.6 0.0 collective-permute-done.2
  47.7 0.1 pad_maximum_fusion
  47.8 5.6 %all-to-all-done.1 = bf16[16,2,2,8,128]{4,3,2,1,0:T(8,128)(2,1)S(1)} async-done(((bf16[16,2,2,8,128]{4,3,2,1,0:T(8,128)(2,1)}), bf16[16,2,2,8,128]{4,3,2,1,0:T(8,128)(2,1)S(1)}, u32[]{:S(2)}, u32[]{:S(2)}) %all-to-all-start.1) | async-done | bytes 131104 | tf_op jit(solution)/shard_map/all_to_all | solution.py:14
  53.4 1.0 fusion.4
  54.4 12.2 %all-to-all-start.2 = ((bf16[16,8,896]{2,1,0:T(8,128)(2,1)}), bf16[16,8,896]{2,1,0:T(8,128)(2,1)S(1)}, u32[]{:S(2)}, u32[]{:S(2)}) async-start(bf16[16,8,896]{2,1,0:T(8,128)(2,1)} %fusion.4), calls=%async_computation.2 | async-start | bytes 458752 | tf_op jit(solution)/shard_map/all_to_all | solution.py:14
  66.6 0.8 dynamic-slice_bitcast_fusion
  67.4 16.2 %all-to-all-done.2 = bf16[16,8,896]{2,1,0:T(8,128)(2,1)S(1)} async-done(((bf16[16,8,896]{2,1,0:T(8,128)(2,1)}), bf16[16,8,896]{2,1,0:T(8,128)(2,1)S(1)}, u32[]{:S(2)}, u32[]{:S(2)}) %all-to-all-start.2) | async-done | bytes 229408 | tf_op jit(solution)/shard_map/all_to_all | solution.py:14
  83.6 0.7 broadcast_in_dim.10
  84.4 5.5 %all-to-all-start.3 = ((bf16[16,8,896]{2,1,0:T(8,128)(2,1)}), bf16[16,8,896]{2,1,0:T(8,128)(2,1)S(1)}, u32[]{:S(2)}, u32[]{:S(2)}) async-start(bf16[16,8,896]{2,1,0:T(8,128)(2,1)} %broadcast_in_dim.10), calls=%async_computation.3 | async-start | bytes 458752 | tf_op jit(solution)/shard_map/all_to_all | solution.py:14
  89.9 4.4 %collective-permute-start.5 = (bf16[8,896]{1,0:T(8,128)(2,1)S(1)}, bf16[8,896]{1,0:T(8,128)(2,1)S(1)}, u32[]{:S(2)}, u32[]{:S(2)}) collective-permute-start(bf16[8,896]{1,0:T(8,128)(2,1)S(1)} %convert_element_type.45), channel_id=1, source_target_pairs={{0,528},{16,512},{512,16},{528,0},{1,529},{17,513},{513,17},{529,1... | collective-permute-start | bytes 43016 | tf_op jit(solution)/shard_map/ppermute | solution.py:31
  94.3 4.2 %collective-permute-start.4 = (bf16[8,896]{1,0:T(8,128)(2,1)S(1)}, bf16[8,896]{1,0:T(8,128)(2,1)S(1)}, u32[]{:S(2)}, u32[]{:S(2)}) collective-permute-start(bf16[8,896]{1,0:T(8,128)(2,1)S(1)} %convert_element_type.45), channel_id=1, source_target_pairs={{0,512},{512,0},{1,513},{513,1},{2,514},{514,2},{3,515},{515,3},{4... | collective-permute-start | bytes 43016 | tf_op jit(solution)/shard_map/ppermute | solution.py:31
  98.5 2.9 %collective-permute-start.3 = (bf16[8,896]{1,0:T(8,128)(2,1)S(1)}, bf16[8,896]{1,0:T(8,128)(2,1)S(1)}, u32[]{:S(2)}, u32[]{:S(2)}) collective-permute-start(bf16[8,896]{1,0:T(8,128)(2,1)S(1)} %convert_element_type.45), channel_id=1, source_target_pairs={{0,16},{16,0},{1,17},{17,1},{2,18},{18,2},{3,19},{19,3},{4,20},{20... | collective-permute-start | bytes 43016 | tf_op jit(solution)/shard_map/ppermute | solution.py:31
  101.4 0.6 fusion.20
  102.0 0.0 collective-permute-done.5
  102.0 1.8 %collective-permute-done.4 = bf16[8,896]{1,0:T(8,128)(2,1)S(1)} collective-permute-done((bf16[8,896]{1,0:T(8,128)(2,1)S(1)}, bf16[8,896]{1,0:T(8,128)(2,1)S(1)}, u32[]{:S(2)}, u32[]{:S(2)}) %collective-permute-start.4) | collective-permute-done | bytes 14368 | tf_op jit(solution)/shard_map/ppermute | solution.py:31
  103.9 0.0 collective-permute-done.3
  103.9 3.2 %all-to-all-done.3 = bf16[16,8,896]{2,1,0:T(8,128)(2,1)S(1)} async-done(((bf16[16,8,896]{2,1,0:T(8,128)(2,1)}), bf16[16,8,896]{2,1,0:T(8,128)(2,1)S(1)}, u32[]{:S(2)}, u32[]{:S(2)}) %all-to-all-start.3) | async-done | bytes 229408 | tf_op jit(solution)/shard_map/all_to_all | solution.py:14
  107.0 0.2 convolution_convert_fusion.1
  107.2 0.1 copy.11
  107.3 0.4 convolution_convert_fusion
  107.8 0.7 maximum_bitcast_fusion
  108.5 6.7 %all-to-all-start.4 = ((bf16[16,8,544]{2,1,0:T(8,128)(2,1)}), bf16[16,8,544]{2,1,0:T(8,128)(2,1)S(1)}, u32[]{:S(2)}, u32[]{:S(2)}) async-start(bf16[16,8,544]{2,1,0:T(8,128)(2,1)} %maximum_bitcast_fusion), calls=%async_computation.4 | async-start | bytes 327680 | tf_op jit(solution)/shard_map/all_to_all | solution.py:14
  115.2 0.0 copy-done
  115.2 1.9 %collective-permute-start.6 = (bf16[128,512]{1,0:T(8,128)(2,1)S(1)}, bf16[128,512]{1,0:T(8,128)(2,1)S(1)}, u32[]{:S(2)}, u32[]{:S(2)}) collective-permute-start(bf16[128,512]{1,0:T(8,128)(2,1)S(1)} %copy-done), channel_id=1, source_target_pairs={{0,16},{16,0},{1,17},{17,1},{2,18},{18,2},{3,19},{19,3},{4,20},{20... | collective-permute-start | bytes 393224 | tf_op jit(solution)/shard_map/ppermute | solution.py:31
  117.1 3.6 %all-to-all-done.4 = bf16[16,8,544]{2,1,0:T(8,128)(2,1)S(1)} async-done(((bf16[16,8,544]{2,1,0:T(8,128)(2,1)}), bf16[16,8,544]{2,1,0:T(8,128)(2,1)S(1)}, u32[]{:S(2)}, u32[]{:S(2)}) %all-to-all-start.4) | async-done | bytes 139296 | tf_op jit(solution)/shard_map/all_to_all | solution.py:14
  120.8 0.7 broadcast_in_dim.11
  121.5 6.4 %all-to-all-start.5 = ((bf16[16,8,544]{2,1,0:T(8,128)(2,1)}), bf16[16,8,544]{2,1,0:T(8,128)(2,1)S(1)}, u32[]{:S(2)}, u32[]{:S(2)}) async-start(bf16[16,8,544]{2,1,0:T(8,128)(2,1)} %broadcast_in_dim.11), calls=%async_computation.5 | async-start | bytes 327680 | tf_op jit(solution)/shard_map/all_to_all | solution.py:14
  127.9 0.0 collective-permute-done.6
  127.9 5.6 %collective-permute-start.7 = (bf16[256,512]{1,0:T(8,128)(2,1)S(1)}, bf16[256,512]{1,0:T(8,128)(2,1)S(1)}, u32[]{:S(2)}, u32[]{:S(2)}) collective-permute-start(bf16[256,512]{1,0:T(8,128)(2,1)S(1)} %pad_maximum_fusion.1), channel_id=1, source_target_pairs={{0,512},{512,0},{1,513},{513,1},{2,514},{514,2},{3,515},{515,3},{4... | collective-permute-start | bytes 786440 | tf_op jit(solution)/shard_map/ppermute | solution.py:31
  133.5 0.0 all-to-all-done.5
  133.5 0.2 fusion.14
  133.6 12.2 %collective-permute-done.7 = bf16[256,512]{1,0:T(8,128)(2,1)S(1)} collective-permute-done((bf16[256,512]{1,0:T(8,128)(2,1)S(1)}, bf16[256,512]{1,0:T(8,128)(2,1)S(1)}, u32[]{:S(2)}, u32[]{:S(2)}) %collective-permute-start.7) | collective-permute-done | bytes 262176 | tf_op jit(solution)/shard_map/ppermute | solution.py:31
  145.8 0.2 fusion.11
  146.0 0.2 fusion.7
  146.2 24.3 %all_to_all.35 = bf16[16,8,512]{2,1,0:T(8,128)(2,1)S(1)} all-to-all(bf16[16,8,512]{2,1,0:T(8,128)(2,1)S(1)} %fusion.7), channel_id=1, replica_groups=mesh['yh'=2,'z'=16,'c'=2,'x'=4,'yl'=4] {'z'}, dimensions={0} | all-to-all | bytes 262144 | tf_op jit(solution)/shard_map/all_to_all | solution.py:14
  170.5 0.6 add.40
  (17 shorter events, 0.2 us)
Async XLA Ops:
  2.6 17.2 %copy-start.1 = (bf16[128,896]{1,0:T(8,128)(2,1)S(1)}, bf16[128,896]{1,0:T(8,128)(2,1)}, u32[]{:S(2)}) copy-start(bf16[128,896]{1,0:T(8,128)(2,1)} %param.6) | copy-start | bytes 688132
  2.6 37.6 %all-to-all-start = ((bf16[64,8,128]{2,1,0:T(8,128)(2,1)}), bf16[64,8,128]{2,1,0:T(8,128)(2,1)S(1)}, u32[]{:S(2)}, u32[]{:S(2)}) async-start(bf16[64,8,128]{2,1,0:T(8,128)(2,1)} %fusion.8), calls=%async_computation | async-start | bytes 262144 | tf_op jit(solution)/shard_map/all_to_all | solution.py:14
  19.8 18.5 %collective-permute-start.1 = (bf16[128,896]{1,0:T(8,128)(2,1)S(1)}, bf16[128,896]{1,0:T(8,128)(2,1)S(1)}, u32[]{:S(2)}, u32[]{:S(2)}) collective-permute-start(bf16[128,896]{1,0:T(8,128)(2,1)S(1)} %copy-done.1), channel_id=1, source_target_pairs={{0,512},{512,0},{1,513},{513,1},{2,514},{514,2},{3,515},{515,3},{4... | collective-permute-start | bytes 688136 | tf_op jit(solution)/shard_map/ppermute | solution.py:31
  25.5 22.1 %collective-permute-start = (bf16[128,896]{1,0:T(8,128)(2,1)S(1)}, bf16[128,896]{1,0:T(8,128)(2,1)S(1)}, u32[]{:S(2)}, u32[]{:S(2)}) collective-permute-start(bf16[128,896]{1,0:T(8,128)(2,1)S(1)} %copy-done.1), channel_id=1, source_target_pairs={{0,16},{16,0},{1,17},{17,1},{2,18},{18,2},{3,19},{19,3},{4,20},{20... | collective-permute-start | bytes 688136 | tf_op jit(solution)/shard_map/ppermute | solution.py:31
  38.3 9.4 %collective-permute-start.2 = (bf16[128,896]{1,0:T(8,128)(2,1)S(1)}, bf16[128,896]{1,0:T(8,128)(2,1)S(1)}, u32[]{:S(2)}, u32[]{:S(2)}) collective-permute-start(bf16[128,896]{1,0:T(8,128)(2,1)S(1)} %collective-permute-done.1), channel_id=1, source_target_pairs={{0,16},{16,0},{1,17},{17,1},{2,18},{18,2},{3,19},{19,3},{4,20},{20... | collective-permute-start | bytes 688136 | tf_op jit(solution)/shard_map/ppermute | solution.py:31
  40.9 12.4 %all-to-all-start.1 = ((bf16[16,2,2,8,128]{4,3,2,1,0:T(8,128)(2,1)}), bf16[16,2,2,8,128]{4,3,2,1,0:T(8,128)(2,1)S(1)}, u32[]{:S(2)}, u32[]{:S(2)}) async-start(bf16[16,2,2,8,128]{4,3,2,1,0:T(8,128)(2,1)} %broadcast_in_dim.9), calls=%async_computation.1 | async-start | bytes 262144 | tf_op jit(solution)/shard_map/all_to_all | solution.py:14
  54.4 29.2 %all-to-all-start.2 = ((bf16[16,8,896]{2,1,0:T(8,128)(2,1)}), bf16[16,8,896]{2,1,0:T(8,128)(2,1)S(1)}, u32[]{:S(2)}, u32[]{:S(2)}) async-start(bf16[16,8,896]{2,1,0:T(8,128)(2,1)} %fusion.4), calls=%async_computation.2 | async-start | bytes 458752 | tf_op jit(solution)/shard_map/all_to_all | solution.py:14
  84.3 17.0 %copy-start.2 = (f32[8,896]{1,0:T(8,128)S(1)}, f32[8,896]{1,0:T(8,128)}, u32[]{:S(2)}) copy-start(f32[8,896]{1,0:T(8,128)} %param.9) | copy-start | bytes 86020
  84.4 17.0 %copy-start.3 = (f32[8,896]{1,0:T(8,128)S(1)}, f32[8,896]{1,0:T(8,128)}, u32[]{:S(2)}) copy-start(f32[8,896]{1,0:T(8,128)} %param.8) | copy-start | bytes 86020
  84.4 22.7 %all-to-all-start.3 = ((bf16[16,8,896]{2,1,0:T(8,128)(2,1)}), bf16[16,8,896]{2,1,0:T(8,128)(2,1)S(1)}, u32[]{:S(2)}, u32[]{:S(2)}) async-start(bf16[16,8,896]{2,1,0:T(8,128)(2,1)} %broadcast_in_dim.10), calls=%async_computation.3 | async-start | bytes 458752 | tf_op jit(solution)/shard_map/all_to_all | solution.py:14
  89.9 12.2 %collective-permute-start.5 = (bf16[8,896]{1,0:T(8,128)(2,1)S(1)}, bf16[8,896]{1,0:T(8,128)(2,1)S(1)}, u32[]{:S(2)}, u32[]{:S(2)}) collective-permute-start(bf16[8,896]{1,0:T(8,128)(2,1)S(1)} %convert_element_type.45), channel_id=1, source_target_pairs={{0,528},{16,512},{512,16},{528,0},{1,529},{17,513},{513,17},{529,1... | collective-permute-start | bytes 43016 | tf_op jit(solution)/shard_map/ppermute | solution.py:31
  94.3 9.6 %collective-permute-start.4 = (bf16[8,896]{1,0:T(8,128)(2,1)S(1)}, bf16[8,896]{1,0:T(8,128)(2,1)S(1)}, u32[]{:S(2)}, u32[]{:S(2)}) collective-permute-start(bf16[8,896]{1,0:T(8,128)(2,1)S(1)} %convert_element_type.45), channel_id=1, source_target_pairs={{0,512},{512,0},{1,513},{513,1},{2,514},{514,2},{3,515},{515,3},{4... | collective-permute-start | bytes 43016 | tf_op jit(solution)/shard_map/ppermute | solution.py:31
  98.5 5.4 %collective-permute-start.3 = (bf16[8,896]{1,0:T(8,128)(2,1)S(1)}, bf16[8,896]{1,0:T(8,128)(2,1)S(1)}, u32[]{:S(2)}, u32[]{:S(2)}) collective-permute-start(bf16[8,896]{1,0:T(8,128)(2,1)S(1)} %convert_element_type.45), channel_id=1, source_target_pairs={{0,16},{16,0},{1,17},{17,1},{2,18},{18,2},{3,19},{19,3},{4,20},{20... | collective-permute-start | bytes 43016 | tf_op jit(solution)/shard_map/ppermute | solution.py:31
  108.5 6.7 %copy-start = (bf16[128,512]{1,0:T(8,128)(2,1)S(1)}, bf16[128,512]{1,0:T(8,128)(2,1)}, u32[]{:S(2)}) copy-start(bf16[128,512]{1,0:T(8,128)(2,1)} %param.5) | copy-start | bytes 393220
  108.5 12.3 %all-to-all-start.4 = ((bf16[16,8,544]{2,1,0:T(8,128)(2,1)}), bf16[16,8,544]{2,1,0:T(8,128)(2,1)S(1)}, u32[]{:S(2)}, u32[]{:S(2)}) async-start(bf16[16,8,544]{2,1,0:T(8,128)(2,1)} %maximum_bitcast_fusion), calls=%async_computation.4 | async-start | bytes 327680 | tf_op jit(solution)/shard_map/all_to_all | solution.py:14
  115.2 12.7 %collective-permute-start.6 = (bf16[128,512]{1,0:T(8,128)(2,1)S(1)}, bf16[128,512]{1,0:T(8,128)(2,1)S(1)}, u32[]{:S(2)}, u32[]{:S(2)}) collective-permute-start(bf16[128,512]{1,0:T(8,128)(2,1)S(1)} %copy-done), channel_id=1, source_target_pairs={{0,16},{16,0},{1,17},{17,1},{2,18},{18,2},{3,19},{19,3},{4,20},{20... | collective-permute-start | bytes 393224 | tf_op jit(solution)/shard_map/ppermute | solution.py:31
  121.5 12.0 %all-to-all-start.5 = ((bf16[16,8,544]{2,1,0:T(8,128)(2,1)}), bf16[16,8,544]{2,1,0:T(8,128)(2,1)S(1)}, u32[]{:S(2)}, u32[]{:S(2)}) async-start(bf16[16,8,544]{2,1,0:T(8,128)(2,1)} %broadcast_in_dim.11), calls=%async_computation.5 | async-start | bytes 327680 | tf_op jit(solution)/shard_map/all_to_all | solution.py:14
  127.9 17.9 %collective-permute-start.7 = (bf16[256,512]{1,0:T(8,128)(2,1)S(1)}, bf16[256,512]{1,0:T(8,128)(2,1)S(1)}, u32[]{:S(2)}, u32[]{:S(2)}) collective-permute-start(bf16[256,512]{1,0:T(8,128)(2,1)S(1)} %pad_maximum_fusion.1), channel_id=1, source_target_pairs={{0,512},{512,0},{1,513},{513,1},{2,514},{514,2},{3,515},{515,3},{4... | collective-permute-start | bytes 786440 | tf_op jit(solution)/shard_map/ppermute | solution.py:31

commit v8 on v7

v8 whole, which is shorter than its diff:
```python
import jax
import jax.numpy as jnp
from jax import lax
from jax.sharding import Mesh, PartitionSpec as P

D = 8192
TOKENS = 8192
DP = ("yh", "z", "c")
TENSOR = ("x", "yl")
OWN = 8


def swap(pieces, axes):
    return lax.all_to_all(pieces, axes, split_axis=0, concat_axis=0, tiled=True)


def to_all(x, axes, count):
    return swap(jnp.broadcast_to(x, (count, *x.shape)), axes)


def total(pieces):
    return jnp.sum(pieces.astype(jnp.float32), axis=0)


def dot(left, right, dims):
    return lax.dot_general(left, right, (dims, ((), ())), preferred_element_type=jnp.float32)


def across(x, *axes):
    last = 2 ** len(axes) - 1
    return lax.ppermute(x, axes, [(i, last - i) for i in range(last + 1)])


def from_own(x, axes):
    for dim, axis in enumerate(axes):
        x = jnp.where(lax.axis_index(axis) == 0, x, jnp.flip(x, dim))
    return x


def step(acts, grad_out, proj_t, first_moment, second_moment):
    bf16 = jnp.bfloat16
    root = jnp.sqrt(jnp.float32(D))
    grad_yh = across(grad_out, "yh")
    grad_c = across(grad_out, "c")
    grad_d = across(grad_yh, "c")
    grad_all = jnp.stack([grad_out, grad_c, grad_yh, grad_d]).reshape(2, 2, 128, -1)
    moment_base = 0.9 * first_moment
    own_rows = lax.dynamic_slice_in_dim(proj_t, lax.axis_index(DP) * OWN, OWN, 0)
    own_rows = own_rows.astype(jnp.float32)
    part = (dot(proj_t, acts, ((1,), (1,))) * (1.0 / root)).astype(bf16)
    got = swap(part.reshape(64, OWN, 128), ("yh", "x", "yl", "c"))
    got, moment_base = lax.optimization_barrier((got, moment_base))
    part = jnp.sum(got.reshape(2, 16, 2, OWN, 128).astype(jnp.float32), axis=1)
    part = from_own(part, ("yh", "c")).astype(bf16)
    coords = to_all(part, TENSOR, 16).transpose(1, 2, 0, 3, 4)
    grad_part = (dot(coords, grad_all, ((0, 1, 4), (0, 1, 2))) / TOKENS).astype(bf16)
    got = swap(grad_part.reshape(16, OWN, -1), "z")
    coords_yh = across(coords[1, 0], "yh")
    coords_d = across(coords[1, 1], "yh", "c")
    coords_c = across(coords[0, 1], "c")
    mine = jnp.stack([coords[0, 0], coords_c, coords_yh, coords_d])
    mine = from_own(mine.reshape(2, 2, 16, OWN, 128), ("yh", "c"))
    mine = mine.transpose(0, 2, 1, 3, 4).reshape(512, 128)
    residual = (root * acts - dot(mine, proj_t, ((0,), (0,)))).astype(bf16)
    residual_yh = across(residual, "yh")
    residual_c = across(residual, "c")
    residual_d = across(residual_yh, "c")
    residual_all = jnp.concatenate([residual, residual_c, residual_yh, residual_d])
    got, own_rows = lax.optimization_barrier((got, own_rows))
    grad_own = total(got)
    low_own = grad_own.astype(bf16)
    low_own, grad_own = lax.optimization_barrier((low_own, grad_own))
    moment_one = moment_base + 0.1 * grad_own
    moment_two = 0.999 * second_moment + 0.001 * grad_own * grad_own
    root_two = jnp.sqrt(moment_two / (1.0 - 0.999**10)) + 1e-08
    adam_step = moment_one / (1.0 - 0.9**10) / root_two
    low = to_all(low_own, "z", 16).reshape(128, -1)
    low, residual_all, adam_step = lax.optimization_barrier((low, residual_all, adam_step))
    back = dot(low, grad_all.reshape(512, -1), ((1,), (1,))).astype(bf16)
    back = total(swap(back.reshape(16, OWN, -1), TENSOR)).astype(bf16)
    back = to_all(back, TENSOR, 16).reshape(128, -1)
    pull = (dot(back, residual_all, ((1,), (0,))) / TOKENS).astype(bf16)
    moved = total(swap(pull.reshape(16, OWN, -1), "z"))
    return (adam_step, own_rows + moved)


def solution(mesh):
    fine = Mesh(mesh.devices.reshape(2, 16, 2, 4, 4), DP + TENSOR)
    whole = P(DP, TENSOR)
    placed = (whole, whole, P(None, TENSOR), whole, whole)
    return jax.shard_map(
        step, mesh=fine, in_specs=placed, out_specs=(whole, whole), check_vma=False
    )
```

time: 172 us -> 164 us (0.953)
  the two profiles are of different devices: /device:TPU:18 before, /device:TPU:8 now
where the time goes in v8:
time: 164 us; the launch traced here: 163 us
  starting transfers between devices  76 us (46%)
  blocking collectives  47.7 us (29%)
  waiting for transfers between devices  31.6 us (19%)
  matrix products  3.91 us (2%)
  other arithmetic  1.66 us (1%)
    all_to_all x3, blocking collectives, swap(): return lax.all_to_all(pieces, axes, split_axis=0, concat_axis=0, tiled=True)  47.7 us
    all_to_all x4, starting transfers between devices, swap(): return lax.all_to_all(pieces, axes, split_axis=0, concat_axis=0, tiled=True)  45.6 us
    ppermute x9, starting transfers between devices, across(): return lax.ppermute(x, axes, [(i, last - i) for i in range(last + 1)])  30.4 us
    ppermute x9, waiting for transfers between devices, across(): return lax.ppermute(x, axes, [(i, last - i) for i in range(last + 1)])  21.4 us
    all_to_all x4, waiting for transfers between devices, swap(): return lax.all_to_all(pieces, axes, split_axis=0, concat_axis=0, tiled=True)  10.2 us
    dot_general x5, matrix products, dot(): lax.dot_general(left, right, (dims, ((), ())), preferred_element_type=jnp...  3.91 us
  transfers between devices with their start and end apart: 13, of which 6 were waited for; matrix products, arithmetic and copies ran while one was open for 1% of the time, Pallas kernels for 0%

profile of v8, /device:TPU:8, one launch (start us, length us, event | category | flops | bytes accessed | tf_op | source)
XLA Modules:
  0.0 163.1 jit_solution(15393722006081744266)
XLA Ops:
  0.6 2.0 %fusion.6 = bf16[64,8,128]{2,1,0:T(8,128)(2,1)} fusion(bf16[512,512]{1,0:T(8,128)(2,1)} %param.7, bf16[128,512]{1,0:T(8,128)(2,1)} %param.5), kind=kOutput, calls=%fused_computation.11 | convolution fusion | flops 67239936 | bytes 786432 | tf_op jit(solution)/shard_map/dot_general | solution.py:26
  2.6 0.0 copy-start.2
  2.6 0.0 copy-start.4
  2.6 17.2 %all-to-all-start = ((bf16[64,8,128]{2,1,0:T(8,128)(2,1)}), bf16[64,8,128]{2,1,0:T(8,128)(2,1)S(1)}, u32[]{:S(2)}, u32[]{:S(2)}) async-start(bf16[64,8,128]{2,1,0:T(8,128)(2,1)} %fusion.6), calls=%async_computation | async-start | bytes 262144 | tf_op jit(solution)/shard_map/all_to_all | solution.py:14
  19.9 0.0 copy-done.2
  19.9 6.6 %collective-permute-start.1 = (bf16[128,896]{1,0:T(8,128)(2,1)S(1)}, bf16[128,896]{1,0:T(8,128)(2,1)S(1)}, u32[]{:S(2)}, u32[]{:S(2)}) collective-permute-start(bf16[128,896]{1,0:T(8,128)(2,1)S(1)} %copy-done.2), channel_id=1, source_target_pairs={{0,512},{512,0},{1,513},{513,1},{2,514},{514,2},{3,515},{515,3},{4... | collective-permute-start | bytes 688136 | tf_op jit(solution)/shard_map/ppermute | solution.py:31
  26.5 1.9 %collective-permute-start = (bf16[128,896]{1,0:T(8,128)(2,1)S(1)}, bf16[128,896]{1,0:T(8,128)(2,1)S(1)}, u32[]{:S(2)}, u32[]{:S(2)}) collective-permute-start(bf16[128,896]{1,0:T(8,128)(2,1)S(1)} %copy-done.2), channel_id=1, source_target_pairs={{0,16},{16,0},{1,17},{17,1},{2,18},{18,2},{3,19},{19,3},{4,20},{20... | collective-permute-start | bytes 688136 | tf_op jit(solution)/shard_map/ppermute | solution.py:31
  28.4 0.0 copy-done.4
  28.5 9.8 %collective-permute-done.1 = bf16[128,896]{1,0:T(8,128)(2,1)S(1)} collective-permute-done((bf16[128,896]{1,0:T(8,128)(2,1)S(1)}, bf16[128,896]{1,0:T(8,128)(2,1)S(1)}, u32[]{:S(2)}, u32[]{:S(2)}) %collective-permute-start.1) | collective-permute-done | bytes 229408 | tf_op jit(solution)/shard_map/ppermute | solution.py:31
  38.2 1.9 %collective-permute-start.2 = (bf16[128,896]{1,0:T(8,128)(2,1)S(1)}, bf16[128,896]{1,0:T(8,128)(2,1)S(1)}, u32[]{:S(2)}, u32[]{:S(2)}) collective-permute-start(bf16[128,896]{1,0:T(8,128)(2,1)S(1)} %collective-permute-done.1), channel_id=1, source_target_pairs={{0,16},{16,0},{1,17},{17,1},{2,18},{18,2},{3,19},{19,3},{4,20},{20... | collective-permute-start | bytes 688136 | tf_op jit(solution)/shard_map/ppermute | solution.py:31
  40.1 0.0 all-to-all-done
  40.2 0.7 broadcast_in_dim.9
  40.9 6.9 %all-to-all-start.1 = ((bf16[16,2,2,8,128]{4,3,2,1,0:T(8,128)(2,1)}), bf16[16,2,2,8,128]{4,3,2,1,0:T(8,128)(2,1)S(1)}, u32[]{:S(2)}, u32[]{:S(2)}) async-start(bf16[16,2,2,8,128]{4,3,2,1,0:T(8,128)(2,1)} %broadcast_in_dim.9), calls=%async_computation.1 | async-start | bytes 262144 | tf_op jit(solution)/shard_map/all_to_all | solution.py:14
  47.8 0.0 collective-permute-done
  47.8 0.0 collective-permute-done.2
  47.8 0.1 pad_maximum_fusion
  47.9 7.4 %all-to-all-done.1 = bf16[16,2,2,8,128]{4,3,2,1,0:T(8,128)(2,1)S(1)} async-done(((bf16[16,2,2,8,128]{4,3,2,1,0:T(8,128)(2,1)}), bf16[16,2,2,8,128]{4,3,2,1,0:T(8,128)(2,1)S(1)}, u32[]{:S(2)}, u32[]{:S(2)}) %all-to-all-start.1) | async-done | bytes 131104 | tf_op jit(solution)/shard_map/all_to_all | solution.py:14
  55.3 1.0 fusion.1
  56.3 0.0 copy-start
  56.3 12.4 %all-to-all-start.2 = ((bf16[16,8,896]{2,1,0:T(8,128)(2,1)}), bf16[16,8,896]{2,1,0:T(8,128)(2,1)S(1)}, u32[]{:S(2)}, u32[]{:S(2)}) async-start(bf16[16,8,896]{2,1,0:T(8,128)(2,1)} %fusion.1), calls=%async_computation.2 | async-start | bytes 458752 | tf_op jit(solution)/shard_map/all_to_all | solution.py:14
  68.7 4.2 %collective-permute-start.5 = (bf16[16,8,128]{2,1,0:T(8,128)(2,1)S(1)}, bf16[16,8,128]{2,1,0:T(8,128)(2,1)S(1)}, u32[]{:S(2)}, u32[]{:S(2)}) collective-permute-start(bf16[16,8,128]{2,1,0:T(8,128)(2,1)S(1)} %get-tuple-element.21), channel_id=1, source_target_pairs={{0,528},{16,512},{512,16},{528,0},{1,529},{17,513},{513,17},{529,1... | collective-permute-start | bytes 98312 | tf_op jit(solution)/shard_map/ppermute | solution.py:31
  73.0 4.2 %collective-permute-start.4 = (bf16[16,8,128]{2,1,0:T(8,128)(2,1)S(1)}, bf16[16,8,128]{2,1,0:T(8,128)(2,1)S(1)}, u32[]{:S(2)}, u32[]{:S(2)}) collective-permute-start(bf16[16,8,128]{2,1,0:T(8,128)(2,1)S(1)} %get-tuple-element.22), channel_id=1, source_target_pairs={{0,512},{512,0},{1,513},{513,1},{2,514},{514,2},{3,515},{515,3},{4... | collective-permute-start | bytes 98312 | tf_op jit(solution)/shard_map/ppermute | solution.py:31
  77.2 3.1 %collective-permute-start.3 = (bf16[16,8,128]{2,1,0:T(8,128)(2,1)S(1)}, bf16[16,8,128]{2,1,0:T(8,128)(2,1)S(1)}, u32[]{:S(2)}, u32[]{:S(2)}) collective-permute-start(bf16[16,8,128]{2,1,0:T(8,128)(2,1)S(1)} %get-tuple-element.23), channel_id=1, source_target_pairs={{0,16},{16,0},{1,17},{17,1},{2,18},{18,2},{3,19},{19,3},{4,20},{20... | collective-permute-start | bytes 98312 | tf_op jit(solution)/shard_map/ppermute | solution.py:31
  80.2 0.0 copy-done
  80.3 0.0 collective-permute-done.5
  80.3 2.4 %collective-permute-done.4 = bf16[16,8,128]{2,1,0:T(8,128)(2,1)S(1)} collective-permute-done((bf16[16,8,128]{2,1,0:T(8,128)(2,1)S(1)}, bf16[16,8,128]{2,1,0:T(8,128)(2,1)S(1)}, u32[]{:S(2)}, u32[]{:S(2)}) %collective-permute-start.4) | collective-permute-done | bytes 32800 | tf_op jit(solution)/shard_map/ppermute | solution.py:31
  82.7 0.0 collective-permute-done.3
  82.8 2.8 %all-to-all-done.2 = bf16[16,8,896]{2,1,0:T(8,128)(2,1)S(1)} async-done(((bf16[16,8,896]{2,1,0:T(8,128)(2,1)}), bf16[16,8,896]{2,1,0:T(8,128)(2,1)S(1)}, u32[]{:S(2)}, u32[]{:S(2)}) %all-to-all-start.2) | async-done | bytes 229408 | tf_op jit(solution)/shard_map/all_to_all | solution.py:14
  85.7 0.7 broadcast_in_dim.10
  86.4 9.1 %all-to-all-start.3 = ((bf16[16,8,896]{2,1,0:T(8,128)(2,1)}), bf16[16,8,896]{2,1,0:T(8,128)(2,1)S(1)}, u32[]{:S(2)}, u32[]{:S(2)}) async-start(bf16[16,8,896]{2,1,0:T(8,128)(2,1)} %broadcast_in_dim.10), calls=%async_computation.3 | async-start | bytes 458752 | tf_op jit(solution)/shard_map/all_to_all | solution.py:14
  95.5 0.0 copy-done.1
  95.5 0.3 fusion.3
  95.7 0.0 copy-start.3
  95.8 4.2 %collective-permute-start.7 = (bf16[128,512]{1,0:T(8,128)(2,1)S(1)}, bf16[128,512]{1,0:T(8,128)(2,1)S(1)}, u32[]{:S(2)}, u32[]{:S(2)}) collective-permute-start(bf16[128,512]{1,0:T(8,128)(2,1)S(1)} %fusion.3), channel_id=1, source_target_pairs={{0,512},{512,0},{1,513},{513,1},{2,514},{514,2},{3,515},{515,3},{4... | collective-permute-start | bytes 393224 | tf_op jit(solution)/shard_map/ppermute | solution.py:31
  100.0 2.2 %collective-permute-start.6 = (bf16[128,512]{1,0:T(8,128)(2,1)S(1)}, bf16[128,512]{1,0:T(8,128)(2,1)S(1)}, u32[]{:S(2)}, u32[]{:S(2)}) collective-permute-start(bf16[128,512]{1,0:T(8,128)(2,1)S(1)} %fusion.3), channel_id=1, source_target_pairs={{0,16},{16,0},{1,17},{17,1},{2,18},{18,2},{3,19},{19,3},{4,20},{20... | collective-permute-start | bytes 393224 | tf_op jit(solution)/shard_map/ppermute | solution.py:31
  102.2 7.9 %collective-permute-done.7 = bf16[128,512]{1,0:T(8,128)(2,1)S(1)} collective-permute-done((bf16[128,512]{1,0:T(8,128)(2,1)S(1)}, bf16[128,512]{1,0:T(8,128)(2,1)S(1)}, u32[]{:S(2)}, u32[]{:S(2)}) %collective-permute-start.7) | collective-permute-done | bytes 131104 | tf_op jit(solution)/shard_map/ppermute | solution.py:31
  110.2 2.0 %collective-permute-start.8 = (bf16[128,512]{1,0:T(8,128)(2,1)S(1)}, bf16[128,512]{1,0:T(8,128)(2,1)S(1)}, u32[]{:S(2)}, u32[]{:S(2)}) collective-permute-start(bf16[128,512]{1,0:T(8,128)(2,1)S(1)} %collective-permute-done.7), channel_id=1, source_target_pairs={{0,16},{16,0},{1,17},{17,1},{2,18},{18,2},{3,19},{19,3},{4,20},{20... | collective-permute-start | bytes 393224 | tf_op jit(solution)/shard_map/ppermute | solution.py:31
  112.2 0.0 collective-permute-done.6
  112.2 1.2 collective-permute-done.8
  113.5 0.0 copy-done.3
  113.5 0.6 fusion.13
  114.1 0.0 all-to-all-done.3
  114.1 0.4 fusion.7
  114.6 11.3 %all_to_all.35 = bf16[16,8,512]{2,1,0:T(8,128)(2,1)S(1)} all-to-all(bf16[16,8,512]{2,1,0:T(8,128)(2,1)S(1)} %fusion.7), channel_id=1, replica_groups=mesh['yh'=2,'z'=16,'c'=2,'x'=4,'yl'=4] {'x','yl'}, dimensions={0} | all-to-all | bytes 262144 | tf_op jit(solution)/shard_map/all_to_all | solution.py:14
  125.9 11.4 %all_to_all.36 = bf16[16,8,512]{2,1,0:T(8,128)(2,1)S(1)} all-to-all(bf16[16,8,512]{2,1,0:T(8,128)(2,1)S(1)} %broadcast_in_dim.11), channel_id=1, replica_groups=mesh['yh'=2,'z'=16,'c'=2,'x'=4,'yl'=4] {'x','yl'}, dimensions={0} | all-to-all | bytes 262144 | tf_op jit(solution)/shard_map/all_to_all | solution.py:14
  137.3 0.2 fusion.5
  137.5 25.0 %all_to_all.37 = bf16[16,8,512]{2,1,0:T(8,128)(2,1)S(1)} all-to-all(bf16[16,8,512]{2,1,0:T(8,128)(2,1)S(1)} %fusion.5), channel_id=1, replica_groups=mesh['yh'=2,'z'=16,'c'=2,'x'=4,'yl'=4] {'z'}, dimensions={0} | all-to-all | bytes 262144 | tf_op jit(solution)/shard_map/all_to_all | solution.py:14
  162.5 0.6 add.31
  (17 shorter events, 0.3 us)
Async XLA Ops:
  2.6 17.3 %copy-start.2 = (bf16[128,896]{1,0:T(8,128)(2,1)S(1)}, bf16[128,896]{1,0:T(8,128)(2,1)}, u32[]{:S(2)}) copy-start(bf16[128,896]{1,0:T(8,128)(2,1)} %param.6) | copy-start | bytes 688132
  2.6 25.8 %copy-start.4 = (f32[8,896]{1,0:T(8,128)S(1)}, f32[8,896]{1,0:T(8,128)}, u32[]{:S(2)}) copy-start(f32[8,896]{1,0:T(8,128)} %param.8) | copy-start | bytes 86020
  2.6 37.5 %all-to-all-start = ((bf16[64,8,128]{2,1,0:T(8,128)(2,1)}), bf16[64,8,128]{2,1,0:T(8,128)(2,1)S(1)}, u32[]{:S(2)}, u32[]{:S(2)}) async-start(bf16[64,8,128]{2,1,0:T(8,128)(2,1)} %fusion.6), calls=%async_computation | async-start | bytes 262144 | tf_op jit(solution)/shard_map/all_to_all | solution.py:14
  19.9 18.3 %collective-permute-start.1 = (bf16[128,896]{1,0:T(8,128)(2,1)S(1)}, bf16[128,896]{1,0:T(8,128)(2,1)S(1)}, u32[]{:S(2)}, u32[]{:S(2)}) collective-permute-start(bf16[128,896]{1,0:T(8,128)(2,1)S(1)} %copy-done.2), channel_id=1, source_target_pairs={{0,512},{512,0},{1,513},{513,1},{2,514},{514,2},{3,515},{515,3},{4... | collective-permute-start | bytes 688136 | tf_op jit(solution)/shard_map/ppermute | solution.py:31
  26.5 21.3 %collective-permute-start = (bf16[128,896]{1,0:T(8,128)(2,1)S(1)}, bf16[128,896]{1,0:T(8,128)(2,1)S(1)}, u32[]{:S(2)}, u32[]{:S(2)}) collective-permute-start(bf16[128,896]{1,0:T(8,128)(2,1)S(1)} %copy-done.2), channel_id=1, source_target_pairs={{0,16},{16,0},{1,17},{17,1},{2,18},{18,2},{3,19},{19,3},{4,20},{20... | collective-permute-start | bytes 688136 | tf_op jit(solution)/shard_map/ppermute | solution.py:31
  38.2 9.5 %collective-permute-start.2 = (bf16[128,896]{1,0:T(8,128)(2,1)S(1)}, bf16[128,896]{1,0:T(8,128)(2,1)S(1)}, u32[]{:S(2)}, u32[]{:S(2)}) collective-permute-start(bf16[128,896]{1,0:T(8,128)(2,1)S(1)} %collective-permute-done.1), channel_id=1, source_target_pairs={{0,16},{16,0},{1,17},{17,1},{2,18},{18,2},{3,19},{19,3},{4,20},{20... | collective-permute-start | bytes 688136 | tf_op jit(solution)/shard_map/ppermute | solution.py:31
  40.9 14.5 %all-to-all-start.1 = ((bf16[16,2,2,8,128]{4,3,2,1,0:T(8,128)(2,1)}), bf16[16,2,2,8,128]{4,3,2,1,0:T(8,128)(2,1)S(1)}, u32[]{:S(2)}, u32[]{:S(2)}) async-start(bf16[16,2,2,8,128]{4,3,2,1,0:T(8,128)(2,1)} %broadcast_in_dim.9), calls=%async_computation.1 | async-start | bytes 262144 | tf_op jit(solution)/shard_map/all_to_all | solution.py:14
  56.3 23.9 %copy-start = (bf16[512,512]{1,0:T(8,128)(2,1)S(1)}, bf16[512,512]{1,0:T(8,128)(2,1)}, u32[]{:S(2)}) copy-start(bf16[512,512]{1,0:T(8,128)(2,1)} %param.7) | copy-start | bytes 1572868
  56.3 29.3 %all-to-all-start.2 = ((bf16[16,8,896]{2,1,0:T(8,128)(2,1)}), bf16[16,8,896]{2,1,0:T(8,128)(2,1)S(1)}, u32[]{:S(2)}, u32[]{:S(2)}) async-start(bf16[16,8,896]{2,1,0:T(8,128)(2,1)} %fusion.1), calls=%async_computation.2 | async-start | bytes 458752 | tf_op jit(solution)/shard_map/all_to_all | solution.py:14
  68.7 11.6 %collective-permute-start.5 = (bf16[16,8,128]{2,1,0:T(8,128)(2,1)S(1)}, bf16[16,8,128]{2,1,0:T(8,128)(2,1)S(1)}, u32[]{:S(2)}, u32[]{:S(2)}) collective-permute-start(bf16[16,8,128]{2,1,0:T(8,128)(2,1)S(1)} %get-tuple-element.21), channel_id=1, source_target_pairs={{0,528},{16,512},{512,16},{528,0},{1,529},{17,513},{513,17},{529,1... | collective-permute-start | bytes 98312 | tf_op jit(solution)/shard_map/ppermute | solution.py:31
  73.0 9.7 %collective-permute-start.4 = (bf16[16,8,128]{2,1,0:T(8,128)(2,1)S(1)}, bf16[16,8,128]{2,1,0:T(8,128)(2,1)S(1)}, u32[]{:S(2)}, u32[]{:S(2)}) collective-permute-start(bf16[16,8,128]{2,1,0:T(8,128)(2,1)S(1)} %get-tuple-element.22), channel_id=1, source_target_pairs={{0,512},{512,0},{1,513},{513,1},{2,514},{514,2},{3,515},{515,3},{4... | collective-permute-start | bytes 98312 | tf_op jit(solution)/shard_map/ppermute | solution.py:31
  77.2 5.5 %collective-permute-start.3 = (bf16[16,8,128]{2,1,0:T(8,128)(2,1)S(1)}, bf16[16,8,128]{2,1,0:T(8,128)(2,1)S(1)}, u32[]{:S(2)}, u32[]{:S(2)}) collective-permute-start(bf16[16,8,128]{2,1,0:T(8,128)(2,1)S(1)} %get-tuple-element.23), channel_id=1, source_target_pairs={{0,16},{16,0},{1,17},{17,1},{2,18},{18,2},{3,19},{19,3},{4,20},{20... | collective-permute-start | bytes 98312 | tf_op jit(solution)/shard_map/ppermute | solution.py:31
  86.4 9.1 %copy-start.1 = (bf16[128,512]{1,0:T(8,128)(2,1)S(1)}, bf16[128,512]{1,0:T(8,128)(2,1)}, u32[]{:S(2)}) copy-start(bf16[128,512]{1,0:T(8,128)(2,1)} %param.5) | copy-start | bytes 393220
  86.4 27.7 %all-to-all-start.3 = ((bf16[16,8,896]{2,1,0:T(8,128)(2,1)}), bf16[16,8,896]{2,1,0:T(8,128)(2,1)S(1)}, u32[]{:S(2)}, u32[]{:S(2)}) async-start(bf16[16,8,896]{2,1,0:T(8,128)(2,1)} %broadcast_in_dim.10), calls=%async_computation.3 | async-start | bytes 458752 | tf_op jit(solution)/shard_map/all_to_all | solution.py:14
  95.7 17.7 %copy-start.3 = (f32[8,896]{1,0:T(8,128)S(1)}, f32[8,896]{1,0:T(8,128)}, u32[]{:S(2)}) copy-start(f32[8,896]{1,0:T(8,128)} %param.9) | copy-start | bytes 86020
  95.8 14.4 %collective-permute-start.7 = (bf16[128,512]{1,0:T(8,128)(2,1)S(1)}, bf16[128,512]{1,0:T(8,128)(2,1)S(1)}, u32[]{:S(2)}, u32[]{:S(2)}) collective-permute-start(bf16[128,512]{1,0:T(8,128)(2,1)S(1)} %fusion.3), channel_id=1, source_target_pairs={{0,512},{512,0},{1,513},{513,1},{2,514},{514,2},{3,515},{515,3},{4... | collective-permute-start | bytes 393224 | tf_op jit(solution)/shard_map/ppermute | solution.py:31
  100.0 12.2 %collective-permute-start.6 = (bf16[128,512]{1,0:T(8,128)(2,1)S(1)}, bf16[128,512]{1,0:T(8,128)(2,1)S(1)}, u32[]{:S(2)}, u32[]{:S(2)}) collective-permute-start(bf16[128,512]{1,0:T(8,128)(2,1)S(1)} %fusion.3), channel_id=1, source_target_pairs={{0,16},{16,0},{1,17},{17,1},{2,18},{18,2},{3,19},{19,3},{4,20},{20... | collective-permute-start | bytes 393224 | tf_op jit(solution)/shard_map/ppermute | solution.py:31
  110.2 3.2 %collective-permute-start.8 = (bf16[128,512]{1,0:T(8,128)(2,1)S(1)}, bf16[128,512]{1,0:T(8,128)(2,1)S(1)}, u32[]{:S(2)}, u32[]{:S(2)}) collective-permute-start(bf16[128,512]{1,0:T(8,128)(2,1)S(1)} %collective-permute-done.7), channel_id=1, source_target_pairs={{0,16},{16,0},{1,17},{17,1},{2,18},{18,2},{3,19},{19,3},{4,20},{20... | collective-permute-start | bytes 393224 | tf_op jit(solution)/shard_map/ppermute | solution.py:31

commit v9 on v8

--- a/solution.py
+++ b/solution.py
@@ -64,9 +64,8 @@
     residual = (root * acts - dot(mine, proj_t, ((0,), (0,)))).astype(bf16)
     residual_yh = across(residual, "yh")
     residual_c = across(residual, "c")
-    residual_d = across(residual_yh, "c")
-    residual_all = jnp.concatenate([residual, residual_c, residual_yh, residual_d])
-    got, own_rows = lax.optimization_barrier((got, own_rows))
+    residual_d = across(residual, "yh", "c")
+    residual_here = jnp.concatenate([residual, residual_c])
     grad_own = total(got)
     low_own = grad_own.astype(bf16)
     low_own, grad_own = lax.optimization_barrier((low_own, grad_own))
@@ -75,12 +74,16 @@
     root_two = jnp.sqrt(moment_two / (1.0 - 0.999**10)) + 1e-08
     adam_step = moment_one / (1.0 - 0.9**10) / root_two
     low = to_all(low_own, "z", 16).reshape(128, -1)
-    low, residual_all, adam_step = lax.optimization_barrier((low, residual_all, adam_step))
+    low, residual_here, own_rows, adam_step = lax.optimization_barrier(
+        (low, residual_here, own_rows, adam_step)
+    )
     back = dot(low, grad_all.reshape(512, -1), ((1,), (1,))).astype(bf16)
     back = total(swap(back.reshape(16, OWN, -1), TENSOR)).astype(bf16)
     back = to_all(back, TENSOR, 16).reshape(128, -1)
-    pull = (dot(back, residual_all, ((1,), (0,))) / TOKENS).astype(bf16)
-    moved = total(swap(pull.reshape(16, OWN, -1), "z"))
+    pull = dot(back[:, 256:384], residual_yh, ((1,), (0,)))
+    pull = pull + dot(back[:, 384:], residual_d, ((1,), (0,)))
+    pull = (pull + dot(back[:, :256], residual_here, ((1,), (0,)))) / TOKENS
+    moved = total(swap(pull.astype(bf16).reshape(16, OWN, -1), "z"))
     return (adam_step, own_rows + moved)
 
 

time: 164 us -> 172 us (1.049)
  the two profiles are of different devices: /device:TPU:8 before, /device:TPU:6 now
where the time goes in v9:
time: 172 us; the launch traced here: 171 us
  starting transfers between devices  84.9 us (49%)
  waiting for transfers between devices  41.5 us (24%)
  blocking collectives  34.8 us (20%)
  matrix products  4.22 us (2%)
  local copies, waits for them, and re-layouts  2.96 us (2%)
    all_to_all x5, starting transfers between devices, swap(): return lax.all_to_all(pieces, axes, split_axis=0, concat_axis=0, tiled=True)  52.6 us
    all_to_all x2, blocking collectives, swap(): return lax.all_to_all(pieces, axes, split_axis=0, concat_axis=0, tiled=True)  34.8 us
    ppermute x9, starting transfers between devices, across(): return lax.ppermute(x, axes, [(i, last - i) for i in range(last + 1)])  32.3 us
    ppermute x9, waiting for transfers between devices, across(): return lax.ppermute(x, axes, [(i, last - i) for i in range(last + 1)])  21.6 us
    all_to_all x5, waiting for transfers between devices, swap(): return lax.all_to_all(pieces, axes, split_axis=0, concat_axis=0, tiled=True)  19.9 us
    dot_general x7, matrix products, dot(): lax.dot_general(left, right, (dims, ((), ())), preferred_element_type=jnp...  4.22 us
  transfers between devices with their start and end apart: 14, of which 8 were waited for; matrix products, arithmetic and copies ran while one was open for 1% of the time, Pallas kernels for 0%

profile of v9, /device:TPU:6, one launch (start us, length us, event | category | flops | bytes accessed | tf_op | source)
XLA Modules:
  0.0 171.1 jit_solution(11515216082588983832)
XLA Ops:
  0.6 2.0 %fusion.8 = bf16[64,8,128]{2,1,0:T(8,128)(2,1)} fusion(bf16[512,512]{1,0:T(8,128)(2,1)} %param.7, bf16[128,512]{1,0:T(8,128)(2,1)} %param.5), kind=kOutput, calls=%fused_computation.13 | convolution fusion | flops 67239936 | bytes 786432 | tf_op jit(solution)/shard_map/dot_general | solution.py:26
  2.6 17.4 %all-to-all-start = ((bf16[64,8,128]{2,1,0:T(8,128)(2,1)}), bf16[64,8,128]{2,1,0:T(8,128)(2,1)S(1)}, u32[]{:S(2)}, u32[]{:S(2)}) async-start(bf16[64,8,128]{2,1,0:T(8,128)(2,1)} %fusion.8), calls=%async_computation | async-start | bytes 262144 | tf_op jit(solution)/shard_map/all_to_all | solution.py:14
  20.1 7.5 %collective-permute-start.1 = (bf16[128,896]{1,0:T(8,128)(2,1)S(1)}, bf16[128,896]{1,0:T(8,128)(2,1)S(1)}, u32[]{:S(2)}, u32[]{:S(2)}) collective-permute-start(bf16[128,896]{1,0:T(8,128)(2,1)S(1)} %copy-done.2), channel_id=1, source_target_pairs={{0,512},{512,0},{1,513},{513,1},{2,514},{514,2},{3,515},{515,3},{4... | collective-permute-start | bytes 688136 | tf_op jit(solution)/shard_map/ppermute | solution.py:31
  27.6 1.9 %collective-permute-start = (bf16[128,896]{1,0:T(8,128)(2,1)S(1)}, bf16[128,896]{1,0:T(8,128)(2,1)S(1)}, u32[]{:S(2)}, u32[]{:S(2)}) collective-permute-start(bf16[128,896]{1,0:T(8,128)(2,1)S(1)} %copy-done.2), channel_id=1, source_target_pairs={{0,16},{16,0},{1,17},{17,1},{2,18},{18,2},{3,19},{19,3},{4,20},{20... | collective-permute-start | bytes 688136 | tf_op jit(solution)/shard_map/ppermute | solution.py:31
  29.5 6.7 %collective-permute-done.1 = bf16[128,896]{1,0:T(8,128)(2,1)S(1)} collective-permute-done((bf16[128,896]{1,0:T(8,128)(2,1)S(1)}, bf16[128,896]{1,0:T(8,128)(2,1)S(1)}, u32[]{:S(2)}, u32[]{:S(2)}) %collective-permute-start.1) | collective-permute-done | bytes 229408 | tf_op jit(solution)/shard_map/ppermute | solution.py:31
  36.2 1.9 %collective-permute-start.2 = (bf16[128,896]{1,0:T(8,128)(2,1)S(1)}, bf16[128,896]{1,0:T(8,128)(2,1)S(1)}, u32[]{:S(2)}, u32[]{:S(2)}) collective-permute-start(bf16[128,896]{1,0:T(8,128)(2,1)S(1)} %collective-permute-done.1), channel_id=1, source_target_pairs={{0,16},{16,0},{1,17},{17,1},{2,18},{18,2},{3,19},{19,3},{4,20},{20... | collective-permute-start | bytes 688136 | tf_op jit(solution)/shard_map/ppermute | solution.py:31
  38.1 0.0 all-to-all-done
  38.2 0.7 broadcast_in_dim.9
  38.8 9.0 %all-to-all-start.1 = ((bf16[16,2,2,8,128]{4,3,2,1,0:T(8,128)(2,1)}), bf16[16,2,2,8,128]{4,3,2,1,0:T(8,128)(2,1)S(1)}, u32[]{:S(2)}, u32[]{:S(2)}) async-start(bf16[16,2,2,8,128]{4,3,2,1,0:T(8,128)(2,1)} %broadcast_in_dim.9), calls=%async_computation.1 | async-start | bytes 262144 | tf_op jit(solution)/shard_map/all_to_all | solution.py:14
  47.8 0.0 collective-permute-done
  47.8 0.0 collective-permute-done.2
  47.8 0.1 pad_maximum_fusion
  48.0 6.6 %all-to-all-done.1 = bf16[16,2,2,8,128]{4,3,2,1,0:T(8,128)(2,1)S(1)} async-done(((bf16[16,2,2,8,128]{4,3,2,1,0:T(8,128)(2,1)}), bf16[16,2,2,8,128]{4,3,2,1,0:T(8,128)(2,1)S(1)}, u32[]{:S(2)}, u32[]{:S(2)}) %all-to-all-start.1) | async-done | bytes 131104 | tf_op jit(solution)/shard_map/all_to_all | solution.py:14
  54.5 1.0 fusion.1
  55.5 12.2 %all-to-all-start.2 = ((bf16[16,8,896]{2,1,0:T(8,128)(2,1)}), bf16[16,8,896]{2,1,0:T(8,128)(2,1)S(1)}, u32[]{:S(2)}, u32[]{:S(2)}) async-start(bf16[16,8,896]{2,1,0:T(8,128)(2,1)} %fusion.1), calls=%async_computation.2 | async-start | bytes 458752 | tf_op jit(solution)/shard_map/all_to_all | solution.py:14
  67.8 3.7 %collective-permute-start.5 = (bf16[16,8,128]{2,1,0:T(8,128)(2,1)S(1)}, bf16[16,8,128]{2,1,0:T(8,128)(2,1)S(1)}, u32[]{:S(2)}, u32[]{:S(2)}) collective-permute-start(bf16[16,8,128]{2,1,0:T(8,128)(2,1)S(1)} %get-tuple-element.19), channel_id=1, source_target_pairs={{0,528},{16,512},{512,16},{528,0},{1,529},{17,513},{513,17},{529,1... | collective-permute-start | bytes 98312 | tf_op jit(solution)/shard_map/ppermute | solution.py:31
  71.5 4.2 %collective-permute-start.4 = (bf16[16,8,128]{2,1,0:T(8,128)(2,1)S(1)}, bf16[16,8,128]{2,1,0:T(8,128)(2,1)S(1)}, u32[]{:S(2)}, u32[]{:S(2)}) collective-permute-start(bf16[16,8,128]{2,1,0:T(8,128)(2,1)S(1)} %get-tuple-element.20), channel_id=1, source_target_pairs={{0,512},{512,0},{1,513},{513,1},{2,514},{514,2},{3,515},{515,3},{4... | collective-permute-start | bytes 98312 | tf_op jit(solution)/shard_map/ppermute | solution.py:31
  75.7 3.6 %collective-permute-start.3 = (bf16[16,8,128]{2,1,0:T(8,128)(2,1)S(1)}, bf16[16,8,128]{2,1,0:T(8,128)(2,1)S(1)}, u32[]{:S(2)}, u32[]{:S(2)}) collective-permute-start(bf16[16,8,128]{2,1,0:T(8,128)(2,1)S(1)} %get-tuple-element.21), channel_id=1, source_target_pairs={{0,16},{16,0},{1,17},{17,1},{2,18},{18,2},{3,19},{19,3},{4,20},{20... | collective-permute-start | bytes 98312 | tf_op jit(solution)/shard_map/ppermute | solution.py:31
  79.3 0.0 collective-permute-done.5
  79.3 1.8 %collective-permute-done.4 = bf16[16,8,128]{2,1,0:T(8,128)(2,1)S(1)} collective-permute-done((bf16[16,8,128]{2,1,0:T(8,128)(2,1)S(1)}, bf16[16,8,128]{2,1,0:T(8,128)(2,1)S(1)}, u32[]{:S(2)}, u32[]{:S(2)}) %collective-permute-start.4) | collective-permute-done | bytes 32800 | tf_op jit(solution)/shard_map/ppermute | solution.py:31
  81.2 0.0 collective-permute-done.3
  81.3 3.2 %all-to-all-done.2 = bf16[16,8,896]{2,1,0:T(8,128)(2,1)S(1)} async-done(((bf16[16,8,896]{2,1,0:T(8,128)(2,1)}), bf16[16,8,896]{2,1,0:T(8,128)(2,1)S(1)}, u32[]{:S(2)}, u32[]{:S(2)}) %all-to-all-start.2) | async-done | bytes 229408 | tf_op jit(solution)/shard_map/all_to_all | solution.py:14
  84.6 0.0 copy-start
  84.6 0.7 broadcast_in_dim.10
  85.3 8.6 %all-to-all-start.3 = ((bf16[16,8,896]{2,1,0:T(8,128)(2,1)}), bf16[16,8,896]{2,1,0:T(8,128)(2,1)S(1)}, u32[]{:S(2)}, u32[]{:S(2)}) async-start(bf16[16,8,896]{2,1,0:T(8,128)(2,1)} %broadcast_in_dim.10), calls=%async_computation.3 | async-start | bytes 458752 | tf_op jit(solution)/shard_map/all_to_all | solution.py:14
  93.9 0.0 copy-start.1
  93.9 0.0 copy-done
  94.0 0.8 copy-done.1
  94.8 0.3 fusion.5
  95.1 3.1 %collective-permute-start.6 = (bf16[128,512]{1,0:T(8,128)(2,1)S(1)}, bf16[128,512]{1,0:T(8,128)(2,1)S(1)}, u32[]{:S(2)}, u32[]{:S(2)}) collective-permute-start(bf16[128,512]{1,0:T(8,128)(2,1)S(1)} %fusion.5), channel_id=1, source_target_pairs={{0,16},{16,0},{1,17},{17,1},{2,18},{18,2},{3,19},{19,3},{4,20},{20... | collective-permute-start | bytes 393224 | tf_op jit(solution)/shard_map/ppermute | solution.py:31
  98.2 0.0 copy-start.3
  98.2 0.9 collective-permute-done.6
  99.1 0.6 fusion.19
  99.8 10.1 %all-to-all-done.3 = bf16[16,8,896]{2,1,0:T(8,128)(2,1)S(1)} async-done(((bf16[16,8,896]{2,1,0:T(8,128)(2,1)}), bf16[16,8,896]{2,1,0:T(8,128)(2,1)S(1)}, u32[]{:S(2)}, u32[]{:S(2)}) %all-to-all-start.3) | async-done | bytes 229408 | tf_op jit(solution)/shard_map/all_to_all | solution.py:14
  109.9 0.4 fusion.9
  110.4 13.9 %all_to_all.35 = bf16[16,8,512]{2,1,0:T(8,128)(2,1)S(1)} all-to-all(bf16[16,8,512]{2,1,0:T(8,128)(2,1)S(1)} %fusion.9), channel_id=1, replica_groups=mesh['yh'=2,'z'=16,'c'=2,'x'=4,'yl'=4] {'x','yl'}, dimensions={0} | all-to-all | bytes 262144 | tf_op jit(solution)/shard_map/all_to_all | solution.py:14
  124.3 0.7 broadcast_in_dim.11
  124.9 5.4 %all-to-all-start.5 = ((bf16[16,8,512]{2,1,0:T(8,128)(2,1)}), bf16[16,8,512]{2,1,0:T(8,128)(2,1)S(1)}, u32[]{:S(2)}, u32[]{:S(2)}) async-start(bf16[16,8,512]{2,1,0:T(8,128)(2,1)} %broadcast_in_dim.11), calls=%async_computation.5 | async-start | bytes 262144 | tf_op jit(solution)/shard_map/all_to_all | solution.py:14
  130.4 1.9 %collective-permute-start.8 = (bf16[128,512]{1,0:T(8,128)(2,1)S(1)}, bf16[128,512]{1,0:T(8,128)(2,1)S(1)}, u32[]{:S(2)}, u32[]{:S(2)}) collective-permute-start(bf16[128,512]{1,0:T(8,128)(2,1)S(1)} %fusion.5), channel_id=1, source_target_pairs={{0,528},{16,512},{512,16},{528,0},{1,529},{17,513},{513,17},{529,1... | collective-permute-start | bytes 393224 | tf_op jit(solution)/shard_map/ppermute | solution.py:31
  132.3 4.5 %collective-permute-start.7 = (bf16[128,512]{1,0:T(8,128)(2,1)S(1)}, bf16[128,512]{1,0:T(8,128)(2,1)S(1)}, u32[]{:S(2)}, u32[]{:S(2)}) collective-permute-start(bf16[128,512]{1,0:T(8,128)(2,1)S(1)} %fusion.5), channel_id=1, source_target_pairs={{0,512},{512,0},{1,513},{513,1},{2,514},{514,2},{3,515},{515,3},{4... | collective-permute-start | bytes 393224 | tf_op jit(solution)/shard_map/ppermute | solution.py:31
  136.8 0.0 all-to-all-done.5
  136.8 0.2 fusion.10
  137.0 3.7 %collective-permute-done.8 = bf16[128,512]{1,0:T(8,128)(2,1)S(1)} collective-permute-done((bf16[128,512]{1,0:T(8,128)(2,1)S(1)}, bf16[128,512]{1,0:T(8,128)(2,1)S(1)}, u32[]{:S(2)}, u32[]{:S(2)}) %collective-permute-start.8) | collective-permute-done | bytes 131104 | tf_op jit(solution)/shard_map/ppermute | solution.py:31
  140.7 0.2 fusion.12
  140.8 8.5 %collective-permute-done.7 = bf16[128,512]{1,0:T(8,128)(2,1)S(1)} collective-permute-done((bf16[128,512]{1,0:T(8,128)(2,1)S(1)}, bf16[128,512]{1,0:T(8,128)(2,1)S(1)}, u32[]{:S(2)}, u32[]{:S(2)}) %collective-permute-start.7) | collective-permute-done | bytes 131104 | tf_op jit(solution)/shard_map/ppermute | solution.py:31
  149.4 0.2 fusion.7
  149.5 20.9 %all_to_all.36 = bf16[16,8,512]{2,1,0:T(8,128)(2,1)S(1)} all-to-all(bf16[16,8,512]{2,1,0:T(8,128)(2,1)S(1)} %fusion.7), channel_id=1, replica_groups=mesh['yh'=2,'z'=16,'c'=2,'x'=4,'yl'=4] {'z'}, dimensions={0} | all-to-all | bytes 262144 | tf_op jit(solution)/shard_map/all_to_all | solution.py:14
  170.4 0.6 add.39
  (20 shorter events, 0.3 us)
Async XLA Ops:
  2.6 17.4 %copy-start.2 = (bf16[128,896]{1,0:T(8,128)(2,1)S(1)}, bf16[128,896]{1,0:T(8,128)(2,1)}, u32[]{:S(2)}) copy-start(bf16[128,896]{1,0:T(8,128)(2,1)} %param.6) | copy-start | bytes 688132
  2.6 26.9 %copy-start.4 = (f32[8,896]{1,0:T(8,128)S(1)}, f32[8,896]{1,0:T(8,128)}, u32[]{:S(2)}) copy-start(f32[8,896]{1,0:T(8,128)} %param.8) | copy-start | bytes 86020
  2.6 35.5 %all-to-all-start = ((bf16[64,8,128]{2,1,0:T(8,128)(2,1)}), bf16[64,8,128]{2,1,0:T(8,128)(2,1)S(1)}, u32[]{:S(2)}, u32[]{:S(2)}) async-start(bf16[64,8,128]{2,1,0:T(8,128)(2,1)} %fusion.8), calls=%async_computation | async-start | bytes 262144 | tf_op jit(solution)/shard_map/all_to_all | solution.py:14
  20.1 16.1 %collective-permute-start.1 = (bf16[128,896]{1,0:T(8,128)(2,1)S(1)}, bf16[128,896]{1,0:T(8,128)(2,1)S(1)}, u32[]{:S(2)}, u32[]{:S(2)}) collective-permute-start(bf16[128,896]{1,0:T(8,128)(2,1)S(1)} %copy-done.2), channel_id=1, source_target_pairs={{0,512},{512,0},{1,513},{513,1},{2,514},{514,2},{3,515},{515,3},{4... | collective-permute-start | bytes 688136 | tf_op jit(solution)/shard_map/ppermute | solution.py:31
  27.6 20.2 %collective-permute-start = (bf16[128,896]{1,0:T(8,128)(2,1)S(1)}, bf16[128,896]{1,0:T(8,128)(2,1)S(1)}, u32[]{:S(2)}, u32[]{:S(2)}) collective-permute-start(bf16[128,896]{1,0:T(8,128)(2,1)S(1)} %copy-done.2), channel_id=1, source_target_pairs={{0,16},{16,0},{1,17},{17,1},{2,18},{18,2},{3,19},{19,3},{4,20},{20... | collective-permute-start | bytes 688136 | tf_op jit(solution)/shard_map/ppermute | solution.py:31
  36.2 11.6 %collective-permute-start.2 = (bf16[128,896]{1,0:T(8,128)(2,1)S(1)}, bf16[128,896]{1,0:T(8,128)(2,1)S(1)}, u32[]{:S(2)}, u32[]{:S(2)}) collective-permute-start(bf16[128,896]{1,0:T(8,128)(2,1)S(1)} %collective-permute-done.1), channel_id=1, source_target_pairs={{0,16},{16,0},{1,17},{17,1},{2,18},{18,2},{3,19},{19,3},{4,20},{20... | collective-permute-start | bytes 688136 | tf_op jit(solution)/shard_map/ppermute | solution.py:31
  38.8 15.7 %all-to-all-start.1 = ((bf16[16,2,2,8,128]{4,3,2,1,0:T(8,128)(2,1)}), bf16[16,2,2,8,128]{4,3,2,1,0:T(8,128)(2,1)S(1)}, u32[]{:S(2)}, u32[]{:S(2)}) async-start(bf16[16,2,2,8,128]{4,3,2,1,0:T(8,128)(2,1)} %broadcast_in_dim.9), calls=%async_computation.1 | async-start | bytes 262144 | tf_op jit(solution)/shard_map/all_to_all | solution.py:14
  55.5 29.0 %all-to-all-start.2 = ((bf16[16,8,896]{2,1,0:T(8,128)(2,1)}), bf16[16,8,896]{2,1,0:T(8,128)(2,1)S(1)}, u32[]{:S(2)}, u32[]{:S(2)}) async-start(bf16[16,8,896]{2,1,0:T(8,128)(2,1)} %fusion.1), calls=%async_computation.2 | async-start | bytes 458752 | tf_op jit(solution)/shard_map/all_to_all | solution.py:14
  67.8 11.5 %collective-permute-start.5 = (bf16[16,8,128]{2,1,0:T(8,128)(2,1)S(1)}, bf16[16,8,128]{2,1,0:T(8,128)(2,1)S(1)}, u32[]{:S(2)}, u32[]{:S(2)}) collective-permute-start(bf16[16,8,128]{2,1,0:T(8,128)(2,1)S(1)} %get-tuple-element.19), channel_id=1, source_target_pairs={{0,528},{16,512},{512,16},{528,0},{1,529},{17,513},{513,17},{529,1... | collective-permute-start | bytes 98312 | tf_op jit(solution)/shard_map/ppermute | solution.py:31
  71.5 9.7 %collective-permute-start.4 = (bf16[16,8,128]{2,1,0:T(8,128)(2,1)S(1)}, bf16[16,8,128]{2,1,0:T(8,128)(2,1)S(1)}, u32[]{:S(2)}, u32[]{:S(2)}) collective-permute-start(bf16[16,8,128]{2,1,0:T(8,128)(2,1)S(1)} %get-tuple-element.20), channel_id=1, source_target_pairs={{0,512},{512,0},{1,513},{513,1},{2,514},{514,2},{3,515},{515,3},{4... | collective-permute-start | bytes 98312 | tf_op jit(solution)/shard_map/ppermute | solution.py:31
  75.7 5.5 %collective-permute-start.3 = (bf16[16,8,128]{2,1,0:T(8,128)(2,1)S(1)}, bf16[16,8,128]{2,1,0:T(8,128)(2,1)S(1)}, u32[]{:S(2)}, u32[]{:S(2)}) collective-permute-start(bf16[16,8,128]{2,1,0:T(8,128)(2,1)S(1)} %get-tuple-element.21), channel_id=1, source_target_pairs={{0,16},{16,0},{1,17},{17,1},{2,18},{18,2},{3,19},{19,3},{4,20},{20... | collective-permute-start | bytes 98312 | tf_op jit(solution)/shard_map/ppermute | solution.py:31
  84.6 9.4 %copy-start = (bf16[512,512]{1,0:T(8,128)(2,1)S(1)}, bf16[512,512]{1,0:T(8,128)(2,1)}, u32[]{:S(2)}) copy-start(bf16[512,512]{1,0:T(8,128)(2,1)} %param.7) | copy-start | bytes 1572868
  85.3 24.6 %all-to-all-start.3 = ((bf16[16,8,896]{2,1,0:T(8,128)(2,1)}), bf16[16,8,896]{2,1,0:T(8,128)(2,1)S(1)}, u32[]{:S(2)}, u32[]{:S(2)}) async-start(bf16[16,8,896]{2,1,0:T(8,128)(2,1)} %broadcast_in_dim.10), calls=%async_computation.3 | async-start | bytes 458752 | tf_op jit(solution)/shard_map/all_to_all | solution.py:14
  93.9 0.9 copy-start.1
  95.1 4.0 %collective-permute-start.6 = (bf16[128,512]{1,0:T(8,128)(2,1)S(1)}, bf16[128,512]{1,0:T(8,128)(2,1)S(1)}, u32[]{:S(2)}, u32[]{:S(2)}) collective-permute-start(bf16[128,512]{1,0:T(8,128)(2,1)S(1)} %fusion.5), channel_id=1, source_target_pairs={{0,16},{16,0},{1,17},{17,1},{2,18},{18,2},{3,19},{19,3},{4,20},{20... | collective-permute-start | bytes 393224 | tf_op jit(solution)/shard_map/ppermute | solution.py:31
  98.2 1.0 copy-start.3
  124.9 11.9 %all-to-all-start.5 = ((bf16[16,8,512]{2,1,0:T(8,128)(2,1)}), bf16[16,8,512]{2,1,0:T(8,128)(2,1)S(1)}, u32[]{:S(2)}, u32[]{:S(2)}) async-start(bf16[16,8,512]{2,1,0:T(8,128)(2,1)} %broadcast_in_dim.11), calls=%async_computation.5 | async-start | bytes 262144 | tf_op jit(solution)/shard_map/all_to_all | solution.py:14
  130.4 10.3 %collective-permute-start.8 = (bf16[128,512]{1,0:T(8,128)(2,1)S(1)}, bf16[128,512]{1,0:T(8,128)(2,1)S(1)}, u32[]{:S(2)}, u32[]{:S(2)}) collective-permute-start(bf16[128,512]{1,0:T(8,128)(2,1)S(1)} %fusion.5), channel_id=1, source_target_pairs={{0,528},{16,512},{512,16},{528,0},{1,529},{17,513},{513,17},{529,1... | collective-permute-start | bytes 393224 | tf_op jit(solution)/shard_map/ppermute | solution.py:31
  132.3 17.1 %collective-permute-start.7 = (bf16[128,512]{1,0:T(8,128)(2,1)S(1)}, bf16[128,512]{1,0:T(8,128)(2,1)S(1)}, u32[]{:S(2)}, u32[]{:S(2)}) collective-permute-start(bf16[128,512]{1,0:T(8,128)(2,1)S(1)} %fusion.5), channel_id=1, source_target_pairs={{0,512},{512,0},{1,513},{513,1},{2,514},{514,2},{3,515},{515,3},{4... | collective-permute-start | bytes 393224 | tf_op jit(solution)/shard_map/ppermute | solution.py:31

commit v10 on v8

--- a/solution.py
+++ b/solution.py
@@ -44,6 +44,9 @@
     grad_c = across(grad_out, "c")
     grad_d = across(grad_yh, "c")
     grad_all = jnp.stack([grad_out, grad_c, grad_yh, grad_d]).reshape(2, 2, 128, -1)
+    acts_c = across(acts, "c")
+    acts_yh = across(acts, "yh")
+    acts_d = across(acts_yh, "c")
     moment_base = 0.9 * first_moment
     own_rows = lax.dynamic_slice_in_dim(proj_t, lax.axis_index(DP) * OWN, OWN, 0)
     own_rows = own_rows.astype(jnp.float32)
@@ -52,21 +55,19 @@
     got, moment_base = lax.optimization_barrier((got, moment_base))
     part = jnp.sum(got.reshape(2, 16, 2, OWN, 128).astype(jnp.float32), axis=1)
     part = from_own(part, ("yh", "c")).astype(bf16)
-    coords = to_all(part, TENSOR, 16).transpose(1, 2, 0, 3, 4)
-    grad_part = (dot(coords, grad_all, ((0, 1, 4), (0, 1, 2))) / TOKENS).astype(bf16)
+    coords = to_all(part, TENSOR, 16)
+    grad_part = (dot(coords, grad_all, ((1, 2, 4), (0, 1, 2))) / TOKENS).astype(bf16)
     got = swap(grad_part.reshape(16, OWN, -1), "z")
-    coords_yh = across(coords[1, 0], "yh")
-    coords_d = across(coords[1, 1], "yh", "c")
-    coords_c = across(coords[0, 1], "c")
-    mine = jnp.stack([coords[0, 0], coords_c, coords_yh, coords_d])
-    mine = from_own(mine.reshape(2, 2, 16, OWN, 128), ("yh", "c"))
-    mine = mine.transpose(0, 2, 1, 3, 4).reshape(512, 128)
-    residual = (root * acts - dot(mine, proj_t, ((0,), (0,)))).astype(bf16)
-    residual_yh = across(residual, "yh")
-    residual_c = across(residual, "c")
-    residual_d = across(residual_yh, "c")
-    residual_all = jnp.concatenate([residual, residual_c, residual_yh, residual_d])
     got, own_rows = lax.optimization_barrier((got, own_rows))
+    coords_yh = across(coords, "yh")
+    coords_d = across(coords, "yh", "c")
+    coords_c = across(coords, "c")
+    ranks = [coords, jnp.flip(coords_c, 2), jnp.flip(coords_yh, 1), jnp.flip(coords_d, (1, 2))]
+    ranks = from_own(jnp.stack(ranks).reshape(2, 2, *coords.shape), ("yh", "c"))
+    acts_all = jnp.concatenate([acts, acts_c, acts_yh, acts_d])
+    ranks = ranks.transpose(0, 2, 1, 5, 3, 4, 6).reshape(512, 512)
+    spanned = dot(ranks, proj_t, ((0,), (0,)))
+    residual = (root * acts_all - spanned).astype(bf16)
     grad_own = total(got)
     low_own = grad_own.astype(bf16)
     low_own, grad_own = lax.optimization_barrier((low_own, grad_own))
@@ -75,12 +76,12 @@
     root_two = jnp.sqrt(moment_two / (1.0 - 0.999**10)) + 1e-08
     adam_step = moment_one / (1.0 - 0.9**10) / root_two
     low = to_all(low_own, "z", 16).reshape(128, -1)
-    low, residual_all, adam_step = lax.optimization_barrier((low, residual_all, adam_step))
+    low, residual, adam_step = lax.optimization_barrier((low, residual, adam_step))
     back = dot(low, grad_all.reshape(512, -1), ((1,), (1,))).astype(bf16)
     back = total(swap(back.reshape(16, OWN, -1), TENSOR)).astype(bf16)
     back = to_all(back, TENSOR, 16).reshape(128, -1)
-    pull = (dot(back, residual_all, ((1,), (0,))) / TOKENS).astype(bf16)
-    moved = total(swap(pull.reshape(16, OWN, -1), "z"))
+    pull = dot(back, residual, ((1,), (0,))) / TOKENS
+    moved = total(swap(pull.astype(bf16).reshape(16, OWN, -1), "z"))
     return (adam_step, own_rows + moved)
 
 

time: 164 us -> 167 us (1.018)
  blocking collectives: 47.7 us -> 40.2 us
  waiting for transfers between devices: 31.6 us -> 36.8 us
  starting transfers between devices: 76 us -> 80.6 us
    all_to_all x4, waiting for transfers between devices: 10.2 us -> 23 us  [swap(): return lax.all_to_all(pieces, axes, split_axis=0, concat_axis=0, tiled=True)]
    ppermute x9, waiting for transfers between devices: 21.4 us -> 13.8 us  [across(): return lax.ppermute(x, axes, [(i, last - i) for i in range(last + 1)])]
    all_to_all x3, blocking collectives: 47.7 us -> 40.2 us  [swap(): return lax.all_to_all(pieces, axes, split_axis=0, concat_axis=0, tiled=True)]
    all_to_all x4, starting transfers between devices: 45.6 us -> 48.5 us  [swap(): return lax.all_to_all(pieces, axes, split_axis=0, concat_axis=0, tiled=True)]
    ppermute x9, starting transfers between devices: 30.4 us -> 32.1 us  [across(): return lax.ppermute(x, axes, [(i, last - i) for i in range(last + 1)])]
  transfers between devices with their start and end apart: 13 -> 13, of which waited for: 6 -> 4; matrix products, arithmetic and copies ran while one was open for 1% -> 2% of each run, Pallas kernels for 0% -> 0%
where the time goes in v10:
time: 167 us; the launch traced here: 166 us
  starting transfers between devices  80.6 us (48%)
  blocking collectives  40.2 us (24%)
  waiting for transfers between devices  36.8 us (22%)
  matrix products  4.12 us (2%)
  other arithmetic  1.89 us (1%)
  local copies, waits for them, and re-layouts  1.77 us (1%)
    all_to_all x4, starting transfers between devices, swap(): return lax.all_to_all(pieces, axes, split_axis=0, concat_axis=0, tiled=True)  48.5 us
    all_to_all x3, blocking collectives, swap(): return lax.all_to_all(pieces, axes, split_axis=0, concat_axis=0, tiled=True)  40.2 us
    ppermute x9, starting transfers between devices, across(): return lax.ppermute(x, axes, [(i, last - i) for i in range(last + 1)])  32.1 us
    all_to_all x4, waiting for transfers between devices, swap(): return lax.all_to_all(pieces, axes, split_axis=0, concat_axis=0, tiled=True)  23 us
    ppermute x9, waiting for transfers between devices, across(): return lax.ppermute(x, axes, [(i, last - i) for i in range(last + 1)])  13.8 us
    dot_general x5, matrix products, dot(): lax.dot_general(left, right, (dims, ((), ())), preferred_element_type=jnp...  4.12 us
  transfers between devices with their start and end apart: 13, of which 4 were waited for; matrix products, arithmetic and copies ran while one was open for 2% of the time, Pallas kernels for 0%

profile of v10, /device:TPU:8, one launch (start us, length us, event | category | flops | bytes accessed | tf_op | source)
XLA Modules:
  0.0 166.4 jit_solution(12833424642872207592)
XLA Ops:
  0.6 2.0 %fusion.5 = bf16[64,8,128]{2,1,0:T(8,128)(2,1)} fusion(bf16[512,512]{1,0:T(8,128)(2,1)} %param.7, bf16[128,512]{1,0:T(8,128)(2,1)} %param.5), kind=kOutput, calls=%fused_computation.9 | convolution fusion | flops 67239936 | bytes 786432 | tf_op jit(solution)/shard_map/dot_general | solution.py:26
  2.6 17.2 %all-to-all-start = ((bf16[64,8,128]{2,1,0:T(8,128)(2,1)}), bf16[64,8,128]{2,1,0:T(8,128)(2,1)S(1)}, u32[]{:S(2)}, u32[]{:S(2)}) async-start(bf16[64,8,128]{2,1,0:T(8,128)(2,1)} %fusion.5), calls=%async_computation | async-start | bytes 262144 | tf_op jit(solution)/shard_map/all_to_all | solution.py:14
  19.9 0.0 copy-done.1
  19.9 6.6 %collective-permute-start.1 = (bf16[128,896]{1,0:T(8,128)(2,1)S(1)}, bf16[128,896]{1,0:T(8,128)(2,1)S(1)}, u32[]{:S(2)}, u32[]{:S(2)}) collective-permute-start(bf16[128,896]{1,0:T(8,128)(2,1)S(1)} %copy-done.1), channel_id=1, source_target_pairs={{0,512},{512,0},{1,513},{513,1},{2,514},{514,2},{3,515},{515,3},{4... | collective-permute-start | bytes 688136 | tf_op jit(solution)/shard_map/ppermute | solution.py:31
  26.5 1.9 %collective-permute-start = (bf16[128,896]{1,0:T(8,128)(2,1)S(1)}, bf16[128,896]{1,0:T(8,128)(2,1)S(1)}, u32[]{:S(2)}, u32[]{:S(2)}) collective-permute-start(bf16[128,896]{1,0:T(8,128)(2,1)S(1)} %copy-done.1), channel_id=1, source_target_pairs={{0,16},{16,0},{1,17},{17,1},{2,18},{18,2},{3,19},{19,3},{4,20},{20... | collective-permute-start | bytes 688136 | tf_op jit(solution)/shard_map/ppermute | solution.py:31
  28.4 0.0 copy-done.4
  28.5 9.8 %collective-permute-done.1 = bf16[128,896]{1,0:T(8,128)(2,1)S(1)} collective-permute-done((bf16[128,896]{1,0:T(8,128)(2,1)S(1)}, bf16[128,896]{1,0:T(8,128)(2,1)S(1)}, u32[]{:S(2)}, u32[]{:S(2)}) %collective-permute-start.1) | collective-permute-done | bytes 229408 | tf_op jit(solution)/shard_map/ppermute | solution.py:31
  38.2 1.9 %collective-permute-start.2 = (bf16[128,896]{1,0:T(8,128)(2,1)S(1)}, bf16[128,896]{1,0:T(8,128)(2,1)S(1)}, u32[]{:S(2)}, u32[]{:S(2)}) collective-permute-start(bf16[128,896]{1,0:T(8,128)(2,1)S(1)} %collective-permute-done.1), channel_id=1, source_target_pairs={{0,16},{16,0},{1,17},{17,1},{2,18},{18,2},{3,19},{19,3},{4,20},{20... | collective-permute-start | bytes 688136 | tf_op jit(solution)/shard_map/ppermute | solution.py:31
  40.2 0.0 all-to-all-done
  40.2 0.7 broadcast_in_dim.9
  40.9 6.9 %all-to-all-start.1 = ((bf16[16,2,2,8,128]{4,3,2,1,0:T(8,128)(2,1)}), bf16[16,2,2,8,128]{4,3,2,1,0:T(8,128)(2,1)S(1)}, u32[]{:S(2)}, u32[]{:S(2)}) async-start(bf16[16,2,2,8,128]{4,3,2,1,0:T(8,128)(2,1)} %broadcast_in_dim.9), calls=%async_computation.1 | async-start | bytes 262144 | tf_op jit(solution)/shard_map/all_to_all | solution.py:14
  47.8 0.0 collective-permute-done
  47.8 0.0 collective-permute-done.2
  47.8 0.1 pad_maximum_fusion
  47.9 7.4 %all-to-all-done.1 = bf16[16,2,2,8,128]{4,3,2,1,0:T(8,128)(2,1)S(1)} async-done(((bf16[16,2,2,8,128]{4,3,2,1,0:T(8,128)(2,1)}), bf16[16,2,2,8,128]{4,3,2,1,0:T(8,128)(2,1)S(1)}, u32[]{:S(2)}, u32[]{:S(2)}) %all-to-all-start.1) | async-done | bytes 131104 | tf_op jit(solution)/shard_map/all_to_all | solution.py:14
  55.4 1.0 fusion.1
  56.4 12.4 %all-to-all-start.2 = ((bf16[16,8,896]{2,1,0:T(8,128)(2,1)}), bf16[16,8,896]{2,1,0:T(8,128)(2,1)S(1)}, u32[]{:S(2)}, u32[]{:S(2)}) async-start(bf16[16,8,896]{2,1,0:T(8,128)(2,1)} %fusion.1), calls=%async_computation.2 | async-start | bytes 458752 | tf_op jit(solution)/shard_map/all_to_all | solution.py:14
  68.7 0.0 copy-done.2
  68.7 5.5 %collective-permute-start.4 = (bf16[128,512]{1,0:T(8,128)(2,1)S(1)}, bf16[128,512]{1,0:T(8,128)(2,1)S(1)}, u32[]{:S(2)}, u32[]{:S(2)}) collective-permute-start(bf16[128,512]{1,0:T(8,128)(2,1)S(1)} %copy-done.2), channel_id=1, source_target_pairs={{0,512},{512,0},{1,513},{513,1},{2,514},{514,2},{3,515},{515,3},{4... | collective-permute-start | bytes 393224 | tf_op jit(solution)/shard_map/ppermute | solution.py:31
  74.3 2.6 %collective-permute-start.8 = (bf16[16,2,2,8,128]{4,3,2,1,0:T(8,128)(2,1)S(1)}, bf16[16,2,2,8,128]{4,3,2,1,0:T(8,128)(2,1)S(1)}, u32[]{:S(2)}, u32[]{:S(2)}) collective-permute-start(bf16[16,2,2,8,128]{4,3,2,1,0:T(8,128)(2,1)S(1)} %all-to-all-done.1), channel_id=1, source_target_pairs={{0,528},{16,512},{512,16},{528,0},{1,529},{17,513},{513,17},{529,1... | collective-permute-start | bytes 393224 | tf_op jit(solution)/shard_map/ppermute | solution.py:31
  76.9 3.6 %collective-permute-start.3 = (bf16[128,512]{1,0:T(8,128)(2,1)S(1)}, bf16[128,512]{1,0:T(8,128)(2,1)S(1)}, u32[]{:S(2)}, u32[]{:S(2)}) collective-permute-start(bf16[128,512]{1,0:T(8,128)(2,1)S(1)} %copy-done.2), channel_id=1, source_target_pairs={{0,16},{16,0},{1,17},{17,1},{2,18},{18,2},{3,19},{19,3},{4,20},{20... | collective-permute-start | bytes 393224 | tf_op jit(solution)/shard_map/ppermute | solution.py:31
  80.5 5.5 %collective-permute-start.7 = (bf16[16,2,2,8,128]{4,3,2,1,0:T(8,128)(2,1)S(1)}, bf16[16,2,2,8,128]{4,3,2,1,0:T(8,128)(2,1)S(1)}, u32[]{:S(2)}, u32[]{:S(2)}) collective-permute-start(bf16[16,2,2,8,128]{4,3,2,1,0:T(8,128)(2,1)S(1)} %all-to-all-done.1), channel_id=1, source_target_pairs={{0,512},{512,0},{1,513},{513,1},{2,514},{514,2},{3,515},{515,3},{4... | collective-permute-start | bytes 393224 | tf_op jit(solution)/shard_map/ppermute | solution.py:31
  86.1 0.0 collective-permute-done.4
  86.1 1.9 %collective-permute-start.5 = (bf16[128,512]{1,0:T(8,128)(2,1)S(1)}, bf16[128,512]{1,0:T(8,128)(2,1)S(1)}, u32[]{:S(2)}, u32[]{:S(2)}) collective-permute-start(bf16[128,512]{1,0:T(8,128)(2,1)S(1)} %collective-permute-done.4), channel_id=1, source_target_pairs={{0,16},{16,0},{1,17},{17,1},{2,18},{18,2},{3,19},{19,3},{4,20},{20... | collective-permute-start | bytes 393224 | tf_op jit(solution)/shard_map/ppermute | solution.py:31
  88.1 2.4 %collective-permute-start.6 = (bf16[16,2,2,8,128]{4,3,2,1,0:T(8,128)(2,1)S(1)}, bf16[16,2,2,8,128]{4,3,2,1,0:T(8,128)(2,1)S(1)}, u32[]{:S(2)}, u32[]{:S(2)}) collective-permute-start(bf16[16,2,2,8,128]{4,3,2,1,0:T(8,128)(2,1)S(1)} %all-to-all-done.1), channel_id=1, source_target_pairs={{0,16},{16,0},{1,17},{17,1},{2,18},{18,2},{3,19},{19,3},{4,20},{20... | collective-permute-start | bytes 393224 | tf_op jit(solution)/shard_map/ppermute | solution.py:31
  90.5 0.0 collective-permute-done.8
  90.5 4.0 %collective-permute-done.7 = bf16[16,2,2,8,128]{4,3,2,1,0:T(8,128)(2,1)S(1)} collective-permute-done((bf16[16,2,2,8,128]{4,3,2,1,0:T(8,128)(2,1)S(1)}, bf16[16,2,2,8,128]{4,3,2,1,0:T(8,128)(2,1)S(1)}, u32[]{:S(2)}, u32[]{:S(2)}) %collective-permute-start.7) | collective-permute-done | bytes 131104 | tf_op jit(solution)/shard_map/ppermute | solution.py:31
  94.6 0.0 collective-permute-done.6
  94.6 0.1 pad_maximum_fusion.1
  94.7 0.1 copy.8
  94.7 0.0 all-to-all-done.2
  94.8 0.7 broadcast_in_dim.10
  95.5 12.0 %all-to-all-start.3 = ((bf16[16,8,896]{2,1,0:T(8,128)(2,1)}), bf16[16,8,896]{2,1,0:T(8,128)(2,1)S(1)}, u32[]{:S(2)}, u32[]{:S(2)}) async-start(bf16[16,8,896]{2,1,0:T(8,128)(2,1)} %broadcast_in_dim.10), calls=%async_computation.3 | async-start | bytes 458752 | tf_op jit(solution)/shard_map/all_to_all | solution.py:14
  107.5 0.1 reverse_select_fusion.1
  107.7 0.1 reverse_select_fusion
  107.8 0.0 collective-permute-done.3
  107.9 0.0 collective-permute-done.5
  107.9 0.0 copy-start.3
  107.9 0.5 subtract_convert_fusion
  108.3 0.3 copy-done.3
  108.6 0.6 fusion.12
  109.3 15.6 %all-to-all-done.3 = bf16[16,8,896]{2,1,0:T(8,128)(2,1)S(1)} async-done(((bf16[16,8,896]{2,1,0:T(8,128)(2,1)}), bf16[16,8,896]{2,1,0:T(8,128)(2,1)S(1)}, u32[]{:S(2)}, u32[]{:S(2)}) %all-to-all-start.3) | async-done | bytes 229408 | tf_op jit(solution)/shard_map/all_to_all | solution.py:14
  124.8 0.4 fusion.6
  125.3 10.4 %all_to_all.35 = bf16[16,8,512]{2,1,0:T(8,128)(2,1)S(1)} all-to-all(bf16[16,8,512]{2,1,0:T(8,128)(2,1)S(1)} %fusion.6), channel_id=1, replica_groups=mesh['yh'=2,'z'=16,'c'=2,'x'=4,'yl'=4] {'x','yl'}, dimensions={0} | all-to-all | bytes 262144 | tf_op jit(solution)/shard_map/all_to_all | solution.py:14
  135.7 11.2 %all_to_all.36 = bf16[16,8,512]{2,1,0:T(8,128)(2,1)S(1)} all-to-all(bf16[16,8,512]{2,1,0:T(8,128)(2,1)S(1)} %broadcast_in_dim.11), channel_id=1, replica_groups=mesh['yh'=2,'z'=16,'c'=2,'x'=4,'yl'=4] {'x','yl'}, dimensions={0} | all-to-all | bytes 262144 | tf_op jit(solution)/shard_map/all_to_all | solution.py:14
  146.9 0.2 fusion.4
  147.1 18.6 %all_to_all.37 = bf16[16,8,512]{2,1,0:T(8,128)(2,1)S(1)} all-to-all(bf16[16,8,512]{2,1,0:T(8,128)(2,1)S(1)} %fusion.4), channel_id=1, replica_groups=mesh['yh'=2,'z'=16,'c'=2,'x'=4,'yl'=4] {'z'}, dimensions={0} | all-to-all | bytes 262144 | tf_op jit(solution)/shard_map/all_to_all | solution.py:14
  165.8 0.6 add.31
  (18 shorter events, 0.2 us)
Async XLA Ops:
  2.6 17.3 %copy-start.1 = (bf16[128,896]{1,0:T(8,128)(2,1)S(1)}, bf16[128,896]{1,0:T(8,128)(2,1)}, u32[]{:S(2)}) copy-start(bf16[128,896]{1,0:T(8,128)(2,1)} %param.6) | copy-start | bytes 688132
  2.6 25.8 %copy-start.4 = (f32[8,896]{1,0:T(8,128)S(1)}, f32[8,896]{1,0:T(8,128)}, u32[]{:S(2)}) copy-start(f32[8,896]{1,0:T(8,128)} %param.8) | copy-start | bytes 86020
  2.6 37.5 %all-to-all-start = ((bf16[64,8,128]{2,1,0:T(8,128)(2,1)}), bf16[64,8,128]{2,1,0:T(8,128)(2,1)S(1)}, u32[]{:S(2)}, u32[]{:S(2)}) async-start(bf16[64,8,128]{2,1,0:T(8,128)(2,1)} %fusion.5), calls=%async_computation | async-start | bytes 262144 | tf_op jit(solution)/shard_map/all_to_all | solution.py:14
  19.9 18.3 %collective-permute-start.1 = (bf16[128,896]{1,0:T(8,128)(2,1)S(1)}, bf16[128,896]{1,0:T(8,128)(2,1)S(1)}, u32[]{:S(2)}, u32[]{:S(2)}) collective-permute-start(bf16[128,896]{1,0:T(8,128)(2,1)S(1)} %copy-done.1), channel_id=1, source_target_pairs={{0,512},{512,0},{1,513},{513,1},{2,514},{514,2},{3,515},{515,3},{4... | collective-permute-start | bytes 688136 | tf_op jit(solution)/shard_map/ppermute | solution.py:31
  26.5 21.3 %collective-permute-start = (bf16[128,896]{1,0:T(8,128)(2,1)S(1)}, bf16[128,896]{1,0:T(8,128)(2,1)S(1)}, u32[]{:S(2)}, u32[]{:S(2)}) collective-permute-start(bf16[128,896]{1,0:T(8,128)(2,1)S(1)} %copy-done.1), channel_id=1, source_target_pairs={{0,16},{16,0},{1,17},{17,1},{2,18},{18,2},{3,19},{19,3},{4,20},{20... | collective-permute-start | bytes 688136 | tf_op jit(solution)/shard_map/ppermute | solution.py:31
  38.2 9.5 %collective-permute-start.2 = (bf16[128,896]{1,0:T(8,128)(2,1)S(1)}, bf16[128,896]{1,0:T(8,128)(2,1)S(1)}, u32[]{:S(2)}, u32[]{:S(2)}) collective-permute-start(bf16[128,896]{1,0:T(8,128)(2,1)S(1)} %collective-permute-done.1), channel_id=1, source_target_pairs={{0,16},{16,0},{1,17},{17,1},{2,18},{18,2},{3,19},{19,3},{4,20},{20... | collective-permute-start | bytes 688136 | tf_op jit(solution)/shard_map/ppermute | solution.py:31
  40.9 14.5 %all-to-all-start.1 = ((bf16[16,2,2,8,128]{4,3,2,1,0:T(8,128)(2,1)}), bf16[16,2,2,8,128]{4,3,2,1,0:T(8,128)(2,1)S(1)}, u32[]{:S(2)}, u32[]{:S(2)}) async-start(bf16[16,2,2,8,128]{4,3,2,1,0:T(8,128)(2,1)} %broadcast_in_dim.9), calls=%async_computation.1 | async-start | bytes 262144 | tf_op jit(solution)/shard_map/all_to_all | solution.py:14
  55.4 30.7 %copy-start = (bf16[512,512]{1,0:T(8,128)(2,1)S(1)}, bf16[512,512]{1,0:T(8,128)(2,1)}, u32[]{:S(2)}) copy-start(bf16[512,512]{1,0:T(8,128)(2,1)} %param.7) | copy-start | bytes 1572868
  56.3 12.4 %copy-start.2 = (bf16[128,512]{1,0:T(8,128)(2,1)S(1)}, bf16[128,512]{1,0:T(8,128)(2,1)}, u32[]{:S(2)}) copy-start(bf16[128,512]{1,0:T(8,128)(2,1)} %param.5) | copy-start | bytes 393220
  56.4 38.4 %all-to-all-start.2 = ((bf16[16,8,896]{2,1,0:T(8,128)(2,1)}), bf16[16,8,896]{2,1,0:T(8,128)(2,1)S(1)}, u32[]{:S(2)}, u32[]{:S(2)}) async-start(bf16[16,8,896]{2,1,0:T(8,128)(2,1)} %fusion.1), calls=%async_computation.2 | async-start | bytes 458752 | tf_op jit(solution)/shard_map/all_to_all | solution.py:14
  68.7 17.4 %collective-permute-start.4 = (bf16[128,512]{1,0:T(8,128)(2,1)S(1)}, bf16[128,512]{1,0:T(8,128)(2,1)S(1)}, u32[]{:S(2)}, u32[]{:S(2)}) collective-permute-start(bf16[128,512]{1,0:T(8,128)(2,1)S(1)} %copy-done.2), channel_id=1, source_target_pairs={{0,512},{512,0},{1,513},{513,1},{2,514},{514,2},{3,515},{515,3},{4... | collective-permute-start | bytes 393224 | tf_op jit(solution)/shard_map/ppermute | solution.py:31
  74.3 16.2 %collective-permute-start.8 = (bf16[16,2,2,8,128]{4,3,2,1,0:T(8,128)(2,1)S(1)}, bf16[16,2,2,8,128]{4,3,2,1,0:T(8,128)(2,1)S(1)}, u32[]{:S(2)}, u32[]{:S(2)}) collective-permute-start(bf16[16,2,2,8,128]{4,3,2,1,0:T(8,128)(2,1)S(1)} %all-to-all-done.1), channel_id=1, source_target_pairs={{0,528},{16,512},{512,16},{528,0},{1,529},{17,513},{513,17},{529,1... | collective-permute-start | bytes 393224 | tf_op jit(solution)/shard_map/ppermute | solution.py:31
  76.9 31.0 %collective-permute-start.3 = (bf16[128,512]{1,0:T(8,128)(2,1)S(1)}, bf16[128,512]{1,0:T(8,128)(2,1)S(1)}, u32[]{:S(2)}, u32[]{:S(2)}) collective-permute-start(bf16[128,512]{1,0:T(8,128)(2,1)S(1)} %copy-done.2), channel_id=1, source_target_pairs={{0,16},{16,0},{1,17},{17,1},{2,18},{18,2},{3,19},{19,3},{4,20},{20... | collective-permute-start | bytes 393224 | tf_op jit(solution)/shard_map/ppermute | solution.py:31
  80.5 14.0 %collective-permute-start.7 = (bf16[16,2,2,8,128]{4,3,2,1,0:T(8,128)(2,1)S(1)}, bf16[16,2,2,8,128]{4,3,2,1,0:T(8,128)(2,1)S(1)}, u32[]{:S(2)}, u32[]{:S(2)}) collective-permute-start(bf16[16,2,2,8,128]{4,3,2,1,0:T(8,128)(2,1)S(1)} %all-to-all-done.1), channel_id=1, source_target_pairs={{0,512},{512,0},{1,513},{513,1},{2,514},{514,2},{3,515},{515,3},{4... | collective-permute-start | bytes 393224 | tf_op jit(solution)/shard_map/ppermute | solution.py:31
  86.1 21.7 %collective-permute-start.5 = (bf16[128,512]{1,0:T(8,128)(2,1)S(1)}, bf16[128,512]{1,0:T(8,128)(2,1)S(1)}, u32[]{:S(2)}, u32[]{:S(2)}) collective-permute-start(bf16[128,512]{1,0:T(8,128)(2,1)S(1)} %collective-permute-done.4), channel_id=1, source_target_pairs={{0,16},{16,0},{1,17},{17,1},{2,18},{18,2},{3,19},{19,3},{4,20},{20... | collective-permute-start | bytes 393224 | tf_op jit(solution)/shard_map/ppermute | solution.py:31
  88.1 6.5 %collective-permute-start.6 = (bf16[16,2,2,8,128]{4,3,2,1,0:T(8,128)(2,1)S(1)}, bf16[16,2,2,8,128]{4,3,2,1,0:T(8,128)(2,1)S(1)}, u32[]{:S(2)}, u32[]{:S(2)}) collective-permute-start(bf16[16,2,2,8,128]{4,3,2,1,0:T(8,128)(2,1)S(1)} %all-to-all-done.1), channel_id=1, source_target_pairs={{0,16},{16,0},{1,17},{17,1},{2,18},{18,2},{3,19},{19,3},{4,20},{20... | collective-permute-start | bytes 393224 | tf_op jit(solution)/shard_map/ppermute | solution.py:31
  95.5 29.3 %all-to-all-start.3 = ((bf16[16,8,896]{2,1,0:T(8,128)(2,1)}), bf16[16,8,896]{2,1,0:T(8,128)(2,1)S(1)}, u32[]{:S(2)}, u32[]{:S(2)}) async-start(bf16[16,8,896]{2,1,0:T(8,128)(2,1)} %broadcast_in_dim.10), calls=%async_computation.3 | async-start | bytes 458752 | tf_op jit(solution)/shard_map/all_to_all | solution.py:14
  107.9 0.8 copy-start.3
